TPU v7x, 256 devices: a whole 4x4x8 slice. The times are simulated.
256 devices in a mesh: gz: 32 (over y, z), gy: 8 (over x, core).
Axes of the slice: x: 4, y: 4, z: 8, core: 2. Of those that a mesh axis runs over, the one named last changes fastest.
Arguments:
- concentration: float32 [512, 64, 128], P('gz', 'gy'), may hold values from 0 to 2
- phases: int32 [512, 64, 128], P('gz', 'gy'), may hold values from 0 to 2, as said below
- grains: int32 [512, 64, 128], P('gz', 'gy'), may hold values from 0 to 63, as said below
- grain_class: int32 [64], replicated, may hold values from 0 to 3
- diffusivity: float32 [3, 4], replicated, may hold values from 1 to 2000
Outputs:
- solution: float32 [512, 64, 128], P('gz', 'gy')
Inputs may be any that keep to these rules, and one draw needn't show every extreme that they name: `phases`: constant on aligned blocks of 8 x 8 x 8 cells. `grains`: constant on aligned blocks of 4 x 4 x 4 cells.
All inputs are finite; a program needn't handle non-finite values.
Results may differ from a plain program's by a relative error of at most 0.0003.
Values sent between devices are 32-bit elements; how exact they have to be, the bound alone decides.
No kernel may reach another device: no remote copies, remote signals or barrier semaphores. Data moves between devices by JAX's collectives and lax.ppermute only.
A program may use at most 64 MiB of HBM per device.

v0:
```python
import jax
import jax.numpy as jnp
from jax import lax
from jax.experimental import pallas as pl
from jax.experimental.pallas import tpu as pltpu
from jax.sharding import PartitionSpec as P

HALO = 12
WZ = 40
BLOCKS = 10
WY = 24
VMEM_BYTES = 48 * 1024 * 1024


def harmonic(near_k, far_k):
    return 2.0 * near_k * far_k / (near_k + far_k)


def dot(left, right):
    return jnp.dot(left, right, precision=lax.Precision.HIGHEST, preferred_element_type=jnp.float32)


def iota(rows, dim, lanes=128):
    return lax.broadcasted_iota(jnp.int32, (rows, lanes), dim)


def matrix(condition, value):
    return jnp.where(condition, jnp.float32(value), jnp.float32(0.0))


def lane_map(make):
    return make(iota(128, 0), iota(128, 1))


class Level:
    def __init__(self, planes, ny, nx, zl, pad, cyclic, y_start, y_total, chunk):
        self.planes, self.ny, self.nx, self.zl, self.pad = planes, ny, nx, zl, pad
        self.cyclic, self.y_start, self.y_total = cyclic, y_start, y_total
        self.rows = planes * ny
        self.chunk = min(chunk, self.rows)

    def chunks(self, start=0, count=None):
        count = self.rows if count is None else count
        at = start
        while at < start + count:
            size = min(self.chunk, start + count - at)
            yield at, size
            at += size

    def neighbours(self, ref, at, size):
        base = self.pad + at
        here = ref[base : base + size]
        below = ref[base - self.ny : base - self.ny + size]
        above = ref[base + self.ny : base + self.ny + size]
        if self.zl > 1:
            cell = iota(size, 1) % (self.zl * self.nx)
            below = pltpu.roll(jnp.where(cell >= (self.zl - 1) * self.nx, below, here), self.nx, 1)
            above = pltpu.roll(jnp.where(cell < self.nx, above, here), 128 - self.nx, 1)
        return (
            here,
            (
                below,
                above,
                ref[base - 1 : base - 1 + size],
                ref[base + 1 : base + 1 + size],
                pltpu.roll(here, 1, 1),
                pltpu.roll(here, 127, 1),
            ),
        )

    def wrap(self, ref):
        if self.cyclic:
            ref[0 : self.pad] = ref[self.rows : self.rows + self.pad]
            ref[self.pad + self.rows : 2 * self.pad + self.rows] = ref[self.pad : 2 * self.pad]

    def build(self, kappa, faces):
        for at, size in self.chunks():
            here, around = self.neighbours(kappa, at, size)
            y = iota(size, 0) % self.ny + self.y_start
            x = iota(size, 1) % self.nx
            keep = (None, None, y != 0, y != self.y_total - 1, x != 0, x != self.nx - 1)
            total = jnp.full((size, 128), 1.0, jnp.float32)
            for number in range(6):
                face = harmonic(here, around[number])
                if keep[number] is not None:
                    face = jnp.where(keep[number], face, 0.0)
                faces[number, at : at + size] = face
                total = total + face
            faces[6, at : at + size] = 0.8 / total
            faces[7, at : at + size] = total

    def coupled(self, field, source, faces, at, size):
        here, around = self.neighbours(field, at, size)
        total = source[at : at + size]
        for number in range(6):
            total = total + faces[number, at : at + size] * around[number]
        return here, total

    def start(self, field, source, faces):
        for at, size in self.chunks():
            field[self.pad + at : self.pad + at + size] = faces[6, at : at + size] * source[at : at + size]
        self.wrap(field)

    def relax(self, field, target, source, faces, start=0, count=None):
        for at, size in self.chunks(start, count):
            here, total = self.coupled(field, source, faces, at, size)
            target[self.pad + at : self.pad + at + size] = 0.2 * here + faces[6, at : at + size] * total
        self.wrap(target)

    def defect(self, field, source, faces, out, start=0, count=None):
        for at, size in self.chunks(start, count):
            here, total = self.coupled(field, source, faces, at, size)
            out[at - start : at - start + size] = total - faces[7, at : at + size] * here

    def pairs(self, ref):
        half = self.rows // 2
        return ref[pl.ds(0, half, stride=2), :] + ref[pl.ds(1, half, stride=2), :]


def kappa_body(class_ref, diff_ref, phases_ref, grains_ref, conc_ref, kappa_ref, up_ref, down_ref):
    num_phases, num_classes = diff_ref.shape
    for block in range(4):
        grain = grains_ref[4 * block]
        phase = phases_ref[4 * block]
        cls = jnp.zeros(grain.shape, jnp.int32)
        for number in range(class_ref.shape[0]):
            cls = jnp.where(grain == number, class_ref[number], cls)
        value = jnp.ones(grain.shape, jnp.float32)
        for p in range(num_phases):
            for c in range(num_classes):
                value = jnp.where((phase == p) & (cls == c), diff_ref[p, c], value)
        kappa_ref[block] = value
        if block > 0:
            up_ref[HALO + block - 1] = value
        if block < 3:
            down_ref[HALO + block] = value
    for z in range(HALO):
        up_ref[z] = conc_ref[16 - HALO + z]
        down_ref[z] = conc_ref[z]


def window(refs, plane):
    return jnp.concatenate([ref[plane] for ref in refs], axis=0)


def build_fine(sources, y_device, kappa, coefs, z_faces):
    kappa[0:8] = jnp.ones((8, 128), jnp.float32)
    kappa[8 + BLOCKS * WY : 16 + BLOCKS * WY] = jnp.ones((8, 128), jnp.float32)
    for block in range(BLOCKS):
        kappa[8 + block * WY : 8 + (block + 1) * WY] = window(sources, WZ + block)
    y = iota(WY, 0) + y_device * 8 - 8
    x = iota(WY, 1)
    for block in range(BLOCKS + 1):
        low, high = max(block - 1, 0), min(block, BLOCKS - 1)
        z_faces[block] = harmonic(
            kappa[8 + low * WY : 8 + (low + 1) * WY], kappa[8 + high * WY : 8 + (high + 1) * WY]
        )
    for block in range(BLOCKS):
        at = 8 + block * WY
        k = kappa[at : at + WY]
        y_low = jnp.where(y == 0, 0.0, harmonic(k, kappa[at - 1 : at - 1 + WY]))
        y_high = jnp.where(y == 63, 0.0, harmonic(k, kappa[at + 1 : at + 1 + WY]))
        x_low = jnp.where(x == 0, 0.0, harmonic(k, pltpu.roll(k, 1, 1)))
        x_high = jnp.where(x == 127, 0.0, harmonic(k, pltpu.roll(k, 127, 1)))
        sides = 1.0 + y_low + y_high + x_low + x_high
        diagonals = (sides + z_faces[block] + k, sides + k + k, sides + k + z_faces[block + 1])
        for number, value in enumerate((k, y_low, y_high, x_low, x_high)):
            coefs[block, number] = value
        for number, value in enumerate(diagonals):
            coefs[block, 5 + number] = 0.8 / value
            coefs[block, 8 + number] = value


def fine_plane(field, sources, coefs, z_faces, z, low=0, size=WY):
    block, p = divmod(z, 4)
    rows = slice(low, low + size)
    at = WY + z * WY + low
    here = field[at : at + size]
    k = coefs[block, 0, rows]
    below = z_faces[block, rows] if p == 0 else k
    above = z_faces[block + 1, rows] if p == 3 else k
    source = window(sources, z) if size == WY else sources[1][z]
    total = (
        source
        + below * field[at - WY : at - WY + size]
        + above * field[at + WY : at + WY + size]
        + coefs[block, 1, rows] * field[at - 1 : at - 1 + size]
        + coefs[block, 2, rows] * field[at + 1 : at + 1 + size]
        + coefs[block, 3, rows] * pltpu.roll(here, 1, 1)
        + coefs[block, 4, rows] * pltpu.roll(here, 127, 1)
    )
    kind = (0, 1, 1, 2)[p]
    return here, total, coefs[block, 5 + kind, rows], coefs[block, 8 + kind, rows]


def level_one(y_device):
    return Level(20, 16, 64, 1, 16, False, y_device * 4 - 4, 32, 160)


def build_one(level, kappa, spread, packed, kappa_one, faces):
    for block in range(BLOCKS):
        spread[block * 32 : block * 32 + WY] = kappa[8 + block * WY : 8 + (block + 1) * WY]
        spread[block * 32 + WY : block * 32 + 32] = jnp.ones((32 - WY, 128), jnp.float32)
    pick = lane_map(lambda r, c: matrix(r == 2 * (c % 64), 0.5))
    packed[...] = dot(spread[pl.ds(0, BLOCKS * 16, stride=2), :], pick)
    ones = jnp.ones((16, 128), jnp.float32)
    kappa_one[0:16] = ones
    kappa_one[336:352] = ones
    for block in range(BLOCKS):
        value = packed[block * 16 : block * 16 + 16]
        kappa_one[16 + block * 32 : 32 + block * 32] = value
        kappa_one[32 + block * 32 : 48 + block * 32] = value
    level.build(kappa_one, faces)


def to_chunk(rows):
    group = iota(8, 1) // 32
    out = rows[0:8]
    for z in range(1, 4):
        out = jnp.where(group == z, rows[8 * z : 8 * z + 8], out)
    return out


def down_body(first, *refs):
    index, low, own, high = refs[:4]
    sources = (low, own, high)
    refs = refs[4:]
    if not first:
        fields, refs = refs[:3], refs[3:]
    chunk, edge, kept, source_one, kept_one = refs[:5]
    kappa, coefs, z_faces, va, vb, rs, spread, packed, kappa_one, faces, oa, tmp = refs[5:]
    y_device = index[1]
    build_fine(sources, y_device, kappa, coefs, z_faces)
    level = level_one(y_device)
    build_one(level, kappa, spread, packed, kappa_one, faces)
    zero = jnp.zeros((WY, 128), jnp.float32)
    for ref in (va, vb):
        ref[0:WY] = zero
        ref[(WZ + 1) * WY : (WZ + 2) * WY] = zero
    if first:
        for z in range(WZ):
            kind = (0, 1, 1, 2)[z % 4]
            va[(z + 1) * WY : (z + 2) * WY] = coefs[z // 4, 5 + kind] * window(sources, z)
    else:
        for z in range(WZ):
            vb[(z + 1) * WY : (z + 2) * WY] = window(fields, z)
        for z in range(WZ):
            here, total, weight, _ = fine_plane(vb, sources, coefs, z_faces, z)
            va[(z + 1) * WY : (z + 2) * WY] = 0.2 * here + weight * total
    for z in range(2, WZ - 2):
        here, total, weight, _ = fine_plane(va, sources, coefs, z_faces, z)
        value = 0.2 * here + weight * total
        vb[(z + 1) * WY : (z + 2) * WY] = value
        if 10 <= z < 30:
            kept[(z - 10) * WY : (z - 9) * WY] = value
    for plane in range(20):
        if 2 <= plane < 18:
            total_defect = 0.0
            for z in (2 * plane, 2 * plane + 1):
                here, total, _, diagonal = fine_plane(vb, sources, coefs, z_faces, z)
                total_defect = total_defect + (total - diagonal * here)
            rs[plane * 32 : plane * 32 + WY] = total_defect
            rs[plane * 32 + WY : plane * 32 + 32] = jnp.zeros((32 - WY, 128), jnp.float32)
        else:
            rs[plane * 32 : plane * 32 + 32] = jnp.zeros((32, 128), jnp.float32)
    mean_x = lane_map(lambda r, c: matrix(r // 2 == c % 64, 0.125))
    source_one[...] = dot(rs[pl.ds(0, 320, stride=2), :] + rs[pl.ds(1, 320, stride=2), :], mean_x)
    for ref in (oa, kept_one):
        ref[0:16] = jnp.zeros((16, 128), jnp.float32)
        ref[336:352] = jnp.zeros((16, 128), jnp.float32)
    level.start(oa, source_one, faces)
    level.relax(oa, kept_one, source_one, faces)
    level.defect(kept_one, source_one, faces, tmp, 6 * 16, 8 * 16)
    for z in range(4):
        tmp[z * 16 : z * 16 + 16] = tmp[z * 32 : z * 32 + 16] + tmp[z * 32 + 16 : z * 32 + 32]
    halves = tmp[pl.ds(0, 32, stride=2), :] + tmp[pl.ds(1, 32, stride=2), :]
    mean_two = lane_map(lambda r, c: matrix((r < 64) & (r // 2 == c % 32), 0.125))
    chunk[0:2] = to_chunk(dot(halves, mean_two))[2:4]
    if first:
        pick_two = lane_map(lambda r, c: matrix((r < 64) & (r == 2 * (c % 32)), 0.5))
        chunk[2:4] = to_chunk(dot(packed[pl.ds(48, 32, stride=2), :], pick_two))[2:4]
    for plane in range(20):
        edge[plane * 4 : plane * 4 + 4] = kept_one[16 + plane * 16 + 4 : 16 + plane * 16 + 8]


def up_body(first, z_devices, *refs):
    index, low, own, high, gathered = refs[:5]
    refs = refs[5:]
    if first:
        labelled = gathered
    else:
        labelled, refs = refs[0], refs[1:]
    edge_low, edge_high, kept, source_one, kept_one, out = refs[:6]
    (kappa, coefs, z_faces, va, vb, spread, packed, kappa_one, faces, oa, ob) = refs[6:17]
    (k2, g2, a2, b2, f2, r2, k3, g3, a3, b3, f3, r3, k4, g4, a4, b4, f4, r4) = refs[17:]
    sources = (low, own, high)
    z_device, y_device = index[0], index[1]
    two = Level(z_devices, 16, 32, 4, 16, True, 0, 16, 128)
    three = Level(z_devices, 8, 16, 2, 8, True, 0, 8, 128)
    four = Level(z_devices, 4, 8, 1, 8, True, 0, 4, 128)

    chunks = z_devices * 8
    for part in range(2):
        k2[pl.ds(two.pad + part, chunks, stride=2), :] = labelled[pl.ds(2 + part, chunks, stride=4), :]
        if first:
            g2[pl.ds(part, chunks, stride=2), :] = gathered[pl.ds(part, chunks, stride=4), :]
    if not first:
        g2 = gathered
    two.wrap(k2)
    two.build(k2, f2)
    mean_three = lane_map(lambda r, c: matrix(c % 32 == (r // 64) * 16 + (r % 32) // 2, 0.125))
    mean_four = lane_map(lambda r, c: matrix((r < 32) & (c % 8 == (r % 16) // 2), 0.125))
    r2[...] = k2[two.pad : two.pad + two.rows]
    k3[three.pad : three.pad + three.rows] = 0.5 * dot(two.pairs(r2), mean_three)
    three.wrap(k3)
    three.build(k3, f3)
    r3[...] = k3[three.pad : three.pad + three.rows]
    k4[four.pad : four.pad + four.rows] = 0.5 * dot(three.pairs(r3), mean_four)
    four.wrap(k4)
    four.build(k4, f4)

    two.start(a2, g2, f2)
    two.relax(a2, b2, g2, f2)
    two.defect(b2, g2, f2, r2)
    g3[...] = dot(two.pairs(r2), mean_three)
    three.start(a3, g3, f3)
    three.relax(a3, b3, g3, f3)
    three.defect(b3, g3, f3, r3)
    g4[...] = dot(three.pairs(r3), mean_four)
    four.start(a4, g4, f4)
    for _ in range(2):
        four.relax(a4, b4, g4, f4)
        four.relax(b4, a4, g4, f4)
    four.relax(a4, b4, g4, f4)

    def correct(level, field, coarse, tmp, spread_lanes):
        value = dot(coarse, spread_lanes)
        half = level.rows // 2
        tmp[pl.ds(0, half, stride=2), :] = value
        tmp[pl.ds(1, half, stride=2), :] = value
        inner = slice(level.pad, level.pad + level.rows)
        field[inner] = field[inner] + tmp[...]
        level.wrap(field)

    from_four = lane_map(lambda r, c: matrix((r < 8) & (r == (c % 16) // 2), 1.0))
    from_three = lane_map(lambda r, c: matrix((r < 32) & (r == (c // 64) * 16 + (c % 32) // 2), 1.0))
    correct(three, b3, b4[four.pad : four.pad + four.rows], r3, from_four)
    three.relax(b3, a3, g3, f3)
    three.relax(a3, b3, g3, f3)
    correct(two, b2, b3[three.pad : three.pad + three.rows], r2, from_three)
    two.relax(b2, a2, g2, f2)
    two.relax(a2, b2, g2, f2)

    build_fine(sources, y_device, kappa, coefs, z_faces)
    level = level_one(y_device)
    build_one(level, kappa, spread, packed, kappa_one, faces)

    near = b2[pl.ds(pl.multiple_of(z_device * 16, 16), 48), :]
    rows = matrix(iota(16, 1, 16) == y_device * 2 - 2 + iota(16, 0, 16) // 2, 1.0)
    spread_y = jnp.concatenate([dot(rows, near[16 * part : 16 * part + 16]) for part in range(3)], axis=0)
    by_z = [
        dot(spread_y, lane_map(lambda r, c, z=z: matrix(r == z * 32 + (c % 64) // 2, 1.0))) for z in range(4)
    ]
    for plane in range(20):
        part, z = divmod(plane // 2 + 1, 4)
        at = 16 + plane * 16
        field = jnp.concatenate(
            [edge_low[plane * 4 : plane * 4 + 4], kept_one[at + 4 : at + 8],
             edge_high[plane * 4 : plane * 4 + 4], jnp.zeros((4, 128), jnp.float32)], axis=0
        )
        oa[at : at + 16] = field + by_z[z][16 * part : 16 * part + 16]
    level.relax(oa, ob, source_one, faces, 4 * 16, 12 * 16)
    level.relax(ob, oa, source_one, faces, 5 * 16, 10 * 16)
    from_one = lane_map(lambda r, c: matrix((r < 64) & (r == c // 2), 1.0))
    value = dot(oa[16 + 80 : 16 + 240], from_one)
    spread[pl.ds(0, 160, stride=2), :] = value
    spread[pl.ds(1, 160, stride=2), :] = value
    for z in range(10, 30):
        at = ((z - 10) // 2) * 32
        va[(z + 1) * WY : (z + 2) * WY] = kept[(z - 10) * WY : (z - 9) * WY] + spread[at : at + WY]
    for z in range(11, 29):
        here, total, weight, _ = fine_plane(va, sources, coefs, z_faces, z)
        vb[(z + 1) * WY : (z + 2) * WY] = 0.2 * here + weight * total
    for z in range(12, 28):
        here, total, weight, _ = fine_plane(vb, sources, coefs, z_faces, z, 8, 8)
        out[z - 12] = 0.2 * here + weight * total


def floats(*shape):
    return jax.ShapeDtypeStruct(shape, jnp.float32)


def call(body, outs, scratch, args, smem):
    vmem = pl.BlockSpec(memory_space=pltpu.VMEM)
    return pl.pallas_call(
        body,
        out_shape=outs,
        in_specs=[pl.BlockSpec(memory_space=pltpu.SMEM)] * smem + [vmem] * (len(args) - smem),
        out_specs=[vmem] * len(outs),
        scratch_shapes=[pltpu.VMEM(shape, jnp.float32) for shape in scratch],
        compiler_params=pltpu.CompilerParams(vmem_limit_bytes=VMEM_BYTES),
    )(*args)


FINE = [(16 + BLOCKS * WY, 128), (BLOCKS, 11, WY, 128), (BLOCKS + 1, WY, 128), ((WZ + 2) * WY, 128), ((WZ + 2) * WY, 128)]
ONE = [(320, 128), (160, 128), (352, 128), (8, 320, 128), (352, 128)]


def down(index, sources, fields):
    first = fields is None
    outs = [
        floats(4 if first else 2, 128), floats(80, 128), floats(20 * WY, 128), floats(320, 128), floats(352, 128)
    ]
    scratch = FINE + [(640, 128)] + ONE + [(128, 128)]
    args = [index, *sources] + ([] if first else list(fields))
    return call(lambda *refs: down_body(first, *refs), outs, scratch, args, 1)


def up(index, sources, gathered, labelled, edges, kept):
    first = labelled is None
    z_devices = lax.axis_size("gz")
    scratch = FINE + ONE + [(352, 128)]
    for ny, pad in ((16, 16), (8, 8), (4, 8)):
        rows = z_devices * ny
        padded = (rows + 2 * pad, 128)
        scratch += [padded, (rows, 128), padded, padded, (8, rows, 128), (rows, 128)]
    args = [index, *sources, gathered] + ([] if first else [labelled]) + [*edges, *kept]
    return call(lambda *refs: up_body(first, z_devices, *refs), [floats(16, 8, 128)], scratch, args, 1)[0]


def shifted(array, axis, step):
    count = lax.axis_size(axis)
    return lax.ppermute(array, axis, [(i, (i + step) % count) for i in range(count)])


def both_sides(array, axis):
    return shifted(array, axis, 1), shifted(array, axis, -1)


def to_all(chunk):
    devices = lax.axis_size("gz") * lax.axis_size("gy")
    copies = jnp.broadcast_to(chunk[None], (devices,) + chunk.shape)
    out = lax.all_to_all(copies, ("gz", "gy"), 0, 0)
    return out.reshape(devices * chunk.shape[0], 128)


def per_device(concentration, phases, grains, grain_class, diffusivity):
    index = jnp.stack([lax.axis_index("gz"), lax.axis_index("gy")]).astype(jnp.int32)
    kappa, up_part, down_part = call(
        kappa_body,
        [floats(4, 8, 128), floats(HALO + 3, 8, 128), floats(HALO + 3, 8, 128)],
        [],
        [grain_class, diffusivity, phases, grains, concentration],
        2,
    )
    before = shifted(up_part, "gz", 1)
    after = shifted(down_part, "gz", -1)
    own = jnp.concatenate(
        [before[:HALO], concentration, after[:HALO], before[HALO:], kappa, after[HALO:]], axis=0
    )
    low, high = both_sides(own, "gy")
    sources = (low, own, high)

    chunk, edge, *kept = down(index, sources, None)
    edges = both_sides(edge, "gy")
    labelled = to_all(chunk)
    field = up(index, sources, labelled, None, edges, kept)

    before = shifted(field[16 - HALO :], "gz", 1)
    after = shifted(field[:HALO], "gz", -1)
    field = jnp.concatenate([before, field, after], axis=0)
    low, high = both_sides(field, "gy")
    chunk, edge, *kept = down(index, sources, (low, field, high))
    edges = both_sides(edge, "gy")
    gathered = to_all(chunk)
    return up(index, sources, gathered, labelled, edges, kept)


def solution(mesh):
    placed = (P("gz", "gy", None), P("gz", "gy", None), P("gz", "gy", None), P(), P())
    return jax.shard_map(
        per_device, mesh=mesh, in_specs=placed, out_specs=P("gz", "gy", None), check_vma=False
    )
```

profile of v0, /device:TPU:1, one launch (start us, length us, event | category | flops | bytes accessed | tf_op | source)
XLA Modules:
  0.0 110.0 jit_solution(5788865037247974504)
XLA Ops:
  4.6 2.5 %collective-permute-start = (f32[15,8,128]{2,1,0:T(8,128)S(1)}, f32[15,8,128]{2,1,0:T(8,128)S(1)}, u32[]{:S(2)}, u32[]{:S(2)}) collective-permute-start(f32[15,8,128]{2,1,0:T(8,128)S(1)} %get-tuple-element.18), channel_id=1, source_target_pairs={{0,8},{8,16},{16,24},{24,32},{32,40},{40,48},{48,56},{56,64},{64,7... | collective-permute-start | bytes 184328 | tf_op jit(solution)/shard_map/ppermute | solution.py:433
  7.1 6.5 %collective-permute-start.1 = (f32[15,8,128]{2,1,0:T(8,128)S(1)}, f32[15,8,128]{2,1,0:T(8,128)S(1)}, u32[]{:S(2)}, u32[]{:S(2)}) collective-permute-start(f32[15,8,128]{2,1,0:T(8,128)S(1)} %get-tuple-element.19), channel_id=1, source_target_pairs={{0,248},{8,0},{16,8},{24,16},{32,24},{40,32},{48,40},{56,48},{64,5... | collective-permute-start | bytes 184328 | tf_op jit(solution)/shard_map/ppermute | solution.py:433
  13.6 1.5 %collective-permute-done = f32[15,8,128]{2,1,0:T(8,128)S(1)} collective-permute-done((f32[15,8,128]{2,1,0:T(8,128)S(1)}, f32[15,8,128]{2,1,0:T(8,128)S(1)}, u32[]{:S(2)}, u32[]{:S(2)}) %collective-permute-start) | collective-permute-done | bytes 61472 | tf_op jit(solution)/shard_map/ppermute | solution.py:433
  15.2 2.7 %collective-permute-start.2 = (f32[50,8,128]{2,1,0:T(8,128)S(1)}, f32[50,8,128]{2,1,0:T(8,128)S(1)}, u32[]{:S(2)}, u32[]{:S(2)}) collective-permute-start(f32[50,8,128]{2,1,0:T(8,128)S(1)} %constant_dynamic-update-slice_fusion.refs_2_), channel_id=1, source_target_pairs={{0,1},{1,2},{2,3},{3,4},{4,5},{5,6},{6,7},{7,0},{8,9},{9,10},{10,1... | collective-permute-start | bytes 614408 | tf_op jit(solution)/shard_map/ppermute | solution.py:433
  17.9 2.6 %collective-permute-done.2.refs_1_ = f32[50,8,128]{2,1,0:T(8,128)S(1)} collective-permute-done((f32[50,8,128]{2,1,0:T(8,128)S(1)}, f32[50,8,128]{2,1,0:T(8,128)S(1)}, u32[]{:S(2)}, u32[]{:S(2)}) %collective-permute-start.2) | collective-permute-done | bytes 204832 | tf_op jit(solution)/shard_map/ppermute | solution.py:433
  20.5 2.5 %collective-permute-done.3.refs_3_ = f32[50,8,128]{2,1,0:T(8,128)S(1)} collective-permute-done((f32[50,8,128]{2,1,0:T(8,128)S(1)}, f32[50,8,128]{2,1,0:T(8,128)S(1)}, u32[]{:S(2)}, u32[]{:S(2)}) %collective-permute-start.3) | collective-permute-done | bytes 204832 | tf_op jit(solution)/shard_map/ppermute | solution.py:433
  23.0 2.1 %shard_map.56 = (f32[4,128]{1,0:T(4,128)S(1)}, f32[80,128]{1,0:T(8,128)S(1)}, f32[480,128]{1,0:T(8,128)S(1)}, f32[320,128]{1,0:T(8,128)S(1)}, f32[352,128]{1,0:T(8,128)S(1)}) custom-call(s32[2]{0:T(128)S(1)} %pad_add_fusion.refs_0_, f32[50,8,128]{2,1,0:T(8,128)S(1)} %collective-permute-done.2.refs_1_, ...), custom_call_target="tpu_custom_call" | custom-call | tf_op jit(solution)/shard_map/pallas_call | solution.py:395
  26.0 9.8 %all-to-all-start = ((f32[256,4,128]{2,1,0:T(4,128)}), f32[256,4,128]{2,1,0:T(4,128)S(1)}, u32[]{:S(2)}, u32[]{:S(2)}) async-start(f32[256,4,128]{2,1,0:T(4,128)} %broadcast_in_dim.4), calls=%async_computation | async-start | bytes 1048576 | tf_op jit(solution)/shard_map/all_to_all | solution.py:443
  35.8 1.6 %collective-permute-start.4 = (f32[80,128]{1,0:T(8,128)S(1)}, f32[80,128]{1,0:T(8,128)S(1)}, u32[]{:S(2)}, u32[]{:S(2)}) collective-permute-start(f32[80,128]{1,0:T(8,128)S(1)} %get-tuple-element.22), channel_id=1, source_target_pairs={{0,1},{1,2},{2,3},{3,4},{4,5},{5,6},{6,7},{7,0},{8,9},{9,10},{10,1... | collective-permute-start | bytes 122888 | tf_op jit(solution)/shard_map/ppermute | solution.py:433
  38.7 2.7 %collective-permute-done.5.refs_6_ = f32[80,128]{1,0:T(8,128)S(1)} collective-permute-done((f32[80,128]{1,0:T(8,128)S(1)}, f32[80,128]{1,0:T(8,128)S(1)}, u32[]{:S(2)}, u32[]{:S(2)}) %collective-permute-start.5) | collective-permute-done | bytes 40992 | tf_op jit(solution)/shard_map/ppermute | solution.py:433
  41.4 14.9 %all-to-all-done = f32[256,4,128]{2,1,0:T(4,128)S(1)} async-done(((f32[256,4,128]{2,1,0:T(4,128)}), f32[256,4,128]{2,1,0:T(4,128)S(1)}, u32[]{:S(2)}, u32[]{:S(2)}) %all-to-all-start) | async-done | bytes 524320 | tf_op jit(solution)/shard_map/all_to_all | solution.py:443
  56.3 5.6 %shard_map.57 = f32[16,8,128]{2,1,0:T(8,128)S(1)} custom-call(s32[2]{0:T(128)S(1)} %pad_add_fusion.refs_0_, f32[50,8,128]{2,1,0:T(8,128)S(1)} %collective-permute-done.2.refs_1_, f32[50,8,128]{2,1,0:T(8,128)S(1)} %constant_dynamic-update-slice_fusion.refs_2_, f32[50,8,128]{2,1,0:T(8,128)S(1)} %collective-permute-done.3.refs_3_, f32[1024,128]{1,0:T(8,128)S(1)} %bitcast.4, ...), custom_call_target="tpu_custom_call" | custom-call | tf_op jit(solution)/shard_map/pallas_call | solution.py:395
  61.9 1.1 %collective-permute-start.6 = (f32[12,8,128]{2,1,0:T(8,128)S(1)}, f32[12,8,128]{2,1,0:T(8,128)S(1)}, u32[]{:S(2)}, u32[]{:S(2)}) collective-permute-start(f32[12,8,128]{2,1,0:T(8,128)S(1)} %get-tuple-element.31), channel_id=1, source_target_pairs={{0,8},{8,16},{16,24},{24,32},{32,40},{40,48},{48,56},{56,64},{64,7... | collective-permute-start | bytes 147464 | tf_op jit(solution)/shard_map/ppermute | solution.py:433
  63.1 3.7 %collective-permute-start.7 = (f32[12,8,128]{2,1,0:T(8,128)S(1)}, f32[12,8,128]{2,1,0:T(8,128)S(1)}, u32[]{:S(2)}, u32[]{:S(2)}) collective-permute-start(f32[12,8,128]{2,1,0:T(8,128)S(1)} %get-tuple-element.32), channel_id=1, source_target_pairs={{0,248},{8,0},{16,8},{24,16},{32,24},{40,32},{48,40},{56,48},{64,5... | collective-permute-start | bytes 147464 | tf_op jit(solution)/shard_map/ppermute | solution.py:433
  66.8 1.9 %collective-permute-done.6 = f32[12,8,128]{2,1,0:T(8,128)S(1)} collective-permute-done((f32[12,8,128]{2,1,0:T(8,128)S(1)}, f32[12,8,128]{2,1,0:T(8,128)S(1)}, u32[]{:S(2)}, u32[]{:S(2)}) %collective-permute-start.6) | collective-permute-done | bytes 49184 | tf_op jit(solution)/shard_map/ppermute | solution.py:433
  68.7 1.7 %collective-permute-start.8 = (f32[40,8,128]{2,1,0:T(8,128)S(1)}, f32[40,8,128]{2,1,0:T(8,128)S(1)}, u32[]{:S(2)}, u32[]{:S(2)}) collective-permute-start(f32[40,8,128]{2,1,0:T(8,128)S(1)} %pad_maximum_fusion.refs_5_), channel_id=1, source_target_pairs={{0,1},{1,2},{2,3},{3,4},{4,5},{5,6},{6,7},{7,0},{8,9},{9,10},{10,1... | collective-permute-start | bytes 491528 | tf_op jit(solution)/shard_map/ppermute | solution.py:433
  70.5 2.3 %collective-permute-done.8.refs_4_ = f32[40,8,128]{2,1,0:T(8,128)S(1)} collective-permute-done((f32[40,8,128]{2,1,0:T(8,128)S(1)}, f32[40,8,128]{2,1,0:T(8,128)S(1)}, u32[]{:S(2)}, u32[]{:S(2)}) %collective-permute-start.8) | collective-permute-done | bytes 163872 | tf_op jit(solution)/shard_map/ppermute | solution.py:433
  72.7 2.5 %collective-permute-done.9.refs_6_ = f32[40,8,128]{2,1,0:T(8,128)S(1)} collective-permute-done((f32[40,8,128]{2,1,0:T(8,128)S(1)}, f32[40,8,128]{2,1,0:T(8,128)S(1)}, u32[]{:S(2)}, u32[]{:S(2)}) %collective-permute-start.9) | collective-permute-done | bytes 163872 | tf_op jit(solution)/shard_map/ppermute | solution.py:433
  75.2 2.5 %shard_map.58 = (f32[2,128]{1,0:T(2,128)S(1)}, f32[80,128]{1,0:T(8,128)S(1)}, f32[480,128]{1,0:T(8,128)S(1)}, f32[320,128]{1,0:T(8,128)S(1)}, f32[352,128]{1,0:T(8,128)S(1)}) custom-call(s32[2]{0:T(128)S(1)} %pad_add_fusion.refs_0_, f32[50,8,128]{2,1,0:T(8,128)S(1)} %collective-permute-done.2.refs_1_, ...), custom_call_target="tpu_custom_call" | custom-call | tf_op jit(solution)/shard_map/pallas_call | solution.py:395
  78.5 9.8 %all-to-all-start.1 = ((f32[256,2,128]{2,1,0:T(2,128)}), f32[256,2,128]{2,1,0:T(2,128)S(1)}, u32[]{:S(2)}, u32[]{:S(2)}) async-start(f32[256,2,128]{2,1,0:T(2,128)} %broadcast_in_dim.5), calls=%async_computation.1 | async-start | bytes 524288 | tf_op jit(solution)/shard_map/all_to_all | solution.py:443
  88.3 1.6 %collective-permute-start.10 = (f32[80,128]{1,0:T(8,128)S(1)}, f32[80,128]{1,0:T(8,128)S(1)}, u32[]{:S(2)}, u32[]{:S(2)}) collective-permute-start(f32[80,128]{1,0:T(8,128)S(1)} %get-tuple-element.27), channel_id=1, source_target_pairs={{0,1},{1,2},{2,3},{3,4},{4,5},{5,6},{6,7},{7,0},{8,9},{9,10},{10,1... | collective-permute-start | bytes 122888 | tf_op jit(solution)/shard_map/ppermute | solution.py:433
  91.2 2.7 %collective-permute-done.11.refs_7_ = f32[80,128]{1,0:T(8,128)S(1)} collective-permute-done((f32[80,128]{1,0:T(8,128)S(1)}, f32[80,128]{1,0:T(8,128)S(1)}, u32[]{:S(2)}, u32[]{:S(2)}) %collective-permute-start.11) | collective-permute-done | bytes 40992 | tf_op jit(solution)/shard_map/ppermute | solution.py:433
  93.8 9.9 %all-to-all-done.1 = f32[256,2,128]{2,1,0:T(2,128)S(1)} async-done(((f32[256,2,128]{2,1,0:T(2,128)}), f32[256,2,128]{2,1,0:T(2,128)S(1)}, u32[]{:S(2)}, u32[]{:S(2)}) %all-to-all-start.1) | async-done | bytes 262176 | tf_op jit(solution)/shard_map/all_to_all | solution.py:443
  103.7 6.3 %shard_map.59 = f32[16,8,128]{2,1,0:T(8,128)} custom-call(s32[2]{0:T(128)S(1)} %pad_add_fusion.refs_0_, f32[50,8,128]{2,1,0:T(8,128)S(1)} %collective-permute-done.2.refs_1_, f32[50,8,128]{2,1,0:T(8,128)S(1)} %constant_dynamic-update-slice_fusion.refs_2_, f32[50,8,128]{2,1,0:T(8,128)S(1)} %collective-permute-done.3.refs_3_, f32[512,128]{1,0:T(8,128)S(1)} %bitcast.6, ...), custom_call_target="tpu_custom_call" | custom-call | tf_op jit(solution)/shard_map/pallas_call | solution.py:395
  (30 shorter events, 8.8 us)
Async XLA Ops:
  0.0 0.8 copy-start
  0.8 0.8 copy-start.1
  1.7 0.8 copy-start.2
  2.5 0.7 copy-start.3
  3.2 0.7 copy-start.4
  4.6 10.5 %collective-permute-start = (f32[15,8,128]{2,1,0:T(8,128)S(1)}, f32[15,8,128]{2,1,0:T(8,128)S(1)}, u32[]{:S(2)}, u32[]{:S(2)}) collective-permute-start(f32[15,8,128]{2,1,0:T(8,128)S(1)} %get-tuple-element.18), channel_id=1, source_target_pairs={{0,8},{8,16},{16,24},{24,32},{32,40},{40,48},{48,56},{56,64},{64,7... | collective-permute-start | bytes 184328 | tf_op jit(solution)/shard_map/ppermute | solution.py:433
  7.1 8.0 %collective-permute-start.1 = (f32[15,8,128]{2,1,0:T(8,128)S(1)}, f32[15,8,128]{2,1,0:T(8,128)S(1)}, u32[]{:S(2)}, u32[]{:S(2)}) collective-permute-start(f32[15,8,128]{2,1,0:T(8,128)S(1)} %get-tuple-element.19), channel_id=1, source_target_pairs={{0,248},{8,0},{16,8},{24,16},{32,24},{40,32},{48,40},{56,48},{64,5... | collective-permute-start | bytes 184328 | tf_op jit(solution)/shard_map/ppermute | solution.py:433
  15.2 5.4 %collective-permute-start.2 = (f32[50,8,128]{2,1,0:T(8,128)S(1)}, f32[50,8,128]{2,1,0:T(8,128)S(1)}, u32[]{:S(2)}, u32[]{:S(2)}) collective-permute-start(f32[50,8,128]{2,1,0:T(8,128)S(1)} %constant_dynamic-update-slice_fusion.refs_2_), channel_id=1, source_target_pairs={{0,1},{1,2},{2,3},{3,4},{4,5},{5,6},{6,7},{7,0},{8,9},{9,10},{10,1... | collective-permute-start | bytes 614408 | tf_op jit(solution)/shard_map/ppermute | solution.py:433
  17.8 5.2 %collective-permute-start.3 = (f32[50,8,128]{2,1,0:T(8,128)S(1)}, f32[50,8,128]{2,1,0:T(8,128)S(1)}, u32[]{:S(2)}, u32[]{:S(2)}) collective-permute-start(f32[50,8,128]{2,1,0:T(8,128)S(1)} %constant_dynamic-update-slice_fusion.refs_2_), channel_id=1, source_target_pairs={{0,7},{1,0},{2,1},{3,2},{4,3},{5,4},{6,5},{7,6},{8,15},{9,8},{10,9... | collective-permute-start | bytes 614408 | tf_op jit(solution)/shard_map/ppermute | solution.py:433
  26.0 30.3 %all-to-all-start = ((f32[256,4,128]{2,1,0:T(4,128)}), f32[256,4,128]{2,1,0:T(4,128)S(1)}, u32[]{:S(2)}, u32[]{:S(2)}) async-start(f32[256,4,128]{2,1,0:T(4,128)} %broadcast_in_dim.4), calls=%async_computation | async-start | bytes 1048576 | tf_op jit(solution)/shard_map/all_to_all | solution.py:443
  35.8 2.9 %collective-permute-start.4 = (f32[80,128]{1,0:T(8,128)S(1)}, f32[80,128]{1,0:T(8,128)S(1)}, u32[]{:S(2)}, u32[]{:S(2)}) collective-permute-start(f32[80,128]{1,0:T(8,128)S(1)} %get-tuple-element.22), channel_id=1, source_target_pairs={{0,1},{1,2},{2,3},{3,4},{4,5},{5,6},{6,7},{7,0},{8,9},{9,10},{10,1... | collective-permute-start | bytes 122888 | tf_op jit(solution)/shard_map/ppermute | solution.py:433
  37.5 4.0 %collective-permute-start.5 = (f32[80,128]{1,0:T(8,128)S(1)}, f32[80,128]{1,0:T(8,128)S(1)}, u32[]{:S(2)}, u32[]{:S(2)}) collective-permute-start(f32[80,128]{1,0:T(8,128)S(1)} %get-tuple-element.22), channel_id=1, source_target_pairs={{0,7},{1,0},{2,1},{3,2},{4,3},{5,4},{6,5},{7,6},{8,15},{9,8},{10,9... | collective-permute-start | bytes 122888 | tf_op jit(solution)/shard_map/ppermute | solution.py:433
  61.9 6.8 %collective-permute-start.6 = (f32[12,8,128]{2,1,0:T(8,128)S(1)}, f32[12,8,128]{2,1,0:T(8,128)S(1)}, u32[]{:S(2)}, u32[]{:S(2)}) collective-permute-start(f32[12,8,128]{2,1,0:T(8,128)S(1)} %get-tuple-element.31), channel_id=1, source_target_pairs={{0,8},{8,16},{16,24},{24,32},{32,40},{40,48},{48,56},{56,64},{64,7... | collective-permute-start | bytes 147464 | tf_op jit(solution)/shard_map/ppermute | solution.py:433
  63.1 5.6 %collective-permute-start.7 = (f32[12,8,128]{2,1,0:T(8,128)S(1)}, f32[12,8,128]{2,1,0:T(8,128)S(1)}, u32[]{:S(2)}, u32[]{:S(2)}) collective-permute-start(f32[12,8,128]{2,1,0:T(8,128)S(1)} %get-tuple-element.32), channel_id=1, source_target_pairs={{0,248},{8,0},{16,8},{24,16},{32,24},{40,32},{48,40},{56,48},{64,5... | collective-permute-start | bytes 147464 | tf_op jit(solution)/shard_map/ppermute | solution.py:433
  68.7 4.0 %collective-permute-start.8 = (f32[40,8,128]{2,1,0:T(8,128)S(1)}, f32[40,8,128]{2,1,0:T(8,128)S(1)}, u32[]{:S(2)}, u32[]{:S(2)}) collective-permute-start(f32[40,8,128]{2,1,0:T(8,128)S(1)} %pad_maximum_fusion.refs_5_), channel_id=1, source_target_pairs={{0,1},{1,2},{2,3},{3,4},{4,5},{5,6},{6,7},{7,0},{8,9},{9,10},{10,1... | collective-permute-start | bytes 491528 | tf_op jit(solution)/shard_map/ppermute | solution.py:433
  70.5 4.7 %collective-permute-start.9 = (f32[40,8,128]{2,1,0:T(8,128)S(1)}, f32[40,8,128]{2,1,0:T(8,128)S(1)}, u32[]{:S(2)}, u32[]{:S(2)}) collective-permute-start(f32[40,8,128]{2,1,0:T(8,128)S(1)} %pad_maximum_fusion.refs_5_), channel_id=1, source_target_pairs={{0,7},{1,0},{2,1},{3,2},{4,3},{5,4},{6,5},{7,6},{8,15},{9,8},{10,9... | collective-permute-start | bytes 491528 | tf_op jit(solution)/shard_map/ppermute | solution.py:433
  78.5 25.2 %all-to-all-start.1 = ((f32[256,2,128]{2,1,0:T(2,128)}), f32[256,2,128]{2,1,0:T(2,128)S(1)}, u32[]{:S(2)}, u32[]{:S(2)}) async-start(f32[256,2,128]{2,1,0:T(2,128)} %broadcast_in_dim.5), calls=%async_computation.1 | async-start | bytes 524288 | tf_op jit(solution)/shard_map/all_to_all | solution.py:443
  88.3 2.9 %collective-permute-start.10 = (f32[80,128]{1,0:T(8,128)S(1)}, f32[80,128]{1,0:T(8,128)S(1)}, u32[]{:S(2)}, u32[]{:S(2)}) collective-permute-start(f32[80,128]{1,0:T(8,128)S(1)} %get-tuple-element.27), channel_id=1, source_target_pairs={{0,1},{1,2},{2,3},{3,4},{4,5},{5,6},{6,7},{7,0},{8,9},{9,10},{10,1... | collective-permute-start | bytes 122888 | tf_op jit(solution)/shard_map/ppermute | solution.py:433
  89.9 3.9 %collective-permute-start.11 = (f32[80,128]{1,0:T(8,128)S(1)}, f32[80,128]{1,0:T(8,128)S(1)}, u32[]{:S(2)}, u32[]{:S(2)}) collective-permute-start(f32[80,128]{1,0:T(8,128)S(1)} %get-tuple-element.27), channel_id=1, source_target_pairs={{0,7},{1,0},{2,1},{3,2},{4,3},{5,4},{6,5},{7,6},{8,15},{9,8},{10,9... | collective-permute-start | bytes 122888 | tf_op jit(solution)/shard_map/ppermute | solution.py:433
where the time goes:
time: 110 us
  waiting for transfers between devices  44.9 us (41%)
  starting transfers between devices  42.2 us (38%)
  Pallas kernels  17.2 us (16%)
  local copies, waits for them, and re-layouts  5.56 us (5%)
    all_to_all x2, waiting for transfers between devices, to_all(): out = lax.all_to_all(copies, ('gz', 'gy'), 0, 0)  24.8 us
    ppermute x12, starting transfers between devices, shifted(): lax.ppermute(array, axis, [(i, (i + step) % count) for i in range(count)])  22.6 us
    ppermute x12, waiting for transfers between devices, shifted(): lax.ppermute(array, axis, [(i, (i + step) % count) for i in range(count)])  20.1 us
    all_to_all x2, starting transfers between devices, to_all(): out = lax.all_to_all(copies, ('gz', 'gy'), 0, 0)  19.6 us
    pallas_call x5, Pallas kernels, call(): pl.pallas_call(body, out_shape=outs, in_specs=[pl.BlockSpec(memory_space=...  17.2 us
    unnamed x15, local copies, waits for them, and re-layouts  3.88 us
  transfers between devices with their start and end apart: 14, of which 12 were waited for; matrix products, arithmetic and copies ran while one was open for 0% of the time, Pallas kernels for 0%

commit v1 on v0

--- a/solution.py
+++ b/solution.py
@@ -64,7 +64,6 @@
                 ref[base - 1 : base - 1 + size],
                 ref[base + 1 : base + 1 + size],
                 pltpu.roll(here, 1, 1),
-                pltpu.roll(here, 127, 1),
             ),
         )
 
@@ -73,70 +72,101 @@
             ref[0 : self.pad] = ref[self.rows : self.rows + self.pad]
             ref[self.pad + self.rows : 2 * self.pad + self.rows] = ref[self.pad : 2 * self.pad]
 
+    def shape(self):
+        return (self.rows + 2 * self.pad, 128)
+
     def build(self, kappa, faces):
+        for number in (0, 2):
+            faces[number, 0 : self.pad] = jnp.zeros((self.pad, 128), jnp.float32)
+            faces[number, self.pad + self.rows :] = jnp.zeros((self.pad, 128), jnp.float32)
         for at, size in self.chunks():
             here, around = self.neighbours(kappa, at, size)
             y = iota(size, 0) % self.ny + self.y_start
             x = iota(size, 1) % self.nx
-            keep = (None, None, y != 0, y != self.y_total - 1, x != 0, x != self.nx - 1)
-            total = jnp.full((size, 128), 1.0, jnp.float32)
-            for number in range(6):
-                face = harmonic(here, around[number])
-                if keep[number] is not None:
-                    face = jnp.where(keep[number], face, 0.0)
-                faces[number, at : at + size] = face
-                total = total + face
-            faces[6, at : at + size] = 0.8 / total
-            faces[7, at : at + size] = total
+            rows = slice(self.pad + at, self.pad + at + size)
+            faces[0, rows] = harmonic(here, around[0])
+            faces[2, rows] = jnp.where((y != 0) & (y != self.y_total), harmonic(here, around[2]), 0.0)
+            faces[3, rows] = jnp.where(x != 0, harmonic(here, around[4]), 0.0)
+        self.wrap(faces.at[0])
+        for at, size in self.chunks():
+            rows = slice(self.pad + at, self.pad + at + size)
+            z_low, around = self.neighbours(faces.at[0], at, size)
+            z_high = around[1]
+            y_high = faces[2, self.pad + at + 1 : self.pad + at + 1 + size]
+            x_low = faces[3, rows]
+            total = 1.0 + z_low + z_high + faces[2, rows] + y_high + x_low + pltpu.roll(x_low, 127, 1)
+            faces[1, rows] = z_high
+            faces[4, rows] = 0.8 / total
+            faces[5, rows] = total
 
     def coupled(self, field, source, faces, at, size):
         here, around = self.neighbours(field, at, size)
-        total = source[at : at + size]
-        for number in range(6):
-            total = total + faces[number, at : at + size] * around[number]
+        rows = slice(self.pad + at, self.pad + at + size)
+        next_rows = slice(self.pad + at + 1, self.pad + at + 1 + size)
+        x_low = faces[3, rows]
+        total = (
+            source[at : at + size]
+            + faces[0, rows] * around[0]
+            + faces[1, rows] * around[1]
+            + faces[2, rows] * around[2]
+            + faces[2, next_rows] * around[3]
+            + x_low * around[4]
+            + pltpu.roll(x_low * here, 127, 1)
+        )
         return here, total
 
     def start(self, field, source, faces):
         for at, size in self.chunks():
-            field[self.pad + at : self.pad + at + size] = faces[6, at : at + size] * source[at : at + size]
+            rows = slice(self.pad + at, self.pad + at + size)
+            field[rows] = faces[4, rows] * source[at : at + size]
         self.wrap(field)
 
     def relax(self, field, target, source, faces, start=0, count=None):
         for at, size in self.chunks(start, count):
             here, total = self.coupled(field, source, faces, at, size)
-            target[self.pad + at : self.pad + at + size] = 0.2 * here + faces[6, at : at + size] * total
+            rows = slice(self.pad + at, self.pad + at + size)
+            target[rows] = 0.2 * here + faces[4, rows] * total
         self.wrap(target)
 
     def defect(self, field, source, faces, out, start=0, count=None):
         for at, size in self.chunks(start, count):
             here, total = self.coupled(field, source, faces, at, size)
-            out[at - start : at - start + size] = total - faces[7, at : at + size] * here
+            diagonal = faces[5, self.pad + at : self.pad + at + size]
+            out[at - start : at - start + size] = total - diagonal * here
 
     def pairs(self, ref):
         half = self.rows // 2
         return ref[pl.ds(0, half, stride=2), :] + ref[pl.ds(1, half, stride=2), :]
 
 
-def kappa_body(class_ref, diff_ref, phases_ref, grains_ref, conc_ref, kappa_ref, up_ref, down_ref):
-    num_phases, num_classes = diff_ref.shape
+def kappa_body(class_hbm, diff_hbm, phases_hbm, grains_hbm, conc_hbm, kappa_ref, up_ref, down_ref, classes, diff, phases, grains, sems):
+    num_phases, num_classes = diff.shape
+    pairs = [(class_hbm, classes), (diff_hbm, diff)]
     for block in range(4):
-        grain = grains_ref[4 * block]
-        phase = phases_ref[4 * block]
-        cls = jnp.zeros(grain.shape, jnp.int32)
-        for number in range(class_ref.shape[0]):
-            cls = jnp.where(grain == number, class_ref[number], cls)
-        value = jnp.ones(grain.shape, jnp.float32)
-        for p in range(num_phases):
-            for c in range(num_classes):
-                value = jnp.where((phase == p) & (cls == c), diff_ref[p, c], value)
-        kappa_ref[block] = value
-        if block > 0:
-            up_ref[HALO + block - 1] = value
-        if block < 3:
-            down_ref[HALO + block] = value
-    for z in range(HALO):
-        up_ref[z] = conc_ref[16 - HALO + z]
-        down_ref[z] = conc_ref[z]
+        pairs += [(phases_hbm.at[4 * block], phases.at[block]), (grains_hbm.at[4 * block], grains.at[block])]
+    pairs += [
+        (conc_hbm.at[16 - HALO : 16], up_ref.at[0:HALO]),
+        (conc_hbm.at[0:HALO], down_ref.at[0:HALO]),
+    ]
+    copies = [pltpu.make_async_copy(source, target, sems.at[i]) for i, (source, target) in enumerate(pairs)]
+    for copy in copies:
+        copy.start()
+    for copy in copies[:-2]:
+        copy.wait()
+    grain = grains[...]
+    phase = phases[...]
+    cls = jnp.zeros(grain.shape, jnp.int32)
+    for number in range(classes.shape[0]):
+        cls = jnp.where(grain == number, classes[number], cls)
+    value = jnp.ones(grain.shape, jnp.float32)
+    for p in range(num_phases):
+        for c in range(num_classes):
+            value = jnp.where((phase == p) & (cls == c), diff[p, c], value)
+    kappa_ref[...] = value
+    up_ref[HALO:] = value[1:]
+    down_ref[HALO:] = value[:3]
+    for copy in copies[-2:]:
+        copy.wait()
 
 
 def window(refs, plane):
@@ -221,18 +251,23 @@
     return out
 
 
-def down_body(first, *refs):
+def down_body(first, copies, *refs):
     index, low, own, high = refs[:4]
     sources = (low, own, high)
     refs = refs[4:]
     if not first:
-        fields, refs = refs[:3], refs[3:]
+        fields, coefs, z_faces, faces, refs = refs[:3], refs[3], refs[4], refs[5], refs[6:]
     chunk, edge, kept, source_one, kept_one = refs[:5]
-    kappa, coefs, z_faces, va, vb, rs, spread, packed, kappa_one, faces, oa, tmp = refs[5:]
+    refs = refs[5:]
+    if first:
+        coefs, z_faces, faces, refs = refs[0], refs[1], refs[2], refs[3:]
+    va, vb, rs, oa, tmp = refs[:5]
     y_device = index[1]
-    build_fine(sources, y_device, kappa, coefs, z_faces)
     level = level_one(y_device)
-    build_one(level, kappa, spread, packed, kappa_one, faces)
+    if first:
+        kappa, spread, packed, kappa_one = refs[5:]
+        build_fine(sources, y_device, kappa, coefs, z_faces)
+        build_one(level, kappa, spread, packed, kappa_one, faces)
     zero = jnp.zeros((WY, 128), jnp.float32)
     for ref in (va, vb):
         ref[0:WY] = zero
@@ -275,49 +310,58 @@
         tmp[z * 16 : z * 16 + 16] = tmp[z * 32 : z * 32 + 16] + tmp[z * 32 + 16 : z * 32 + 32]
     halves = tmp[pl.ds(0, 32, stride=2), :] + tmp[pl.ds(1, 32, stride=2), :]
     mean_two = lane_map(lambda r, c: matrix((r < 64) & (r // 2 == c % 32), 0.125))
-    chunk[0:2] = to_chunk(dot(halves, mean_two))[2:4]
+    values = [to_chunk(dot(halves, mean_two))[2:4]]
     if first:
         pick_two = lane_map(lambda r, c: matrix((r < 64) & (r == 2 * (c % 32)), 0.5))
-        chunk[2:4] = to_chunk(dot(packed[pl.ds(48, 32, stride=2), :], pick_two))[2:4]
+        values.append(to_chunk(dot(packed[pl.ds(48, 32, stride=2), :], pick_two))[2:4])
+    repeats = 4 // len(values)
+    tile = jnp.concatenate(values * repeats, axis=0)
+    for at in range(0, copies // repeats):
+        chunk[at * 8 : at * 8 + 8] = tile
     for plane in range(20):
         edge[plane * 4 : plane * 4 + 4] = kept_one[16 + plane * 16 + 4 : 16 + plane * 16 + 8]
 
 
-def up_body(first, z_devices, *refs):
-    index, low, own, high, gathered = refs[:5]
-    refs = refs[5:]
-    if first:
-        labelled = gathered
+def coarse_levels(z_devices):
+    return (
+        Level(z_devices, 16, 32, 4, 16, True, 0, 16, 128),
+        Level(z_devices, 8, 16, 2, 8, True, 0, 8, 128),
+        Level(z_devices, 4, 8, 1, 8, True, 0, 4, 128),
+    )
+
+
+def coarse_body(first, z_devices, *refs):
+    two, three, four = coarse_levels(z_devices)
+    index, gathered = refs[:2]
+    refs = refs[2:]
+    if first:
+        near, f2, f3, f4 = refs[:4]
+        refs = refs[4:]
     else:
-        labelled, refs = refs[0], refs[1:]
-    edge_low, edge_high, kept, source_one, kept_one, out = refs[:6]
-    (kappa, coefs, z_faces, va, vb, spread, packed, kappa_one, faces, oa, ob) = refs[6:17]
-    (k2, g2, a2, b2, f2, r2, k3, g3, a3, b3, f3, r3, k4, g4, a4, b4, f4, r4) = refs[17:]
-    sources = (low, own, high)
-    z_device, y_device = index[0], index[1]
-    two = Level(z_devices, 16, 32, 4, 16, True, 0, 16, 128)
-    three = Level(z_devices, 8, 16, 2, 8, True, 0, 8, 128)
-    four = Level(z_devices, 4, 8, 1, 8, True, 0, 4, 128)
-
-    chunks = z_devices * 8
-    for part in range(2):
-        k2[pl.ds(two.pad + part, chunks, stride=2), :] = labelled[pl.ds(2 + part, chunks, stride=4), :]
-        if first:
-            g2[pl.ds(part, chunks, stride=2), :] = gathered[pl.ds(part, chunks, stride=4), :]
-    if not first:
-        g2 = gathered
-    two.wrap(k2)
-    two.build(k2, f2)
+        f2, f3, f4, near = refs[:4]
+        refs = refs[4:]
+    a2, b2, r2, a3, b3, r3, g3, a4, b4, g4 = refs[:10]
+    z_device = index[0]
     mean_three = lane_map(lambda r, c: matrix(c % 32 == (r // 64) * 16 + (r % 32) // 2, 0.125))
     mean_four = lane_map(lambda r, c: matrix((r < 32) & (c % 8 == (r % 16) // 2), 0.125))
-    r2[...] = k2[two.pad : two.pad + two.rows]
-    k3[three.pad : three.pad + three.rows] = 0.5 * dot(two.pairs(r2), mean_three)
-    three.wrap(k3)
-    three.build(k3, f3)
-    r3[...] = k3[three.pad : three.pad + three.rows]
-    k4[four.pad : four.pad + four.rows] = 0.5 * dot(three.pairs(r3), mean_four)
-    four.wrap(k4)
-    four.build(k4, f4)
+    if first:
+        g2, k2, k3, k4 = refs[10:]
+        chunks = z_devices * 8
+        for part in range(2):
+            k2[pl.ds(two.pad + part, chunks, stride=2), :] = gathered[pl.ds(2 + part, chunks, stride=4), :]
+            g2[pl.ds(part, chunks, stride=2), :] = gathered[pl.ds(part, chunks, stride=4), :]
+        two.wrap(k2)
+        two.build(k2, f2)
+        r2[...] = k2[two.pad : two.pad + two.rows]
+        k3[three.pad : three.pad + three.rows] = 0.5 * dot(two.pairs(r2), mean_three)
+        three.wrap(k3)
+        three.build(k3, f3)
+        r3[...] = k3[three.pad : three.pad + three.rows]
+        k4[four.pad : four.pad + four.rows] = 0.5 * dot(three.pairs(r3), mean_four)
+        four.wrap(k4)
+        four.build(k4, f4)
+    else:
+        g2 = gathered
 
     two.start(a2, g2, f2)
     two.relax(a2, b2, g2, f2)
@@ -350,12 +394,13 @@
     correct(two, b2, b3[three.pad : three.pad + three.rows], r2, from_three)
     two.relax(b2, a2, g2, f2)
     two.relax(a2, b2, g2, f2)
-
-    build_fine(sources, y_device, kappa, coefs, z_faces)
+    near[...] = b2[pl.ds(pl.multiple_of(z_device * 16, 16), 48), :]
+
+
+def up_body(index, low, own, high, coefs, z_faces, faces, near, edge_low, edge_high, kept, source_one, kept_one, out, va, vb, spread, oa, ob):
+    sources = (low, own, high)
+    y_device = index[1]
     level = level_one(y_device)
-    build_one(level, kappa, spread, packed, kappa_one, faces)
-
-    near = b2[pl.ds(pl.multiple_of(z_device * 16, 16), 48), :]
     rows = matrix(iota(16, 1, 16) == y_device * 2 - 2 + iota(16, 0, 16) // 2, 1.0)
     spread_y = jnp.concatenate([dot(rows, near[16 * part : 16 * part + 16]) for part in range(3)], axis=0)
     by_z = [
@@ -390,42 +435,70 @@
     return jax.ShapeDtypeStruct(shape, jnp.float32)
 
 
-def call(body, outs, scratch, args, smem):
+def call(body, outs, scratch, args, smem=1, any_space=False):
     vmem = pl.BlockSpec(memory_space=pltpu.VMEM)
+    rest = pl.BlockSpec(memory_space=pl.ANY) if any_space else vmem
     return pl.pallas_call(
         body,
         out_shape=outs,
-        in_specs=[pl.BlockSpec(memory_space=pltpu.SMEM)] * smem + [vmem] * (len(args) - smem),
+        in_specs=[pl.BlockSpec(memory_space=pltpu.SMEM)] * smem + [rest] * (len(args) - smem),
         out_specs=[vmem] * len(outs),
-        scratch_shapes=[pltpu.VMEM(shape, jnp.float32) for shape in scratch],
+        scratch_shapes=[pltpu.VMEM(s, jnp.float32) if isinstance(s, tuple) else s for s in scratch],
         compiler_params=pltpu.CompilerParams(vmem_limit_bytes=VMEM_BYTES),
     )(*args)
 
 
-FINE = [(16 + BLOCKS * WY, 128), (BLOCKS, 11, WY, 128), (BLOCKS + 1, WY, 128), ((WZ + 2) * WY, 128), ((WZ + 2) * WY, 128)]
-ONE = [(320, 128), (160, 128), (352, 128), (8, 320, 128), (352, 128)]
-
-
-def down(index, sources, fields):
+FIELD = ((WZ + 2) * WY, 128)
+COEFS = [(BLOCKS, 11, WY, 128), (BLOCKS + 1, WY, 128), (6, 352, 128)]
+
+
+def device_count():
+    return lax.axis_size("gz") * lax.axis_size("gy")
+
+
+def down(index, sources, fields, coefs):
     first = fields is None
+    copies = device_count()
     outs = [
-        floats(4 if first else 2, 128), floats(80, 128), floats(20 * WY, 128), floats(320, 128), floats(352, 128)
+        floats(copies * (4 if first else 2), 128),
+        floats(80, 128),
+        floats(20 * WY, 128),
+        floats(320, 128),
+        floats(352, 128),
     ]
-    scratch = FINE + [(640, 128)] + ONE + [(128, 128)]
-    args = [index, *sources] + ([] if first else list(fields))
-    return call(lambda *refs: down_body(first, *refs), outs, scratch, args, 1)
-
-
-def up(index, sources, gathered, labelled, edges, kept):
-    first = labelled is None
+    scratch = [FIELD, FIELD, (640, 128), (352, 128), (128, 128)]
+    if first:
+        outs += [floats(*shape) for shape in COEFS]
+        scratch += [(16 + BLOCKS * WY, 128), (320, 128), (160, 128), (352, 128)]
+        args = [index, *sources]
+    else:
+        args = [index, *sources, *fields, *coefs]
+    result = call(lambda *refs: down_body(first, copies, *refs), outs, scratch, args)
+    return result[0], result[1], result[2:5], result[5:] if first else coefs
+
+
+def coarse(index, gathered, faces):
+    first = faces is None
     z_devices = lax.axis_size("gz")
-    scratch = FINE + ONE + [(352, 128)]
-    for ny, pad in ((16, 16), (8, 8), (4, 8)):
-        rows = z_devices * ny
-        padded = (rows + 2 * pad, 128)
-        scratch += [padded, (rows, 128), padded, padded, (8, rows, 128), (rows, 128)]
-    args = [index, *sources, gathered] + ([] if first else [labelled]) + [*edges, *kept]
-    return call(lambda *refs: up_body(first, z_devices, *refs), [floats(16, 8, 128)], scratch, args, 1)[0]
+    levels = coarse_levels(z_devices)
+    outs, scratch = [floats(48, 128)], []
+    if first:
+        outs += [floats(6, *level.shape()) for level in levels]
+    for number, level in enumerate(levels):
+        scratch += [level.shape(), level.shape(), (level.rows, 128)]
+        if number > 0:
+            scratch += [(level.rows, 128)]
+    scratch = scratch[:9] + [(levels[2].rows, 128)]
+    if first:
+        scratch += [(levels[0].rows, 128)] + [level.shape() for level in levels]
+    args = [index, gathered] + ([] if first else list(faces))
+    near, *new = call(lambda *refs: coarse_body(first, z_devices, *refs), outs, scratch, args)
+    return near, new if first else faces
+
+
+def up(index, sources, coefs, near, edges, kept):
+    scratch = [FIELD, FIELD, (320, 128), (352, 128), (352, 128)]
+    return call(up_body, [floats(16, 8, 128)], scratch, [index, *sources, *coefs, near, *edges, *kept])[0]
 
 
 def shifted(array, axis, step):
@@ -437,21 +510,38 @@
     return shifted(array, axis, 1), shifted(array, axis, -1)
 
 
-def to_all(chunk):
-    devices = lax.axis_size("gz") * lax.axis_size("gy")
-    copies = jnp.broadcast_to(chunk[None], (devices,) + chunk.shape)
+def to_all(copies):
+    devices = device_count()
+    copies = copies.reshape(devices, copies.shape[0] // devices, 128)
     out = lax.all_to_all(copies, ("gz", "gy"), 0, 0)
-    return out.reshape(devices * chunk.shape[0], 128)
+    return out.reshape(out.shape[0] * out.shape[1], 128)
+
+
+def cycle(index, sources, fields, coefs, coarse_faces):
+    copies, edge, kept, coefs = down(index, sources, fields, coefs)
+    gathered = to_all(copies)
+    edge, _ = lax.optimization_barrier((edge, gathered))
+    edges = both_sides(edge, "gy")
+    near, coarse_faces = coarse(index, gathered, coarse_faces)
+    return up(index, sources, coefs, near, edges, kept), coefs, coarse_faces
 
 
 def per_device(concentration, phases, grains, grain_class, diffusivity):
     index = jnp.stack([lax.axis_index("gz"), lax.axis_index("gy")]).astype(jnp.int32)
+    plane = (4,) + phases.shape[1:]
     kappa, up_part, down_part = call(
         kappa_body,
-        [floats(4, 8, 128), floats(HALO + 3, 8, 128), floats(HALO + 3, 8, 128)],
-        [],
+        [floats(*plane), floats(HALO + 3, 8, 128), floats(HALO + 3, 8, 128)],
+        [
+            pltpu.SMEM(grain_class.shape, jnp.int32),
+            pltpu.SMEM(diffusivity.shape, jnp.float32),
+            pltpu.VMEM(plane, jnp.int32),
+            pltpu.VMEM(plane, jnp.int32),
+            pltpu.SemaphoreType.DMA((12,)),
+        ],
         [grain_class, diffusivity, phases, grains, concentration],
-        2,
+        0,
+        True,
     )
     before = shifted(up_part, "gz", 1)
     after = shifted(down_part, "gz", -1)
@@ -460,20 +550,13 @@
     )
     low, high = both_sides(own, "gy")
     sources = (low, own, high)
-
-    chunk, edge, *kept = down(index, sources, None)
-    edges = both_sides(edge, "gy")
-    labelled = to_all(chunk)
-    field = up(index, sources, labelled, None, edges, kept)
+    field, coefs, coarse_faces = cycle(index, sources, None, None, None)
 
     before = shifted(field[16 - HALO :], "gz", 1)
     after = shifted(field[:HALO], "gz", -1)
     field = jnp.concatenate([before, field, after], axis=0)
     low, high = both_sides(field, "gy")
-    chunk, edge, *kept = down(index, sources, (low, field, high))
-    edges = both_sides(edge, "gy")
-    gathered = to_all(chunk)
-    return up(index, sources, gathered, labelled, edges, kept)
+    return cycle(index, sources, (low, field, high), coefs, coarse_faces)[0]
 
 
 def solution(mesh):

time: 110 us -> 110 us (level)
  blocking collectives: 0 us -> 56.1 us
  waiting for transfers between devices: 44.9 us -> 10 us
  starting transfers between devices: 42.2 us -> 21.8 us
  local copies, waits for them, and re-layouts: 5.56 us -> 3.89 us
    all_to_all x0 -> x2, blocking collectives: none -> 56.1 us  [to_all(): out = lax.all_to_all(copies, ('gz', 'gy'), 0, 0)]
    all_to_all x2 -> x0, waiting for transfers between devices: 24.8 us -> none  [to_all(): out = lax.all_to_all(copies, ('gz', 'gy'), 0, 0)]
    all_to_all x2 -> x0, starting transfers between devices: 19.6 us -> none  [to_all(): out = lax.all_to_all(copies, ('gz', 'gy'), 0, 0)]
    ppermute x12, waiting for transfers between devices: 20.1 us -> 10 us  [shifted(): lax.ppermute(array, axis, [(i, (i + step) % count) for i in range(count)])]
    broadcast_in_dim x2 -> x0, local copies, waits for them, and re-layouts: 1.68 us -> none  [to_all(): copies = jnp.broadcast_to(chunk[None], (devices,) + chunk.shape)]
    pallas_call x5 -> x7, Pallas kernels: 17.2 us -> 18 us  [call(): pl.pallas_call(body, out_shape=outs, in_specs=[pl.BlockSpec(memory_space=...]
  transfers between devices with their start and end apart: 14 -> 12, of which waited for: 12 -> 4; matrix products, arithmetic and copies ran while one was open for 0% -> 0% of each run, Pallas kernels for 0% -> 8%
where the time goes in v1:
time: 110 us
  blocking collectives  56.1 us (51%)
  starting transfers between devices  21.8 us (20%)
  Pallas kernels  18 us (16%)
  waiting for transfers between devices  10 us (9%)
  local copies, waits for them, and re-layouts  3.89 us (4%)
    all_to_all x2, blocking collectives, to_all(): out = lax.all_to_all(copies, ('gz', 'gy'), 0, 0)  56.1 us
    ppermute x12, starting transfers between devices, shifted(): lax.ppermute(array, axis, [(i, (i + step) % count) for i in range(count)])  21.8 us
    pallas_call x7, Pallas kernels, call(): pl.pallas_call(body, out_shape=outs, in_specs=[pl.BlockSpec(memory_space=...  18 us
    ppermute x12, waiting for transfers between devices, shifted(): lax.ppermute(array, axis, [(i, (i + step) % count) for i in range(count)])  10 us
    unnamed x15, local copies, waits for them, and re-layouts  3.88 us
  transfers between devices with their start and end apart: 12, of which 4 were waited for; matrix products, arithmetic and copies ran while one was open for 0% of the time, Pallas kernels for 8%

profile of v1, /device:TPU:1, one launch (start us, length us, event | category | flops | bytes accessed | tf_op | source)
XLA Modules:
  0.0 110.1 jit_solution(9495242308101385670)
XLA Ops:
  0.0 0.8 copy-done
  0.8 0.8 copy-done.1
  1.7 0.8 copy-done.2
  4.7 2.5 %collective-permute-start = (f32[15,8,128]{2,1,0:T(8,128)S(1)}, f32[15,8,128]{2,1,0:T(8,128)S(1)}, u32[]{:S(2)}, u32[]{:S(2)}) collective-permute-start(f32[15,8,128]{2,1,0:T(8,128)S(1)} %get-tuple-element.27), channel_id=1, source_target_pairs={{0,8},{8,16},{16,24},{24,32},{32,40},{40,48},{48,56},{56,64},{64,7... | collective-permute-start | bytes 184328 | tf_op jit(solution)/shard_map/ppermute | solution.py:506
  7.2 6.5 %collective-permute-start.1 = (f32[15,8,128]{2,1,0:T(8,128)S(1)}, f32[15,8,128]{2,1,0:T(8,128)S(1)}, u32[]{:S(2)}, u32[]{:S(2)}) collective-permute-start(f32[15,8,128]{2,1,0:T(8,128)S(1)} %get-tuple-element.28), channel_id=1, source_target_pairs={{0,248},{8,0},{16,8},{24,16},{32,24},{40,32},{48,40},{56,48},{64,5... | collective-permute-start | bytes 184328 | tf_op jit(solution)/shard_map/ppermute | solution.py:506
  13.7 1.5 %collective-permute-done = f32[15,8,128]{2,1,0:T(8,128)S(1)} collective-permute-done((f32[15,8,128]{2,1,0:T(8,128)S(1)}, f32[15,8,128]{2,1,0:T(8,128)S(1)}, u32[]{:S(2)}, u32[]{:S(2)}) %collective-permute-start) | collective-permute-done | bytes 61472 | tf_op jit(solution)/shard_map/ppermute | solution.py:506
  15.3 1.6 %collective-permute-start.3 = (f32[50,8,128]{2,1,0:T(8,128)S(1)}, f32[50,8,128]{2,1,0:T(8,128)S(1)}, u32[]{:S(2)}, u32[]{:S(2)}) collective-permute-start(f32[50,8,128]{2,1,0:T(8,128)S(1)} %constant_dynamic-update-slice_fusion.refs_2_.own), channel_id=1, source_target_pairs={{0,7},{1,0},{2,1},{3,2},{4,3},{5,4},{6,5},{7,6},{8,15},{9,8},{10,9... | collective-permute-start | bytes 614408 | tf_op jit(solution)/shard_map/ppermute | solution.py:506
  16.8 1.1 %collective-permute-start.2 = (f32[50,8,128]{2,1,0:T(8,128)S(1)}, f32[50,8,128]{2,1,0:T(8,128)S(1)}, u32[]{:S(2)}, u32[]{:S(2)}) collective-permute-start(f32[50,8,128]{2,1,0:T(8,128)S(1)} %constant_dynamic-update-slice_fusion.refs_2_.own), channel_id=1, source_target_pairs={{0,1},{1,2},{2,3},{3,4},{4,5},{5,6},{6,7},{7,0},{8,9},{9,10},{10,1... | collective-permute-start | bytes 614408 | tf_op jit(solution)/shard_map/ppermute | solution.py:506
  18.0 3.3 %collective-permute-done.3.refs_3_.high = f32[50,8,128]{2,1,0:T(8,128)S(1)} collective-permute-done((f32[50,8,128]{2,1,0:T(8,128)S(1)}, f32[50,8,128]{2,1,0:T(8,128)S(1)}, u32[]{:S(2)}, u32[]{:S(2)}) %collective-permute-start.3) | collective-permute-done | bytes 204832 | tf_op jit(solution)/shard_map/ppermute | solution.py:506
  21.4 2.2 %shard_map.56 = (f32[1024,128]{1,0:T(8,128)S(1)}, f32[80,128]{1,0:T(8,128)S(1)}, f32[480,128]{1,0:T(8,128)S(1)}, f32[320,128]{1,0:T(8,128)S(1)}, f32[352,128]{1,...) custom-call(s32[2]{0:T(128)S(1)} %pad_add_fusion.refs_0_.index, ...), custom_call_target="tpu_custom_call" | custom-call | tf_op jit(solution)/shard_map/pallas_call | solution.py:441
  23.5 30.7 %all_to_all.10 = f32[256,4,128]{2,1,0:T(4,128)S(1)} all-to-all(f32[256,4,128]{2,1,0:T(4,128)S(1)} %bitcast.8), channel_id=1, replica_groups=mesh['gz'=32,'gy'=8] {'gz','gy'}, dimensions={0} | all-to-all | bytes 1048576 | tf_op jit(solution)/shard_map/all_to_all | solution.py:516
  54.2 1.7 %collective-permute-start.4 = (f32[80,128]{1,0:T(8,128)S(1)}, f32[80,128]{1,0:T(8,128)S(1)}, u32[]{:S(2)}, u32[]{:S(2)}) collective-permute-start(f32[80,128]{1,0:T(8,128)S(1)} %get-tuple-element.36), channel_id=1, source_target_pairs={{0,1},{1,2},{2,3},{3,4},{4,5},{5,6},{6,7},{7,0},{8,9},{9,10},{10,1... | collective-permute-start | bytes 122888 | tf_op jit(solution)/shard_map/ppermute | solution.py:506
  56.0 4.9 %shard_map.57 = (f32[48,128]{1,0:T(8,128)S(1)}, f32[6,544,128]{2,1,0:T(8,128)S(1)}, f32[6,272,128]{2,1,0:T(8,128)S(1)}, f32[6,144,128]{2,1,0:T(8,128)S(1)}) custom-call(s32[2]{0:T(128)S(1)} %pad_add_fusion.refs_0_.index, f32[1024,128]{1,0:T(8,128)S(1)} %bitcast.6), custom_call_target="tpu_custom_call" | custom-call | tf_op jit(solution)/shard_map/pallas_call | solution.py:441
  60.9 1.7 %shard_map.58 = f32[16,8,128]{2,1,0:T(8,128)S(1)} custom-call(s32[2]{0:T(128)S(1)} %pad_add_fusion.refs_0_.index, f32[50,8,128]{2,1,0:T(8,128)S(1)} %collective-permute-done.2.refs_1_.low, f32[50,8,128]{2,1,0:T(8,128)S(1)} %constant_dynamic-update-slice_fusion.refs_2_.own, f32[50,8,128]{2,1,0:T(8,128)S(1)} %collective-permute-done.3.refs_3_.high, ...), custom_call_target="tpu_custom_call" | custom-call | tf_op jit(solution)/shard_map/pallas_call | solution.py:441
  62.6 1.1 %collective-permute-start.6 = (f32[12,8,128]{2,1,0:T(8,128)S(1)}, f32[12,8,128]{2,1,0:T(8,128)S(1)}, u32[]{:S(2)}, u32[]{:S(2)}) collective-permute-start(f32[12,8,128]{2,1,0:T(8,128)S(1)} %get-tuple-element.49), channel_id=1, source_target_pairs={{0,8},{8,16},{16,24},{24,32},{32,40},{40,48},{48,56},{56,64},{64,7... | collective-permute-start | bytes 147464 | tf_op jit(solution)/shard_map/ppermute | solution.py:506
  63.7 3.7 %collective-permute-start.7 = (f32[12,8,128]{2,1,0:T(8,128)S(1)}, f32[12,8,128]{2,1,0:T(8,128)S(1)}, u32[]{:S(2)}, u32[]{:S(2)}) collective-permute-start(f32[12,8,128]{2,1,0:T(8,128)S(1)} %get-tuple-element.50), channel_id=1, source_target_pairs={{0,248},{8,0},{16,8},{24,16},{32,24},{40,32},{48,40},{56,48},{64,5... | collective-permute-start | bytes 147464 | tf_op jit(solution)/shard_map/ppermute | solution.py:506
  67.4 2.2 %collective-permute-done.6 = f32[12,8,128]{2,1,0:T(8,128)S(1)} collective-permute-done((f32[12,8,128]{2,1,0:T(8,128)S(1)}, f32[12,8,128]{2,1,0:T(8,128)S(1)}, u32[]{:S(2)}, u32[]{:S(2)}) %collective-permute-start.6) | collective-permute-done | bytes 49184 | tf_op jit(solution)/shard_map/ppermute | solution.py:506
  70.2 1.2 %collective-permute-start.8 = (f32[40,8,128]{2,1,0:T(8,128)S(1)}, f32[40,8,128]{2,1,0:T(8,128)S(1)}, u32[]{:S(2)}, u32[]{:S(2)}) collective-permute-start(f32[40,8,128]{2,1,0:T(8,128)S(1)} %pad_maximum_fusion.refs_5_), channel_id=1, source_target_pairs={{0,1},{1,2},{2,3},{3,4},{4,5},{5,6},{6,7},{7,0},{8,9},{9,10},{10,1... | collective-permute-start | bytes 491528 | tf_op jit(solution)/shard_map/ppermute | solution.py:506
  71.4 3.0 %collective-permute-done.9.refs_6_ = f32[40,8,128]{2,1,0:T(8,128)S(1)} collective-permute-done((f32[40,8,128]{2,1,0:T(8,128)S(1)}, f32[40,8,128]{2,1,0:T(8,128)S(1)}, u32[]{:S(2)}, u32[]{:S(2)}) %collective-permute-start.9) | collective-permute-done | bytes 163872 | tf_op jit(solution)/shard_map/ppermute | solution.py:506
  74.4 2.1 %shard_map.59 = (f32[512,128]{1,0:T(8,128)S(1)}, f32[80,128]{1,0:T(8,128)S(1)}, f32[480,128]{1,0:T(8,128)S(1)}, f32[320,128]{1,0:T(8,128)S(1)}, f32[352,128]{1,0:T(8,128)S(1)}) custom-call(s32[2]{0:T(128)S(1)} %pad_add_fusion.refs_0_.index, f32[50,8,128]{2,1,0:T(8,128)S(1)} %collective-permute-done.2.refs_1_.low, ...), custom_call_target="tpu_custom_call" | custom-call | tf_op jit(solution)/shard_map/pallas_call | solution.py:441
  76.5 25.4 %all_to_all.11 = f32[256,2,128]{2,1,0:T(2,128)S(1)} all-to-all(f32[256,2,128]{2,1,0:T(2,128)S(1)} %bitcast.9), channel_id=1, replica_groups=mesh['gz'=32,'gy'=8] {'gz','gy'}, dimensions={0} | all-to-all | bytes 524288 | tf_op jit(solution)/shard_map/all_to_all | solution.py:516
  101.9 1.7 %collective-permute-start.10 = (f32[80,128]{1,0:T(8,128)S(1)}, f32[80,128]{1,0:T(8,128)S(1)}, u32[]{:S(2)}, u32[]{:S(2)}) collective-permute-start(f32[80,128]{1,0:T(8,128)S(1)} %get-tuple-element.45), channel_id=1, source_target_pairs={{0,1},{1,2},{2,3},{3,4},{4,5},{5,6},{6,7},{7,0},{8,9},{9,10},{10,1... | collective-permute-start | bytes 122888 | tf_op jit(solution)/shard_map/ppermute | solution.py:506
  103.6 4.2 %shard_map.60.near = f32[48,128]{1,0:T(8,128)S(1)} custom-call(s32[2]{0:T(128)S(1)} %pad_add_fusion.refs_0_.index, f32[512,128]{1,0:T(8,128)S(1)} %bitcast.7, f32[6,544,128]{2,1,0:T(8,128)S(1)} %get-tuple-element.41.refs_2_, f32[6,272,128]{2,1,0:T(8,128)S(1)} %get-tuple-element.42.refs_3_, f32[6,144,128]{2,1,0:T(8,128)S(1)} %get-tuple-element.43.refs_4_), custom_call_target="tpu_custom_call" | custom-call | tf_op jit(solution)/shard_map/pallas_call | solution.py:441
  107.8 2.3 %shard_map.61 = f32[16,8,128]{2,1,0:T(8,128)} custom-call(s32[2]{0:T(128)S(1)} %pad_add_fusion.refs_0_.index, f32[50,8,128]{2,1,0:T(8,128)S(1)} %collective-permute-done.2.refs_1_.low, f32[50,8,128]{2,1,0:T(8,128)S(1)} %constant_dynamic-update-slice_fusion.refs_2_.own, f32[50,8,128]{2,1,0:T(8,128)S(1)} %collective-permute-done.3.refs_3_.high, ...), custom_call_target="tpu_custom_call" | custom-call | tf_op jit(solution)/shard_map/pallas_call | solution.py:441
  (28 shorter events, 2.8 us)
Async XLA Ops:
  0.0 0.8 copy-start
  0.8 0.8 copy-start.1
  1.7 0.8 copy-start.2
  2.5 0.7 copy-start.3
  3.2 0.7 copy-start.4
  4.7 10.5 %collective-permute-start = (f32[15,8,128]{2,1,0:T(8,128)S(1)}, f32[15,8,128]{2,1,0:T(8,128)S(1)}, u32[]{:S(2)}, u32[]{:S(2)}) collective-permute-start(f32[15,8,128]{2,1,0:T(8,128)S(1)} %get-tuple-element.27), channel_id=1, source_target_pairs={{0,8},{8,16},{16,24},{24,32},{32,40},{40,48},{48,56},{56,64},{64,7... | collective-permute-start | bytes 184328 | tf_op jit(solution)/shard_map/ppermute | solution.py:506
  7.2 8.0 %collective-permute-start.1 = (f32[15,8,128]{2,1,0:T(8,128)S(1)}, f32[15,8,128]{2,1,0:T(8,128)S(1)}, u32[]{:S(2)}, u32[]{:S(2)}) collective-permute-start(f32[15,8,128]{2,1,0:T(8,128)S(1)} %get-tuple-element.28), channel_id=1, source_target_pairs={{0,248},{8,0},{16,8},{24,16},{32,24},{40,32},{48,40},{56,48},{64,5... | collective-permute-start | bytes 184328 | tf_op jit(solution)/shard_map/ppermute | solution.py:506
  15.3 6.1 %collective-permute-start.3 = (f32[50,8,128]{2,1,0:T(8,128)S(1)}, f32[50,8,128]{2,1,0:T(8,128)S(1)}, u32[]{:S(2)}, u32[]{:S(2)}) collective-permute-start(f32[50,8,128]{2,1,0:T(8,128)S(1)} %constant_dynamic-update-slice_fusion.refs_2_.own), channel_id=1, source_target_pairs={{0,7},{1,0},{2,1},{3,2},{4,3},{5,4},{6,5},{7,6},{8,15},{9,8},{10,9... | collective-permute-start | bytes 614408 | tf_op jit(solution)/shard_map/ppermute | solution.py:506
  16.8 4.5 %collective-permute-start.2 = (f32[50,8,128]{2,1,0:T(8,128)S(1)}, f32[50,8,128]{2,1,0:T(8,128)S(1)}, u32[]{:S(2)}, u32[]{:S(2)}) collective-permute-start(f32[50,8,128]{2,1,0:T(8,128)S(1)} %constant_dynamic-update-slice_fusion.refs_2_.own), channel_id=1, source_target_pairs={{0,1},{1,2},{2,3},{3,4},{4,5},{5,6},{6,7},{7,0},{8,9},{9,10},{10,1... | collective-permute-start | bytes 614408 | tf_op jit(solution)/shard_map/ppermute | solution.py:506
  54.2 6.7 %collective-permute-start.5 = (f32[80,128]{1,0:T(8,128)S(1)}, f32[80,128]{1,0:T(8,128)S(1)}, u32[]{:S(2)}, u32[]{:S(2)}) collective-permute-start(f32[80,128]{1,0:T(8,128)S(1)} %get-tuple-element.36), channel_id=1, source_target_pairs={{0,7},{1,0},{2,1},{3,2},{4,3},{5,4},{6,5},{7,6},{8,15},{9,8},{10,9... | collective-permute-start | bytes 122888 | tf_op jit(solution)/shard_map/ppermute | solution.py:506
  54.2 6.7 %collective-permute-start.4 = (f32[80,128]{1,0:T(8,128)S(1)}, f32[80,128]{1,0:T(8,128)S(1)}, u32[]{:S(2)}, u32[]{:S(2)}) collective-permute-start(f32[80,128]{1,0:T(8,128)S(1)} %get-tuple-element.36), channel_id=1, source_target_pairs={{0,1},{1,2},{2,3},{3,4},{4,5},{5,6},{6,7},{7,0},{8,9},{9,10},{10,1... | collective-permute-start | bytes 122888 | tf_op jit(solution)/shard_map/ppermute | solution.py:506
  62.6 7.0 %collective-permute-start.6 = (f32[12,8,128]{2,1,0:T(8,128)S(1)}, f32[12,8,128]{2,1,0:T(8,128)S(1)}, u32[]{:S(2)}, u32[]{:S(2)}) collective-permute-start(f32[12,8,128]{2,1,0:T(8,128)S(1)} %get-tuple-element.49), channel_id=1, source_target_pairs={{0,8},{8,16},{16,24},{24,32},{32,40},{40,48},{48,56},{56,64},{64,7... | collective-permute-start | bytes 147464 | tf_op jit(solution)/shard_map/ppermute | solution.py:506
  63.7 5.9 %collective-permute-start.7 = (f32[12,8,128]{2,1,0:T(8,128)S(1)}, f32[12,8,128]{2,1,0:T(8,128)S(1)}, u32[]{:S(2)}, u32[]{:S(2)}) collective-permute-start(f32[12,8,128]{2,1,0:T(8,128)S(1)} %get-tuple-element.50), channel_id=1, source_target_pairs={{0,248},{8,0},{16,8},{24,16},{32,24},{40,32},{48,40},{56,48},{64,5... | collective-permute-start | bytes 147464 | tf_op jit(solution)/shard_map/ppermute | solution.py:506
  69.6 4.8 %collective-permute-start.9 = (f32[40,8,128]{2,1,0:T(8,128)S(1)}, f32[40,8,128]{2,1,0:T(8,128)S(1)}, u32[]{:S(2)}, u32[]{:S(2)}) collective-permute-start(f32[40,8,128]{2,1,0:T(8,128)S(1)} %pad_maximum_fusion.refs_5_), channel_id=1, source_target_pairs={{0,7},{1,0},{2,1},{3,2},{4,3},{5,4},{6,5},{7,6},{8,15},{9,8},{10,9... | collective-permute-start | bytes 491528 | tf_op jit(solution)/shard_map/ppermute | solution.py:506
  70.2 4.2 %collective-permute-start.8 = (f32[40,8,128]{2,1,0:T(8,128)S(1)}, f32[40,8,128]{2,1,0:T(8,128)S(1)}, u32[]{:S(2)}, u32[]{:S(2)}) collective-permute-start(f32[40,8,128]{2,1,0:T(8,128)S(1)} %pad_maximum_fusion.refs_5_), channel_id=1, source_target_pairs={{0,1},{1,2},{2,3},{3,4},{4,5},{5,6},{6,7},{7,0},{8,9},{9,10},{10,1... | collective-permute-start | bytes 491528 | tf_op jit(solution)/shard_map/ppermute | solution.py:506
  101.9 5.9 %collective-permute-start.11 = (f32[80,128]{1,0:T(8,128)S(1)}, f32[80,128]{1,0:T(8,128)S(1)}, u32[]{:S(2)}, u32[]{:S(2)}) collective-permute-start(f32[80,128]{1,0:T(8,128)S(1)} %get-tuple-element.45), channel_id=1, source_target_pairs={{0,7},{1,0},{2,1},{3,2},{4,3},{5,4},{6,5},{7,6},{8,15},{9,8},{10,9... | collective-permute-start | bytes 122888 | tf_op jit(solution)/shard_map/ppermute | solution.py:506
  101.9 5.9 %collective-permute-start.10 = (f32[80,128]{1,0:T(8,128)S(1)}, f32[80,128]{1,0:T(8,128)S(1)}, u32[]{:S(2)}, u32[]{:S(2)}) collective-permute-start(f32[80,128]{1,0:T(8,128)S(1)} %get-tuple-element.45), channel_id=1, source_target_pairs={{0,1},{1,2},{2,3},{3,4},{4,5},{5,6},{6,7},{7,0},{8,9},{9,10},{10,1... | collective-permute-start | bytes 122888 | tf_op jit(solution)/shard_map/ppermute | solution.py:506

commit v2 on v1

v2 whole, which is shorter than its diff:
```python
import jax
import jax.numpy as jnp
from jax import lax
from jax.experimental import pallas as pl
from jax.experimental.pallas import tpu as pltpu
from jax.sharding import PartitionSpec as P

HALO = 12
WZ = 40
BLOCKS = 10
WY = 24
NEAR = 9
SPAN = 20
VMEM_BYTES = 48 * 1024 * 1024


def harmonic(near_k, far_k):
    return 2.0 * near_k * far_k / (near_k + far_k)


def dot(left, right):
    return jnp.dot(left, right, precision=lax.Precision.HIGHEST, preferred_element_type=jnp.float32)


def iota(rows, dim, lanes=128):
    return lax.broadcasted_iota(jnp.int32, (rows, lanes), dim)


def matrix(condition, value):
    return jnp.where(condition, jnp.float32(value), jnp.float32(0.0))


def lane_map(make):
    return make(iota(128, 0), iota(128, 1))


class Level:
    def __init__(self, planes, ny, nx, zl, pad, y_start, y_total, chunk):
        self.planes, self.ny, self.nx, self.zl, self.pad = planes, ny, nx, zl, pad
        self.y_start, self.y_total = y_start, y_total
        self.rows = planes * ny
        self.chunk = min(chunk, self.rows)

    def chunks(self, start=0, count=None):
        count = self.rows if count is None else count
        at = start
        while at < start + count:
            size = min(self.chunk, start + count - at)
            yield at, size
            at += size

    def neighbours(self, ref, at, size):
        base = self.pad + at
        here = ref[base : base + size]
        below = ref[base - self.ny : base - self.ny + size]
        above = ref[base + self.ny : base + self.ny + size]
        if self.zl > 1:
            cell = iota(size, 1) % (self.zl * self.nx)
            below = pltpu.roll(jnp.where(cell >= (self.zl - 1) * self.nx, below, here), self.nx, 1)
            above = pltpu.roll(jnp.where(cell < self.nx, above, here), 128 - self.nx, 1)
        return (
            here,
            (
                below,
                above,
                ref[base - 1 : base - 1 + size],
                ref[base + 1 : base + 1 + size],
                pltpu.roll(here, 1, 1),
            ),
        )

    def close(self, ref, value):
        edge = jnp.full((self.pad, 128), value, jnp.float32)
        ref[0 : self.pad] = edge
        ref[self.pad + self.rows : 2 * self.pad + self.rows] = edge

    def shape(self):
        return (self.rows + 2 * self.pad, 128)

    def build(self, kappa, faces):
        for number in (0, 2):
            self.close(faces.at[number], 0.0)
        for at, size in self.chunks():
            here, around = self.neighbours(kappa, at, size)
            y = iota(size, 0) % self.ny + self.y_start
            x = iota(size, 1) % self.nx
            rows = slice(self.pad + at, self.pad + at + size)
            faces[0, rows] = harmonic(here, around[0])
            faces[2, rows] = jnp.where((y != 0) & (y != self.y_total), harmonic(here, around[2]), 0.0)
            faces[3, rows] = jnp.where(x != 0, harmonic(here, around[4]), 0.0)
        for at, size in self.chunks():
            rows = slice(self.pad + at, self.pad + at + size)
            z_low, around = self.neighbours(faces.at[0], at, size)
            z_high = around[1]
            y_high = faces[2, self.pad + at + 1 : self.pad + at + 1 + size]
            x_low = faces[3, rows]
            total = 1.0 + z_low + z_high + faces[2, rows] + y_high + x_low + pltpu.roll(x_low, 127, 1)
            faces[1, rows] = z_high
            faces[4, rows] = 0.8 / total
            faces[5, rows] = total

    def coupled(self, field, source, faces, at, size):
        here, around = self.neighbours(field, at, size)
        rows = slice(self.pad + at, self.pad + at + size)
        next_rows = slice(self.pad + at + 1, self.pad + at + 1 + size)
        x_low = faces[3, rows]
        total = (
            source[at : at + size]
            + faces[0, rows] * around[0]
            + faces[1, rows] * around[1]
            + faces[2, rows] * around[2]
            + faces[2, next_rows] * around[3]
            + x_low * around[4]
            + pltpu.roll(x_low * here, 127, 1)
        )
        return here, total

    def start(self, field, source, faces):
        for at, size in self.chunks():
            rows = slice(self.pad + at, self.pad + at + size)
            field[rows] = faces[4, rows] * source[at : at + size]

    def relax(self, field, target, source, faces, start=0, count=None):
        for at, size in self.chunks(start, count):
            here, total = self.coupled(field, source, faces, at, size)
            rows = slice(self.pad + at, self.pad + at + size)
            target[rows] = 0.2 * here + faces[4, rows] * total

    def defect(self, field, source, faces, out, start=0, count=None):
        for at, size in self.chunks(start, count):
            here, total = self.coupled(field, source, faces, at, size)
            diagonal = faces[5, self.pad + at : self.pad + at + size]
            out[at - start : at - start + size] = total - diagonal * here

    def pairs(self, ref):
        half = self.rows // 2
        return ref[pl.ds(0, half, stride=2), :] + ref[pl.ds(1, half, stride=2), :]


def parities(index):
    return index[0] % 2 == 0, index[1] % 2 == 0


def kappa_body(index, class_hbm, diff_hbm, phases_hbm, grains_hbm, conc_hbm, kappa_ref, mate_ref, other_ref, classes, diff, phases, grains, sems):
    even, _ = parities(index)
    num_phases, num_classes = diff.shape
    pairs = [(class_hbm, classes), (diff_hbm, diff)]
    for block in range(4):
        pairs += [(phases_hbm.at[4 * block], phases.at[block]), (grains_hbm.at[4 * block], grains.at[block])]
    top = 16 - HALO
    pairs += [
        (conc_hbm.at[pl.ds(jnp.where(even, top, 0), HALO)], mate_ref.at[0:HALO]),
        (conc_hbm.at[pl.ds(jnp.where(even, 0, top), HALO)], other_ref.at[0:HALO]),
    ]
    copies = [pltpu.make_async_copy(source, target, sems.at[i]) for i, (source, target) in enumerate(pairs)]
    for copy in copies:
        copy.start()
    for copy in copies[:-2]:
        copy.wait()
    grain = grains[...]
    phase = phases[...]
    cls = jnp.zeros(grain.shape, jnp.int32)
    for number in range(classes.shape[0]):
        cls = jnp.where(grain == number, classes[number], cls)
    value = jnp.ones(grain.shape, jnp.float32)
    for p in range(num_phases):
        for c in range(num_classes):
            value = jnp.where((phase == p) & (cls == c), diff[p, c], value)
    kappa_ref[...] = value
    mate_ref[HALO:] = jnp.where(even, value[1:], value[:3])
    other_ref[HALO:] = jnp.where(even, value[:3], value[1:])
    for copy in copies[-2:]:
        copy.wait()


def window(refs, plane, even):
    mate, own, other = (ref[plane] for ref in refs)
    return jnp.concatenate([jnp.where(even, other, mate), own, jnp.where(even, mate, other)], axis=0)


def build_fine(sources, even, y_device, kappa, coefs, z_faces):
    kappa[0:8] = jnp.ones((8, 128), jnp.float32)
    kappa[8 + BLOCKS * WY : 16 + BLOCKS * WY] = jnp.ones((8, 128), jnp.float32)
    for block in range(BLOCKS):
        kappa[8 + block * WY : 8 + (block + 1) * WY] = window(sources, WZ + block, even)
    y = iota(WY, 0) + y_device * 8 - 8
    x = iota(WY, 1)
    for block in range(BLOCKS + 1):
        low, high = max(block - 1, 0), min(block, BLOCKS - 1)
        z_faces[block] = harmonic(
            kappa[8 + low * WY : 8 + (low + 1) * WY], kappa[8 + high * WY : 8 + (high + 1) * WY]
        )
    for block in range(BLOCKS):
        at = 8 + block * WY
        k = kappa[at : at + WY]
        y_low = jnp.where(y == 0, 0.0, harmonic(k, kappa[at - 1 : at - 1 + WY]))
        y_high = jnp.where(y == 63, 0.0, harmonic(k, kappa[at + 1 : at + 1 + WY]))
        x_low = jnp.where(x == 0, 0.0, harmonic(k, pltpu.roll(k, 1, 1)))
        x_high = jnp.where(x == 127, 0.0, harmonic(k, pltpu.roll(k, 127, 1)))
        sides = 1.0 + y_low + y_high + x_low + x_high
        diagonals = (sides + z_faces[block] + k, sides + k + k, sides + k + z_faces[block + 1])
        for number, value in enumerate((k, y_low, y_high, x_low, x_high)):
            coefs[block, number] = value
        for number, value in enumerate(diagonals):
            coefs[block, 5 + number] = 0.8 / value
            coefs[block, 8 + number] = value


def fine_plane(field, source, coefs, z_faces, z, low=0, size=WY):
    block, p = divmod(z, 4)
    rows = slice(low, low + size)
    at = WY + z * WY + low
    here = field[at : at + size]
    k = coefs[block, 0, rows]
    below = z_faces[block, rows] if p == 0 else k
    above = z_faces[block + 1, rows] if p == 3 else k
    total = (
        source[z * WY + low : z * WY + low + size]
        + below * field[at - WY : at - WY + size]
        + above * field[at + WY : at + WY + size]
        + coefs[block, 1, rows] * field[at - 1 : at - 1 + size]
        + coefs[block, 2, rows] * field[at + 1 : at + 1 + size]
        + coefs[block, 3, rows] * pltpu.roll(here, 1, 1)
        + coefs[block, 4, rows] * pltpu.roll(here, 127, 1)
    )
    kind = (0, 1, 1, 2)[p]
    return here, total, coefs[block, 5 + kind, rows], coefs[block, 8 + kind, rows]


def level_one(y_device):
    return Level(20, 16, 64, 1, 16, y_device * 4 - 4, 32, 160)


def build_one(level, kappa, spread, packed, kappa_one, faces):
    for block in range(BLOCKS):
        spread[block * 32 : block * 32 + WY] = kappa[8 + block * WY : 8 + (block + 1) * WY]
        spread[block * 32 + WY : block * 32 + 32] = jnp.ones((32 - WY, 128), jnp.float32)
    pick = lane_map(lambda r, c: matrix(r == 2 * (c % 64), 0.5))
    packed[...] = dot(spread[pl.ds(0, BLOCKS * 16, stride=2), :], pick)
    level.close(kappa_one, 1.0)
    for block in range(BLOCKS):
        value = packed[block * 16 : block * 16 + 16]
        kappa_one[16 + block * 32 : 32 + block * 32] = value
        kappa_one[32 + block * 32 : 48 + block * 32] = value
    level.build(kappa_one, faces)


def to_chunk(rows):
    group = iota(8, 1) // 32
    out = rows[0:8]
    for z in range(1, 4):
        out = jnp.where(group == z, rows[8 * z : 8 * z + 8], out)
    return out


def down_body(first, copies, *refs):
    index, refs = refs[0], refs[1:]
    if first:
        sources, refs = refs[:3], refs[3:]
    else:
        fields, (source, coefs, z_faces, faces), refs = refs[:3], refs[3:7], refs[7:]
    chunk, edge, kept, source_one, kept_one = refs[:5]
    refs = refs[5:]
    if first:
        (source, coefs, z_faces, faces), refs = refs[:4], refs[4:]
    va, vb, rs, oa, tmp = refs[:5]
    _, even = parities(index)
    y_device = index[1]
    level = level_one(y_device)
    if first:
        kappa, spread, packed, kappa_one = refs[5:]
        build_fine(sources, even, y_device, kappa, coefs, z_faces)
        build_one(level, kappa, spread, packed, kappa_one, faces)
    zero = jnp.zeros((WY, 128), jnp.float32)
    for ref in (va, vb):
        ref[0:WY] = zero
        ref[(WZ + 1) * WY : (WZ + 2) * WY] = zero
    if first:
        for z in range(WZ):
            kind = (0, 1, 1, 2)[z % 4]
            value = window(sources, z, even)
            source[z * WY : (z + 1) * WY] = value
            va[(z + 1) * WY : (z + 2) * WY] = coefs[z // 4, 5 + kind] * value
    else:
        for z in range(WZ):
            vb[(z + 1) * WY : (z + 2) * WY] = window(fields, z, even)
        for z in range(WZ):
            here, total, weight, _ = fine_plane(vb, source, coefs, z_faces, z)
            va[(z + 1) * WY : (z + 2) * WY] = 0.2 * here + weight * total
    for z in range(2, WZ - 2):
        here, total, weight, _ = fine_plane(va, source, coefs, z_faces, z)
        value = 0.2 * here + weight * total
        vb[(z + 1) * WY : (z + 2) * WY] = value
        if 10 <= z < 30:
            kept[(z - 10) * WY : (z - 9) * WY] = value
    for plane in range(20):
        if 2 <= plane < 18:
            total_defect = 0.0
            for z in (2 * plane, 2 * plane + 1):
                here, total, _, diagonal = fine_plane(vb, source, coefs, z_faces, z)
                total_defect = total_defect + (total - diagonal * here)
            rs[plane * 32 : plane * 32 + WY] = total_defect
            rs[plane * 32 + WY : plane * 32 + 32] = jnp.zeros((32 - WY, 128), jnp.float32)
        else:
            rs[plane * 32 : plane * 32 + 32] = jnp.zeros((32, 128), jnp.float32)
    mean_x = lane_map(lambda r, c: matrix(r // 2 == c % 64, 0.125))
    source_one[...] = dot(rs[pl.ds(0, 320, stride=2), :] + rs[pl.ds(1, 320, stride=2), :], mean_x)
    for ref in (oa, kept_one):
        level.close(ref, 0.0)
    level.start(oa, source_one, faces)
    level.relax(oa, kept_one, source_one, faces)
    level.defect(kept_one, source_one, faces, tmp, 6 * 16, 8 * 16)
    for z in range(4):
        tmp[z * 16 : z * 16 + 16] = tmp[z * 32 : z * 32 + 16] + tmp[z * 32 + 16 : z * 32 + 32]
    halves = tmp[pl.ds(0, 32, stride=2), :] + tmp[pl.ds(1, 32, stride=2), :]
    mean_two = lane_map(lambda r, c: matrix((r < 64) & (r // 2 == c % 32), 0.125))
    values = [to_chunk(dot(halves, mean_two))[2:4]]
    if first:
        pick_two = lane_map(lambda r, c: matrix((r < 64) & (r == 2 * (c % 32)), 0.5))
        values.append(to_chunk(dot(packed[pl.ds(48, 32, stride=2), :], pick_two))[2:4])
    repeats = 4 // len(values)
    tile = jnp.concatenate(values * repeats, axis=0)
    for at in range(0, copies // repeats):
        chunk[at * 8 : at * 8 + 8] = tile
    for plane in range(20):
        edge[plane * 4 : plane * 4 + 4] = kept_one[16 + plane * 16 + 4 : 16 + plane * 16 + 8]


def coarse_levels():
    return (
        Level(SPAN, 16, 32, 4, 16, 0, 16, 160),
        Level(SPAN, 8, 16, 2, 8, 0, 8, 160),
        Level(SPAN, 4, 8, 1, 8, 0, 4, 128),
    )


def coarse_body(first, z_devices, *refs):
    two, three, four = coarse_levels()
    index, same, mate = refs[:3]
    refs = refs[3:]
    if first:
        near, f2, f3, f4 = refs[:4]
    else:
        f2, f3, f4, near = refs[:4]
    a2, b2, g2, r2, a3, b3, g3, r3, a4, b4, g4, cut_same, cut_mate = refs[4:17]
    z_device = index[0]
    even = index[1] % 2 == 0
    per = 4 if first else 2
    rows = 4 * per
    for number in range(SPAN):
        at = lax.rem(z_device + (number - NEAR + 4 * z_devices), z_devices) * rows
        at = pl.multiple_of(at, 8)
        cut_same[number * rows : (number + 1) * rows] = same[pl.ds(at, rows), :]
        cut_mate[number * rows : (number + 1) * rows] = mate[pl.ds(at, rows), :]

    def interleave(target, start, part):
        for y in range(2):
            take = pl.ds(part + y, 4 * SPAN, stride=per)
            one, two_ = cut_same[take, :], cut_mate[take, :]
            target[pl.ds(start + y, 4 * SPAN, stride=4), :] = jnp.where(even, one, two_)
            target[pl.ds(start + 2 + y, 4 * SPAN, stride=4), :] = jnp.where(even, two_, one)

    interleave(g2, 0, 0)
    mean_three = lane_map(lambda r, c: matrix(c % 32 == (r // 64) * 16 + (r % 32) // 2, 0.125))
    mean_four = lane_map(lambda r, c: matrix((r < 32) & (c % 8 == (r % 16) // 2), 0.125))
    if first:
        k2, k3, k4 = refs[17:]
        interleave(k2, two.pad, 2)
        two.close(k2, 1.0)
        two.build(k2, f2)
        r2[...] = k2[two.pad : two.pad + two.rows]
        k3[three.pad : three.pad + three.rows] = 0.5 * dot(two.pairs(r2), mean_three)
        three.close(k3, 1.0)
        three.build(k3, f3)
        r3[...] = k3[three.pad : three.pad + three.rows]
        k4[four.pad : four.pad + four.rows] = 0.5 * dot(three.pairs(r3), mean_four)
        four.close(k4, 1.0)
        four.build(k4, f4)
    for level, fields in ((two, (a2, b2)), (three, (a3, b3)), (four, (a4, b4))):
        for field in fields:
            level.close(field, 0.0)

    two.start(a2, g2, f2)
    two.relax(a2, b2, g2, f2)
    two.defect(b2, g2, f2, r2)
    g3[...] = dot(two.pairs(r2), mean_three)
    three.start(a3, g3, f3)
    three.relax(a3, b3, g3, f3)
    three.defect(b3, g3, f3, r3)
    g4[...] = dot(three.pairs(r3), mean_four)
    four.start(a4, g4, f4)
    for _ in range(2):
        four.relax(a4, b4, g4, f4)
        four.relax(b4, a4, g4, f4)
    four.relax(a4, b4, g4, f4)

    def correct(level, field, start, count, coarse, tmp, spread_lanes):
        value = dot(coarse, spread_lanes)
        tmp[pl.ds(0, count // 2, stride=2), :] = value
        tmp[pl.ds(1, count // 2, stride=2), :] = value
        inner = slice(level.pad + start, level.pad + start + count)
        field[inner] = field[inner] + tmp[0:count]

    from_four = lane_map(lambda r, c: matrix((r < 8) & (r == (c % 16) // 2), 1.0))
    from_three = lane_map(lambda r, c: matrix((r < 32) & (r == (c // 64) * 16 + (c % 32) // 2), 1.0))
    low = NEAR - 3
    correct(three, b3, 8 * low, 48, b4[four.pad + 4 * low : four.pad + 4 * low + 24], r3, from_four)
    three.relax(b3, a3, g3, f3, 8 * low, 48)
    low = NEAR - 1
    three.relax(a3, b3, g3, f3, 8 * low, 24)
    correct(two, b2, 16 * low, 48, b3[three.pad + 8 * low : three.pad + 8 * low + 24], r2, from_three)
    two.relax(b2, a2, g2, f2, 16 * low, 48)
    two.relax(a2, b2, g2, f2, 16 * low, 48)
    near[...] = b2[two.pad + 16 * low : two.pad + 16 * low + 48]


def up_body(last, *refs):
    index, source, coefs, z_faces, faces, near, edge_mate, edge_other, kept, source_one, kept_one, out = refs[:12]
    refs = refs[12:]
    if not last:
        (mate, other), refs = refs[:2], refs[2:]
    va, vb, spread, oa, ob = refs
    even_z, even = parities(index)
    y_device = index[1]
    level = level_one(y_device)
    rows = matrix(iota(16, 1, 16) == y_device * 2 - 2 + iota(16, 0, 16) // 2, 1.0)
    spread_y = jnp.concatenate([dot(rows, near[16 * part : 16 * part + 16]) for part in range(3)], axis=0)
    by_z = [
        dot(spread_y, lane_map(lambda r, c, z=z: matrix(r == z * 32 + (c % 64) // 2, 1.0))) for z in range(4)
    ]
    for plane in range(20):
        part, z = divmod(plane // 2 + 1, 4)
        at = 16 + plane * 16
        one, two = edge_mate[plane * 4 : plane * 4 + 4], edge_other[plane * 4 : plane * 4 + 4]
        field = jnp.concatenate(
            [jnp.where(even, two, one), kept_one[at + 4 : at + 8], jnp.where(even, one, two),
             jnp.zeros((4, 128), jnp.float32)], axis=0
        )
        oa[at : at + 16] = field + by_z[z][16 * part : 16 * part + 16]
    level.relax(oa, ob, source_one, faces, 4 * 16, 12 * 16)
    level.relax(ob, oa, source_one, faces, 5 * 16, 10 * 16)
    from_one = lane_map(lambda r, c: matrix((r < 64) & (r == c // 2), 1.0))
    value = dot(oa[16 + 80 : 16 + 240], from_one)
    spread[pl.ds(0, 160, stride=2), :] = value
    spread[pl.ds(1, 160, stride=2), :] = value
    for z in range(10, 30):
        at = ((z - 10) // 2) * 32
        va[(z + 1) * WY : (z + 2) * WY] = kept[(z - 10) * WY : (z - 9) * WY] + spread[at : at + WY]
    for z in range(11, 29):
        here, total, weight, _ = fine_plane(va, source, coefs, z_faces, z)
        vb[(z + 1) * WY : (z + 2) * WY] = 0.2 * here + weight * total
    for z in range(12, 28):
        here, total, weight, _ = fine_plane(vb, source, coefs, z_faces, z, 8, 8)
        out[z - 12] = 0.2 * here + weight * total
    if not last:
        top = 16 - HALO
        mate[...] = out[pl.ds(jnp.where(even_z, top, 0), HALO)]
        other[...] = out[pl.ds(jnp.where(even_z, 0, top), HALO)]


def floats(*shape):
    return jax.ShapeDtypeStruct(shape, jnp.float32)


def call(body, outs, scratch, args, inputs=pltpu.VMEM):
    vmem = pl.BlockSpec(memory_space=pltpu.VMEM)
    return pl.pallas_call(
        body,
        out_shape=outs,
        in_specs=[pl.BlockSpec(memory_space=pltpu.SMEM)] + [pl.BlockSpec(memory_space=inputs)] * (len(args) - 1),
        out_specs=[vmem] * len(outs),
        scratch_shapes=[pltpu.VMEM(s, jnp.float32) if isinstance(s, tuple) else s for s in scratch],
        compiler_params=pltpu.CompilerParams(vmem_limit_bytes=VMEM_BYTES),
    )(*args)


FIELD = ((WZ + 2) * WY, 128)
SHARED = [(WZ * WY, 128), (BLOCKS, 11, WY, 128), (BLOCKS + 1, WY, 128), (6, 352, 128)]
Z_AXIS = ("gz",)
Y_AXIS = ("gx", "core")


def down(index, arrays, shared):
    first = shared is None
    copies = lax.axis_size("gz") * lax.axis_size("gx")
    outs = [
        floats(copies * (4 if first else 2), 128),
        floats(80, 128),
        floats(20 * WY, 128),
        floats(320, 128),
        floats(352, 128),
    ]
    scratch = [FIELD, FIELD, (640, 128), (352, 128), (128, 128)]
    if first:
        outs += [floats(*shape) for shape in SHARED]
        scratch += [(16 + BLOCKS * WY, 128), (320, 128), (160, 128), (352, 128)]
        args = [index, *arrays]
    else:
        args = [index, *arrays, *shared]
    result = call(lambda *refs: down_body(first, copies, *refs), outs, scratch, args)
    return result[0], result[1], result[2:5], result[5:] if first else shared


def coarse(index, gathered, faces):
    first = faces is None
    z_devices = lax.axis_size("gz")
    levels = coarse_levels()
    outs, scratch = [floats(48, 128)], []
    if first:
        outs += [floats(6, *level.shape()) for level in levels]
    for level in levels:
        scratch += [level.shape(), level.shape(), (level.rows, 128), (level.rows, 128)]
    cut = (SPAN * (16 if first else 8), 128)
    scratch = scratch[:11] + [cut, cut]
    if first:
        scratch += [level.shape() for level in levels]
    args = [index, *gathered] + ([] if first else list(faces))
    near, *new = call(lambda *refs: coarse_body(first, z_devices, *refs), outs, scratch, args)
    return near, new if first else faces


def up(index, shared, near, edges, kept, last):
    outs = [floats(16, 8, 128)] + ([] if last else [floats(HALO, 8, 128)] * 2)
    scratch = [FIELD, FIELD, (320, 128), (352, 128), (352, 128)]
    return call(
        lambda *refs: up_body(last, *refs), outs, scratch, [index, *shared, near, *edges, *kept]
    )


def mate_of(i):
    return i + 1 if i % 2 == 0 else i - 1


def other_of(i):
    return i - 1 if i % 2 == 0 else i + 1


def swap(array, axis, partner):
    count = 1
    for name in axis:
        count *= lax.axis_size(name)
    return lax.ppermute(array, axis, [(i, partner(i) % count) for i in range(count)])


def swaps(mate, other, axis):
    far = swap(other, axis, other_of)
    return swap(mate, axis, mate_of), far


def to_all(copies):
    peers = lax.axis_size("gz") * lax.axis_size("gx")
    copies = copies.reshape(peers, copies.shape[0] // peers, 128)
    out = lax.all_to_all(copies, ("gz", "gx"), 0, 0)
    out = out.reshape(out.shape[0] * out.shape[1], 128)
    return out, swap(out, Y_AXIS, mate_of)


def stack(index, parts, own):
    even = index[0] % 2 == 0
    mate, other = parts
    before, after = jnp.where(even, other, mate), jnp.where(even, mate, other)
    pieces = [before[:HALO], own[0], after[:HALO]]
    if len(own) > 1:
        pieces += [before[HALO:], own[1], after[HALO:]]
    return jnp.concatenate(pieces, axis=0)


def cycle(index, arrays, shared, coarse_faces, last):
    copies, edge, kept, shared = down(index, arrays, shared)
    edges = swaps(edge, edge, Y_AXIS)
    gathered = to_all(copies)
    near, coarse_faces = coarse(index, gathered, coarse_faces)
    return up(index, shared, near, edges, kept, last), shared, coarse_faces


def per_device(concentration, phases, grains, grain_class, diffusivity):
    y_device = lax.axis_index("gx") * lax.axis_size("core") + lax.axis_index("core")
    index = jnp.stack([lax.axis_index("gz"), y_device]).astype(jnp.int32)
    plane = (4,) + phases.shape[1:]
    part = floats(HALO + 3, 8, 128)
    kappa, *parts = call(
        kappa_body,
        [floats(*plane), part, part],
        [
            pltpu.SMEM(grain_class.shape, jnp.int32),
            pltpu.SMEM(diffusivity.shape, jnp.float32),
            pltpu.VMEM(plane, jnp.int32),
            pltpu.VMEM(plane, jnp.int32),
            pltpu.SemaphoreType.DMA((12,)),
        ],
        [index] + [
            pltpu.with_memory_space_constraint(array, pltpu.HBM)
            for array in (grain_class, diffusivity, phases, grains, concentration)
        ],
        pltpu.HBM,
    )
    own = stack(index, swaps(*parts, Z_AXIS), (concentration, kappa))
    mate, other = swaps(own, own, Y_AXIS)
    (field, *parts), shared, faces = cycle(index, (mate, own, other), None, None, False)

    own = stack(index, swaps(*parts, Z_AXIS), (field,))
    mate, other = swaps(own, own, Y_AXIS)
    return cycle(index, (mate, own, other), shared, faces, True)[0][0]


def solution(mesh):
    z_devices, y_devices = mesh.shape["gz"], mesh.shape["gy"]
    cores = jax.sharding.Mesh(mesh.devices.reshape(z_devices, y_devices // 2, 2), ("gz", "gx", "core"))
    split = P("gz", ("gx", "core"), None)
    return jax.shard_map(
        per_device, mesh=cores, in_specs=(split, split, split, P(), P()), out_specs=split, check_vma=False
    )
```

time: 110 us -> 94 us (0.85)
  blocking collectives: 56.1 us -> 39.4 us
  waiting for transfers between devices: 10 us -> 15 us
  local copies, waits for them, and re-layouts: 3.89 us -> 0.87 us
  Pallas kernels: 18 us -> 15.7 us
    all_to_all x2, blocking collectives: 56.1 us -> 39.4 us  [to_all(): out = lax.all_to_all(copies, ('gz', 'gx'), 0, 0)]
    ppermute x12 -> x14, waiting for transfers between devices: 10 us -> 15 us  [swap(): lax.ppermute(array, axis, [(i, partner(i) % count) for i in range(count)])]
    unnamed x15 -> x5, local copies, waits for them, and re-layouts: 3.88 us -> 0.86 us
    pallas_call x7, Pallas kernels: 18 us -> 15.7 us  [call(): pl.pallas_call(body, out_shape=outs, in_specs=[pl.BlockSpec(memory_space=...]
    ppermute x12 -> x14, starting transfers between devices: 21.8 us -> 22.6 us  [swap(): lax.ppermute(array, axis, [(i, partner(i) % count) for i in range(count)])]
  transfers between devices with their start and end apart: 12 -> 14, of which waited for: 4 -> 6; matrix products, arithmetic and copies ran while one was open for 0% -> 0% of each run, Pallas kernels for 8% -> 6%
where the time goes in v2:
time: 94 us; the launch traced here: 93.8 us
  blocking collectives  39.4 us (42%)
  starting transfers between devices  22.6 us (24%)
  Pallas kernels  15.7 us (17%)
  waiting for transfers between devices  15 us (16%)
    all_to_all x2, blocking collectives, to_all(): out = lax.all_to_all(copies, ('gz', 'gx'), 0, 0)  39.4 us
    ppermute x14, starting transfers between devices, swap(): lax.ppermute(array, axis, [(i, partner(i) % count) for i in range(count)])  22.6 us
    pallas_call x7, Pallas kernels, call(): pl.pallas_call(body, out_shape=outs, in_specs=[pl.BlockSpec(memory_space=...  15.7 us
    ppermute x14, waiting for transfers between devices, swap(): lax.ppermute(array, axis, [(i, partner(i) % count) for i in range(count)])  15 us
  transfers between devices with their start and end apart: 14, of which 6 were waited for; matrix products, arithmetic and copies ran while one was open for 0% of the time, Pallas kernels for 6%

profile of v2, /device:TPU:1, one launch (start us, length us, event | category | flops | bytes accessed | tf_op | source)
XLA Modules:
  0.0 93.8 jit_solution(4357551360022989800)
XLA Ops:
  0.1 1.6 %shard_map.55 = (f32[4,8,128]{2,1,0:T(8,128)S(1)}, f32[15,8,128]{2,1,0:T(8,128)S(1)}, f32[15,8,128]{2,1,0:T(8,128)S(1)}) custom-call(s32[2]{0:T(128)S(1)} %pad_add_fusion.index.refs_0_, s32[64]{0:T(128)} %class_hbm.1, f32[3,4]{1,0:T(4,128)} %diff_hbm.1, s32[16,8,128]{2,1,0:T(8,128)} %phases_hbm.1, s32[16,8,128]{2,1,0:T(8,128)} %grains_hbm.1, ...), custom_call_target="tpu_custom_call" | custom-call | tf_op jit(solution)/shard_map/pallas_call | solution.py:467
  1.7 8.9 %collective-permute-start = (f32[15,8,128]{2,1,0:T(8,128)S(1)}, f32[15,8,128]{2,1,0:T(8,128)S(1)}, u32[]{:S(2)}, u32[]{:S(2)}) collective-permute-start(f32[15,8,128]{2,1,0:T(8,128)S(1)} %get-tuple-element.29), channel_id=1, source_target_pairs={{0,248},{8,16},{16,8},{24,32},{32,24},{40,48},{48,40},{56,64},{64,... | collective-permute-start | bytes 184328 | tf_op jit(solution)/shard_map/ppermute | solution.py:542
  10.6 1.6 %collective-permute-done = f32[15,8,128]{2,1,0:T(8,128)S(1)} collective-permute-done((f32[15,8,128]{2,1,0:T(8,128)S(1)}, f32[15,8,128]{2,1,0:T(8,128)S(1)}, u32[]{:S(2)}, u32[]{:S(2)}) %collective-permute-start) | collective-permute-done | bytes 61472 | tf_op jit(solution)/shard_map/ppermute | solution.py:542
  12.2 1.5 %collective-permute-done.1 = f32[15,8,128]{2,1,0:T(8,128)S(1)} collective-permute-done((f32[15,8,128]{2,1,0:T(8,128)S(1)}, f32[15,8,128]{2,1,0:T(8,128)S(1)}, u32[]{:S(2)}, u32[]{:S(2)}) %collective-permute-start.1) | collective-permute-done | bytes 61472 | tf_op jit(solution)/shard_map/ppermute | solution.py:542
  13.7 0.8 constant_dynamic-update-slice_fusion.3
  14.6 3.3 %collective-permute-start.3 = (f32[50,8,128]{2,1,0:T(8,128)S(1)}, f32[50,8,128]{2,1,0:T(8,128)S(1)}, u32[]{:S(2)}, u32[]{:S(2)}) collective-permute-start(f32[50,8,128]{2,1,0:T(8,128)S(1)} %constant_dynamic-update-slice_fusion.refs_2_), channel_id=1, source_target_pairs={{0,7},{1,2},{2,1},{3,4},{4,3},{5,6},{6,5},{7,0},{8,15},{9,10},{10,... | collective-permute-start | bytes 614408 | tf_op jit(solution)/shard_map/ppermute | solution.py:542
  17.9 3.7 %collective-permute-done.3.refs_3_ = f32[50,8,128]{2,1,0:T(8,128)S(1)} collective-permute-done((f32[50,8,128]{2,1,0:T(8,128)S(1)}, f32[50,8,128]{2,1,0:T(8,128)S(1)}, u32[]{:S(2)}, u32[]{:S(2)}) %collective-permute-start.3) | collective-permute-done | bytes 204832 | tf_op jit(solution)/shard_map/ppermute | solution.py:542
  21.6 2.2 %shard_map.56 = (f32[512,128]{1,0:T(8,128)S(1)}, f32[80,128]{1,0:T(8,128)S(1)}, f32[480,128]{1,0:T(8,128)S(1)}, f32[320,128]{1,0:T(8,128)S(1)}, f32[352,128]{1,0...) custom-call(s32[2]{0:T(128)S(1)} %pad_add_fusion.index.refs_0_, ...), custom_call_target="tpu_custom_call" | custom-call | tf_op jit(solution)/shard_map/pallas_call | solution.py:467
  23.8 21.1 %all_to_all.10 = f32[128,4,128]{2,1,0:T(4,128)S(1)} all-to-all(f32[128,4,128]{2,1,0:T(4,128)S(1)} %bitcast.10), channel_id=1, replica_groups=mesh['gz'=32,'gx'=4,'core'=2] {'gz','gx'}, dimensions={0} | all-to-all | bytes 524288 | tf_op jit(solution)/shard_map/all_to_all | solution.py:553
  44.9 3.0 %collective-permute-start.4 = (f32[512,128]{1,0:T(8,128)S(1)}, f32[512,128]{1,0:T(8,128)S(1)}, u32[]{:S(2)}, u32[]{:S(2)}) collective-permute-start(f32[512,128]{1,0:T(8,128)S(1)} %bitcast.6), channel_id=1, source_target_pairs={{0,1},{1,0},{2,3},{3,2},{4,5},{5,4},{6,7},{7,6},{8,9},{9,8},{10,11... | collective-permute-start | bytes 786440 | tf_op jit(solution)/shard_map/ppermute | solution.py:542
  47.9 0.8 collective-permute-start.5
  49.0 3.1 %shard_map.57 = (f32[48,128]{1,0:T(8,128)S(1)}, f32[6,352,128]{2,1,0:T(8,128)S(1)}, f32[6,176,128]{2,1,0:T(8,128)S(1)}, f32[6,96,128]{2,1,0:T(8,128)S(1)}) custom-call(s32[2]{0:T(128)S(1)} %pad_add_fusion.index.refs_0_, f32[512,128]{1,0:T(8,128)S(1)} %bitcast.7, f32[512,128]{1,0:T(8,128)S(1)} %collective-permute-done.4.refs_2_), custom_call_target="tpu_custom_call" | custom-call | tf_op jit(solution)/shard_map/pallas_call | solution.py:467
  52.1 1.7 %shard_map.58 = (f32[16,8,128]{2,1,0:T(8,128)S(1)}, f32[12,8,128]{2,1,0:T(8,128)S(1)}, f32[12,8,128]{2,1,0:T(8,128)S(1)}) custom-call(s32[2]{0:T(128)S(1)} %pad_add_fusion.index.refs_0_, f32[960,128]{1,0:T(8,128)S(1)} %get-tuple-element.32.refs_1_.refs_4_, f32[10,11,24,128]{3,2,1,0:T(8,128)S(1)} %get-tuple-element.33.refs_2_.refs_5_, ...), custom_call_target="tpu_custom_call" | custom-call | tf_op jit(solution)/shard_map/pallas_call | solution.py:467
  53.8 1.1 %collective-permute-start.7 = (f32[12,8,128]{2,1,0:T(8,128)S(1)}, f32[12,8,128]{2,1,0:T(8,128)S(1)}, u32[]{:S(2)}, u32[]{:S(2)}) collective-permute-start(f32[12,8,128]{2,1,0:T(8,128)S(1)} %get-tuple-element.42), channel_id=1, source_target_pairs={{0,248},{8,16},{16,8},{24,32},{32,24},{40,48},{48,40},{56,64},{64,... | collective-permute-start | bytes 147464 | tf_op jit(solution)/shard_map/ppermute | solution.py:542
  54.9 0.3 collective-permute-start.8
  55.3 4.9 %collective-permute-done.7 = f32[12,8,128]{2,1,0:T(8,128)S(1)} collective-permute-done((f32[12,8,128]{2,1,0:T(8,128)S(1)}, f32[12,8,128]{2,1,0:T(8,128)S(1)}, u32[]{:S(2)}, u32[]{:S(2)}) %collective-permute-start.7) | collective-permute-done | bytes 49184 | tf_op jit(solution)/shard_map/ppermute | solution.py:542
  60.2 1.9 %collective-permute-start.10 = (f32[40,8,128]{2,1,0:T(8,128)S(1)}, f32[40,8,128]{2,1,0:T(8,128)S(1)}, u32[]{:S(2)}, u32[]{:S(2)}) collective-permute-start(f32[40,8,128]{2,1,0:T(8,128)S(1)} %pad_maximum_fusion.refs_2_), channel_id=1, source_target_pairs={{0,7},{1,2},{2,1},{3,4},{4,3},{5,6},{6,5},{7,0},{8,15},{9,10},{10,... | collective-permute-start | bytes 491528 | tf_op jit(solution)/shard_map/ppermute | solution.py:542
  62.1 3.0 %collective-permute-done.10.refs_3_ = f32[40,8,128]{2,1,0:T(8,128)S(1)} collective-permute-done((f32[40,8,128]{2,1,0:T(8,128)S(1)}, f32[40,8,128]{2,1,0:T(8,128)S(1)}, u32[]{:S(2)}, u32[]{:S(2)}) %collective-permute-start.10) | collective-permute-done | bytes 163872 | tf_op jit(solution)/shard_map/ppermute | solution.py:542
  65.1 2.0 %shard_map.59 = (f32[256,128]{1,0:T(8,128)S(1)}, f32[80,128]{1,0:T(8,128)S(1)}, f32[480,128]{1,0:T(8,128)S(1)}, f32[320,128]{1,0:T(8,128)S(1)}, f32[352,128]{1,0:T(8,128)S(1)}) custom-call(s32[2]{0:T(128)S(1)} %pad_add_fusion.index.refs_0_, f32[40,8,128]{2,1,0:T(8,128)S(1)} %collective-permute-done.9.refs_1_, f32[40,8,128]{2,1,0:T(8,128)S(1)} %pad_maximum_fusion.refs_2_, ...), custom_call_target="tpu_custom_call" | custom-call | tf_op jit(solution)/shard_map/pallas_call | solution.py:467
  67.1 18.3 %all_to_all.11 = f32[128,2,128]{2,1,0:T(2,128)S(1)} all-to-all(f32[128,2,128]{2,1,0:T(2,128)S(1)} %bitcast.11), channel_id=1, replica_groups=mesh['gz'=32,'gx'=4,'core'=2] {'gz','gx'}, dimensions={0} | all-to-all | bytes 262144 | tf_op jit(solution)/shard_map/all_to_all | solution.py:553
  85.5 2.1 %collective-permute-start.11 = (f32[256,128]{1,0:T(8,128)S(1)}, f32[256,128]{1,0:T(8,128)S(1)}, u32[]{:S(2)}, u32[]{:S(2)}) collective-permute-start(f32[256,128]{1,0:T(8,128)S(1)} %bitcast.8), channel_id=1, source_target_pairs={{0,1},{1,0},{2,3},{3,2},{4,5},{5,4},{6,7},{7,6},{8,9},{9,8},{10,11... | collective-permute-start | bytes 393224 | tf_op jit(solution)/shard_map/ppermute | solution.py:542
  87.7 1.0 %collective-permute-start.12 = (f32[80,128]{1,0:T(8,128)S(1)}, f32[80,128]{1,0:T(8,128)S(1)}, u32[]{:S(2)}, u32[]{:S(2)}) collective-permute-start(f32[80,128]{1,0:T(8,128)S(1)} %get-tuple-element.49), channel_id=1, source_target_pairs={{0,1},{1,0},{2,3},{3,2},{4,5},{5,4},{6,7},{7,6},{8,9},{9,8},{10,11... | collective-permute-start | bytes 122888 | tf_op jit(solution)/shard_map/ppermute | solution.py:542
  88.6 2.8 %shard_map.60.refs_5_ = f32[48,128]{1,0:T(8,128)S(1)} custom-call(s32[2]{0:T(128)S(1)} %pad_add_fusion.index.refs_0_, f32[256,128]{1,0:T(8,128)S(1)} %bitcast.9, f32[256,128]{1,0:T(8,128)S(1)} %collective-permute-done.11.refs_2_, f32[6,352,128]{2,1,0:T(8,128)S(1)} %get-tuple-element.46.refs_3_, f32[6,176,128]{2,1,0:T(8,128)S(1)} %get-tuple-element.47.refs_4_, ...), custom_call_target="tpu_custom_call" | custom-call | tf_op jit(solution)/shard_map/pallas_call | solution.py:467
  91.5 2.3 %shard_map.61 = f32[16,8,128]{2,1,0:T(8,128)} custom-call(s32[2]{0:T(128)S(1)} %pad_add_fusion.index.refs_0_, f32[960,128]{1,0:T(8,128)S(1)} %get-tuple-element.32.refs_1_.refs_4_, f32[10,11,24,128]{3,2,1,0:T(8,128)S(1)} %get-tuple-element.33.refs_2_.refs_5_, f32[11,24,128]{2,1,0:T(8,128)S(1)} %get-tuple-element.34.refs_3_.refs_6_, ...), custom_call_target="tpu_custom_call" | custom-call | tf_op jit(solution)/shard_map/pallas_call | solution.py:467
  (23 shorter events, 0.6 us)
Async XLA Ops:
  1.7 10.6 %collective-permute-start = (f32[15,8,128]{2,1,0:T(8,128)S(1)}, f32[15,8,128]{2,1,0:T(8,128)S(1)}, u32[]{:S(2)}, u32[]{:S(2)}) collective-permute-start(f32[15,8,128]{2,1,0:T(8,128)S(1)} %get-tuple-element.29), channel_id=1, source_target_pairs={{0,248},{8,16},{16,8},{24,32},{32,24},{40,48},{48,40},{56,64},{64,... | collective-permute-start | bytes 184328 | tf_op jit(solution)/shard_map/ppermute | solution.py:542
  10.6 3.1 %collective-permute-start.1 = (f32[15,8,128]{2,1,0:T(8,128)S(1)}, f32[15,8,128]{2,1,0:T(8,128)S(1)}, u32[]{:S(2)}, u32[]{:S(2)}) collective-permute-start(f32[15,8,128]{2,1,0:T(8,128)S(1)} %get-tuple-element.30), channel_id=1, source_target_pairs={{0,8},{8,0},{16,24},{24,16},{32,40},{40,32},{48,56},{56,48},{64,72... | collective-permute-start | bytes 184328 | tf_op jit(solution)/shard_map/ppermute | solution.py:542
  14.6 7.0 %collective-permute-start.3 = (f32[50,8,128]{2,1,0:T(8,128)S(1)}, f32[50,8,128]{2,1,0:T(8,128)S(1)}, u32[]{:S(2)}, u32[]{:S(2)}) collective-permute-start(f32[50,8,128]{2,1,0:T(8,128)S(1)} %constant_dynamic-update-slice_fusion.refs_2_), channel_id=1, source_target_pairs={{0,7},{1,2},{2,1},{3,4},{4,3},{5,6},{6,5},{7,0},{8,15},{9,10},{10,... | collective-permute-start | bytes 614408 | tf_op jit(solution)/shard_map/ppermute | solution.py:542
  17.9 3.7 %collective-permute-start.2 = (f32[50,8,128]{2,1,0:T(8,128)S(1)}, f32[50,8,128]{2,1,0:T(8,128)S(1)}, u32[]{:S(2)}, u32[]{:S(2)}) collective-permute-start(f32[50,8,128]{2,1,0:T(8,128)S(1)} %constant_dynamic-update-slice_fusion.refs_2_), channel_id=1, source_target_pairs={{0,1},{1,0},{2,3},{3,2},{4,5},{5,4},{6,7},{7,6},{8,9},{9,8},{10,11... | collective-permute-start | bytes 614408 | tf_op jit(solution)/shard_map/ppermute | solution.py:542
  44.9 4.1 %collective-permute-start.4 = (f32[512,128]{1,0:T(8,128)S(1)}, f32[512,128]{1,0:T(8,128)S(1)}, u32[]{:S(2)}, u32[]{:S(2)}) collective-permute-start(f32[512,128]{1,0:T(8,128)S(1)} %bitcast.6), channel_id=1, source_target_pairs={{0,1},{1,0},{2,3},{3,2},{4,5},{5,4},{6,7},{7,6},{8,9},{9,8},{10,11... | collective-permute-start | bytes 786440 | tf_op jit(solution)/shard_map/ppermute | solution.py:542
  47.8 4.3 %collective-permute-start.6 = (f32[80,128]{1,0:T(8,128)S(1)}, f32[80,128]{1,0:T(8,128)S(1)}, u32[]{:S(2)}, u32[]{:S(2)}) collective-permute-start(f32[80,128]{1,0:T(8,128)S(1)} %get-tuple-element.38), channel_id=1, source_target_pairs={{0,7},{1,2},{2,1},{3,4},{4,3},{5,6},{6,5},{7,0},{8,15},{9,10},{10,... | collective-permute-start | bytes 122888 | tf_op jit(solution)/shard_map/ppermute | solution.py:542
  47.9 4.3 %collective-permute-start.5 = (f32[80,128]{1,0:T(8,128)S(1)}, f32[80,128]{1,0:T(8,128)S(1)}, u32[]{:S(2)}, u32[]{:S(2)}) collective-permute-start(f32[80,128]{1,0:T(8,128)S(1)} %get-tuple-element.38), channel_id=1, source_target_pairs={{0,1},{1,0},{2,3},{3,2},{4,5},{5,4},{6,7},{7,6},{8,9},{9,8},{10,11... | collective-permute-start | bytes 122888 | tf_op jit(solution)/shard_map/ppermute | solution.py:542
  53.8 6.3 %collective-permute-start.7 = (f32[12,8,128]{2,1,0:T(8,128)S(1)}, f32[12,8,128]{2,1,0:T(8,128)S(1)}, u32[]{:S(2)}, u32[]{:S(2)}) collective-permute-start(f32[12,8,128]{2,1,0:T(8,128)S(1)} %get-tuple-element.42), channel_id=1, source_target_pairs={{0,248},{8,16},{16,8},{24,32},{32,24},{40,48},{48,40},{56,64},{64,... | collective-permute-start | bytes 147464 | tf_op jit(solution)/shard_map/ppermute | solution.py:542
  54.9 5.2 %collective-permute-start.8 = (f32[12,8,128]{2,1,0:T(8,128)S(1)}, f32[12,8,128]{2,1,0:T(8,128)S(1)}, u32[]{:S(2)}, u32[]{:S(2)}) collective-permute-start(f32[12,8,128]{2,1,0:T(8,128)S(1)} %get-tuple-element.43), channel_id=1, source_target_pairs={{0,8},{8,0},{16,24},{24,16},{32,40},{40,32},{48,56},{56,48},{64,72... | collective-permute-start | bytes 147464 | tf_op jit(solution)/shard_map/ppermute | solution.py:542
  60.2 4.9 %collective-permute-start.10 = (f32[40,8,128]{2,1,0:T(8,128)S(1)}, f32[40,8,128]{2,1,0:T(8,128)S(1)}, u32[]{:S(2)}, u32[]{:S(2)}) collective-permute-start(f32[40,8,128]{2,1,0:T(8,128)S(1)} %pad_maximum_fusion.refs_2_), channel_id=1, source_target_pairs={{0,7},{1,2},{2,1},{3,4},{4,3},{5,6},{6,5},{7,0},{8,15},{9,10},{10,... | collective-permute-start | bytes 491528 | tf_op jit(solution)/shard_map/ppermute | solution.py:542
  62.1 3.0 %collective-permute-start.9 = (f32[40,8,128]{2,1,0:T(8,128)S(1)}, f32[40,8,128]{2,1,0:T(8,128)S(1)}, u32[]{:S(2)}, u32[]{:S(2)}) collective-permute-start(f32[40,8,128]{2,1,0:T(8,128)S(1)} %pad_maximum_fusion.refs_2_), channel_id=1, source_target_pairs={{0,1},{1,0},{2,3},{3,2},{4,5},{5,4},{6,7},{7,6},{8,9},{9,8},{10,11... | collective-permute-start | bytes 491528 | tf_op jit(solution)/shard_map/ppermute | solution.py:542
  85.5 3.2 %collective-permute-start.11 = (f32[256,128]{1,0:T(8,128)S(1)}, f32[256,128]{1,0:T(8,128)S(1)}, u32[]{:S(2)}, u32[]{:S(2)}) collective-permute-start(f32[256,128]{1,0:T(8,128)S(1)} %bitcast.8), channel_id=1, source_target_pairs={{0,1},{1,0},{2,3},{3,2},{4,5},{5,4},{6,7},{7,6},{8,9},{9,8},{10,11... | collective-permute-start | bytes 393224 | tf_op jit(solution)/shard_map/ppermute | solution.py:542
  87.5 3.9 %collective-permute-start.13 = (f32[80,128]{1,0:T(8,128)S(1)}, f32[80,128]{1,0:T(8,128)S(1)}, u32[]{:S(2)}, u32[]{:S(2)}) collective-permute-start(f32[80,128]{1,0:T(8,128)S(1)} %get-tuple-element.49), channel_id=1, source_target_pairs={{0,7},{1,2},{2,1},{3,4},{4,3},{5,6},{6,5},{7,0},{8,15},{9,10},{10,... | collective-permute-start | bytes 122888 | tf_op jit(solution)/shard_map/ppermute | solution.py:542
  87.7 3.8 %collective-permute-start.12 = (f32[80,128]{1,0:T(8,128)S(1)}, f32[80,128]{1,0:T(8,128)S(1)}, u32[]{:S(2)}, u32[]{:S(2)}) collective-permute-start(f32[80,128]{1,0:T(8,128)S(1)} %get-tuple-element.49), channel_id=1, source_target_pairs={{0,1},{1,0},{2,3},{3,2},{4,5},{5,4},{6,7},{7,6},{8,9},{9,8},{10,11... | collective-permute-start | bytes 122888 | tf_op jit(solution)/shard_map/ppermute | solution.py:542

commit v3 on v2

--- a/solution.py
+++ b/solution.py
@@ -19,7 +19,14 @@
 
 
 def dot(left, right):
-    return jnp.dot(left, right, precision=lax.Precision.HIGHEST, preferred_element_type=jnp.float32)
+    right = right.astype(jnp.bfloat16)
+    total = None
+    for _ in range(3):
+        part = left.astype(jnp.bfloat16)
+        left = left - part.astype(jnp.float32)
+        product = jnp.dot(part, right, preferred_element_type=jnp.float32)
+        total = product if total is None else total + product
+    return total
 
 
 def iota(rows, dim, lanes=128):
@@ -55,7 +62,7 @@
         below = ref[base - self.ny : base - self.ny + size]
         above = ref[base + self.ny : base + self.ny + size]
         if self.zl > 1:
-            cell = iota(size, 1) % (self.zl * self.nx)
+            cell = iota(size, 1) & (self.zl * self.nx - 1)
             below = pltpu.roll(jnp.where(cell >= (self.zl - 1) * self.nx, below, here), self.nx, 1)
             above = pltpu.roll(jnp.where(cell < self.nx, above, here), 128 - self.nx, 1)
         return (
@@ -82,8 +89,8 @@
             self.close(faces.at[number], 0.0)
         for at, size in self.chunks():
             here, around = self.neighbours(kappa, at, size)
-            y = iota(size, 0) % self.ny + self.y_start
-            x = iota(size, 1) % self.nx
+            y = (iota(size, 0) & (self.ny - 1)) + self.y_start
+            x = iota(size, 1) & (self.nx - 1)
             rows = slice(self.pad + at, self.pad + at + size)
             faces[0, rows] = harmonic(here, around[0])
             faces[2, rows] = jnp.where((y != 0) & (y != self.y_total), harmonic(here, around[2]), 0.0)
@@ -141,7 +148,7 @@
     return index[0] % 2 == 0, index[1] % 2 == 0
 
 
-def kappa_body(index, class_hbm, diff_hbm, phases_hbm, grains_hbm, conc_hbm, kappa_ref, mate_ref, other_ref, classes, diff, phases, grains, sems):
+def kappa_body(index, class_hbm, diff_hbm, phases_hbm, grains_hbm, conc_hbm, kappa_ref, own_ref, mate_ref, other_ref, classes, diff, phases, grains, sems):
     even, _ = parities(index)
     num_phases, num_classes = diff.shape
     pairs = [(class_hbm, classes), (diff_hbm, diff)]
@@ -151,11 +158,12 @@
     pairs += [
         (conc_hbm.at[pl.ds(jnp.where(even, top, 0), HALO)], mate_ref.at[0:HALO]),
         (conc_hbm.at[pl.ds(jnp.where(even, 0, top), HALO)], other_ref.at[0:HALO]),
+        (conc_hbm, own_ref),
     ]
     copies = [pltpu.make_async_copy(source, target, sems.at[i]) for i, (source, target) in enumerate(pairs)]
     for copy in copies:
         copy.start()
-    for copy in copies[:-2]:
+    for copy in copies[:-3]:
         copy.wait()
     grain = grains[...]
     phase = phases[...]
@@ -169,7 +177,7 @@
     kappa_ref[...] = value
     mate_ref[HALO:] = jnp.where(even, value[1:], value[:3])
     other_ref[HALO:] = jnp.where(even, value[:3], value[1:])
-    for copy in copies[-2:]:
+    for copy in copies[-3:]:
         copy.wait()
 
 
@@ -235,7 +243,7 @@
     for block in range(BLOCKS):
         spread[block * 32 : block * 32 + WY] = kappa[8 + block * WY : 8 + (block + 1) * WY]
         spread[block * 32 + WY : block * 32 + 32] = jnp.ones((32 - WY, 128), jnp.float32)
-    pick = lane_map(lambda r, c: matrix(r == 2 * (c % 64), 0.5))
+    pick = lane_map(lambda r, c: matrix(r == 2 * (c & 63), 0.5))
     packed[...] = dot(spread[pl.ds(0, BLOCKS * 16, stride=2), :], pick)
     level.close(kappa_one, 1.0)
     for block in range(BLOCKS):
@@ -246,7 +254,7 @@
 
 
 def to_chunk(rows):
-    group = iota(8, 1) // 32
+    group = iota(8, 1) >> 5
     out = rows[0:8]
     for z in range(1, 4):
         out = jnp.where(group == z, rows[8 * z : 8 * z + 8], out)
@@ -303,7 +311,7 @@
             rs[plane * 32 + WY : plane * 32 + 32] = jnp.zeros((32 - WY, 128), jnp.float32)
         else:
             rs[plane * 32 : plane * 32 + 32] = jnp.zeros((32, 128), jnp.float32)
-    mean_x = lane_map(lambda r, c: matrix(r // 2 == c % 64, 0.125))
+    mean_x = lane_map(lambda r, c: matrix(r >> 1 == (c & 63), 0.125))
     source_one[...] = dot(rs[pl.ds(0, 320, stride=2), :] + rs[pl.ds(1, 320, stride=2), :], mean_x)
     for ref in (oa, kept_one):
         level.close(ref, 0.0)
@@ -313,10 +321,10 @@
     for z in range(4):
         tmp[z * 16 : z * 16 + 16] = tmp[z * 32 : z * 32 + 16] + tmp[z * 32 + 16 : z * 32 + 32]
     halves = tmp[pl.ds(0, 32, stride=2), :] + tmp[pl.ds(1, 32, stride=2), :]
-    mean_two = lane_map(lambda r, c: matrix((r < 64) & (r // 2 == c % 32), 0.125))
+    mean_two = lane_map(lambda r, c: matrix((r < 64) & (r >> 1 == (c & 31)), 0.125))
     values = [to_chunk(dot(halves, mean_two))[2:4]]
     if first:
-        pick_two = lane_map(lambda r, c: matrix((r < 64) & (r == 2 * (c % 32)), 0.5))
+        pick_two = lane_map(lambda r, c: matrix((r < 64) & (r == 2 * (c & 31)), 0.5))
         values.append(to_chunk(dot(packed[pl.ds(48, 32, stride=2), :], pick_two))[2:4])
     repeats = 4 // len(values)
     tile = jnp.concatenate(values * repeats, axis=0)
@@ -361,8 +369,8 @@
             target[pl.ds(start + 2 + y, 4 * SPAN, stride=4), :] = jnp.where(even, two_, one)
 
     interleave(g2, 0, 0)
-    mean_three = lane_map(lambda r, c: matrix(c % 32 == (r // 64) * 16 + (r % 32) // 2, 0.125))
-    mean_four = lane_map(lambda r, c: matrix((r < 32) & (c % 8 == (r % 16) // 2), 0.125))
+    mean_three = lane_map(lambda r, c: matrix((c & 31) == (r >> 6) * 16 + ((r & 31) >> 1), 0.125))
+    mean_four = lane_map(lambda r, c: matrix((r < 32) & ((c & 7) == (r & 15) >> 1), 0.125))
     if first:
         k2, k3, k4 = refs[17:]
         interleave(k2, two.pad, 2)
@@ -401,8 +409,8 @@
         inner = slice(level.pad + start, level.pad + start + count)
         field[inner] = field[inner] + tmp[0:count]
 
-    from_four = lane_map(lambda r, c: matrix((r < 8) & (r == (c % 16) // 2), 1.0))
-    from_three = lane_map(lambda r, c: matrix((r < 32) & (r == (c // 64) * 16 + (c % 32) // 2), 1.0))
+    from_four = lane_map(lambda r, c: matrix((r < 8) & (r == (c & 15) >> 1), 1.0))
+    from_three = lane_map(lambda r, c: matrix((r < 32) & (r == (c >> 6) * 16 + ((c & 31) >> 1)), 1.0))
     low = NEAR - 3
     correct(three, b3, 8 * low, 48, b4[four.pad + 4 * low : four.pad + 4 * low + 24], r3, from_four)
     three.relax(b3, a3, g3, f3, 8 * low, 48)
@@ -423,10 +431,10 @@
     even_z, even = parities(index)
     y_device = index[1]
     level = level_one(y_device)
-    rows = matrix(iota(16, 1, 16) == y_device * 2 - 2 + iota(16, 0, 16) // 2, 1.0)
+    rows = matrix(iota(16, 1, 16) == y_device * 2 - 2 + (iota(16, 0, 16) >> 1), 1.0)
     spread_y = jnp.concatenate([dot(rows, near[16 * part : 16 * part + 16]) for part in range(3)], axis=0)
     by_z = [
-        dot(spread_y, lane_map(lambda r, c, z=z: matrix(r == z * 32 + (c % 64) // 2, 1.0))) for z in range(4)
+        dot(spread_y, lane_map(lambda r, c, z=z: matrix(r == z * 32 + ((c & 63) >> 1), 1.0))) for z in range(4)
     ]
     for plane in range(20):
         part, z = divmod(plane // 2 + 1, 4)
@@ -439,7 +447,7 @@
         oa[at : at + 16] = field + by_z[z][16 * part : 16 * part + 16]
     level.relax(oa, ob, source_one, faces, 4 * 16, 12 * 16)
     level.relax(ob, oa, source_one, faces, 5 * 16, 10 * 16)
-    from_one = lane_map(lambda r, c: matrix((r < 64) & (r == c // 2), 1.0))
+    from_one = lane_map(lambda r, c: matrix((r < 64) & (r == c >> 1), 1.0))
     value = dot(oa[16 + 80 : 16 + 240], from_one)
     spread[pl.ds(0, 160, stride=2), :] = value
     spread[pl.ds(1, 160, stride=2), :] = value
@@ -578,15 +586,15 @@
     index = jnp.stack([lax.axis_index("gz"), y_device]).astype(jnp.int32)
     plane = (4,) + phases.shape[1:]
     part = floats(HALO + 3, 8, 128)
-    kappa, *parts = call(
+    kappa, block, *parts = call(
         kappa_body,
-        [floats(*plane), part, part],
+        [floats(*plane), floats(*phases.shape), part, part],
         [
             pltpu.SMEM(grain_class.shape, jnp.int32),
             pltpu.SMEM(diffusivity.shape, jnp.float32),
             pltpu.VMEM(plane, jnp.int32),
             pltpu.VMEM(plane, jnp.int32),
-            pltpu.SemaphoreType.DMA((12,)),
+            pltpu.SemaphoreType.DMA((13,)),
         ],
         [index] + [
             pltpu.with_memory_space_constraint(array, pltpu.HBM)
@@ -594,7 +602,7 @@
         ],
         pltpu.HBM,
     )
-    own = stack(index, swaps(*parts, Z_AXIS), (concentration, kappa))
+    own = stack(index, swaps(*parts, Z_AXIS), (block, kappa))
     mate, other = swaps(own, own, Y_AXIS)
     (field, *parts), shared, faces = cycle(index, (mate, own, other), None, None, False)
 

time: 94 us -> 92.6 us (0.985)
  no operation moved by 1% of the time
where the time goes in v3:
time: 92.6 us; the launch traced here: 92.4 us
  blocking collectives  39.4 us (43%)
  starting transfers between devices  22.7 us (25%)
  Pallas kernels  15.1 us (16%)
  waiting for transfers between devices  14.9 us (16%)
    all_to_all x2, blocking collectives, to_all(): out = lax.all_to_all(copies, ('gz', 'gx'), 0, 0)  39.4 us
    ppermute x14, starting transfers between devices, swap(): lax.ppermute(array, axis, [(i, partner(i) % count) for i in range(count)])  22.7 us
    pallas_call x7, Pallas kernels, call(): pl.pallas_call(body, out_shape=outs, in_specs=[pl.BlockSpec(memory_space=...  15.1 us
    ppermute x14, waiting for transfers between devices, swap(): lax.ppermute(array, axis, [(i, partner(i) % count) for i in range(count)])  14.9 us
  transfers between devices with their start and end apart: 14, of which 6 were waited for; matrix products, arithmetic and copies ran while one was open for 0% of the time, Pallas kernels for 6%

profile of v3, /device:TPU:1, one launch (start us, length us, event | category | flops | bytes accessed | tf_op | source)
XLA Modules:
  0.0 92.4 jit_solution(2394524414631324859)
XLA Ops:
  0.1 1.7 %shard_map.55 = (f32[4,8,128]{2,1,0:T(8,128)S(1)}, f32[16,8,128]{2,1,0:T(8,128)S(1)}, f32[15,8,128]{2,1,0:T(8,128)S(1)}, f32[15,8,128]{2,1,0:T(8,128)S(1)}) custom-call(s32[2]{0:T(128)S(1)} %pad_add_fusion.index.refs_0_, s32[64]{0:T(128)} %class_hbm.1, f32[3,4]{1,0:T(4,128)} %diff_hbm.1, s32[16,8,128]{2,1,0:T(8,128)} %phases_hbm.1, ...), custom_call_target="tpu_custom_call" | custom-call | tf_op jit(solution)/shard_map/pallas_call | solution.py:475
  1.8 8.9 %collective-permute-start = (f32[15,8,128]{2,1,0:T(8,128)S(1)}, f32[15,8,128]{2,1,0:T(8,128)S(1)}, u32[]{:S(2)}, u32[]{:S(2)}) collective-permute-start(f32[15,8,128]{2,1,0:T(8,128)S(1)} %get-tuple-element.30), channel_id=1, source_target_pairs={{0,248},{8,16},{16,8},{24,32},{32,24},{40,48},{48,40},{56,64},{64,... | collective-permute-start | bytes 184328 | tf_op jit(solution)/shard_map/ppermute | solution.py:550
  10.7 1.6 %collective-permute-done = f32[15,8,128]{2,1,0:T(8,128)S(1)} collective-permute-done((f32[15,8,128]{2,1,0:T(8,128)S(1)}, f32[15,8,128]{2,1,0:T(8,128)S(1)}, u32[]{:S(2)}, u32[]{:S(2)}) %collective-permute-start) | collective-permute-done | bytes 61472 | tf_op jit(solution)/shard_map/ppermute | solution.py:550
  12.3 1.5 %collective-permute-done.1 = f32[15,8,128]{2,1,0:T(8,128)S(1)} collective-permute-done((f32[15,8,128]{2,1,0:T(8,128)S(1)}, f32[15,8,128]{2,1,0:T(8,128)S(1)}, u32[]{:S(2)}, u32[]{:S(2)}) %collective-permute-start.1) | collective-permute-done | bytes 61472 | tf_op jit(solution)/shard_map/ppermute | solution.py:550
  13.9 3.3 %collective-permute-start.3 = (f32[50,8,128]{2,1,0:T(8,128)S(1)}, f32[50,8,128]{2,1,0:T(8,128)S(1)}, u32[]{:S(2)}, u32[]{:S(2)}) collective-permute-start(f32[50,8,128]{2,1,0:T(8,128)S(1)} %constant_dynamic-update-slice_fusion.refs_2_), channel_id=1, source_target_pairs={{0,7},{1,2},{2,1},{3,4},{4,3},{5,6},{6,5},{7,0},{8,15},{9,10},{10,... | collective-permute-start | bytes 614408 | tf_op jit(solution)/shard_map/ppermute | solution.py:550
  17.2 3.7 %collective-permute-done.3.refs_3_ = f32[50,8,128]{2,1,0:T(8,128)S(1)} collective-permute-done((f32[50,8,128]{2,1,0:T(8,128)S(1)}, f32[50,8,128]{2,1,0:T(8,128)S(1)}, u32[]{:S(2)}, u32[]{:S(2)}) %collective-permute-start.3) | collective-permute-done | bytes 204832 | tf_op jit(solution)/shard_map/ppermute | solution.py:550
  20.9 2.1 %shard_map.56 = (f32[512,128]{1,0:T(8,128)S(1)}, f32[80,128]{1,0:T(8,128)S(1)}, f32[480,128]{1,0:T(8,128)S(1)}, f32[320,128]{1,0:T(8,128)S(1)}, f32[352,128]{1,0...) custom-call(s32[2]{0:T(128)S(1)} %pad_add_fusion.index.refs_0_, ...), custom_call_target="tpu_custom_call" | custom-call | tf_op jit(solution)/shard_map/pallas_call | solution.py:475
  23.0 21.1 %all_to_all.10 = f32[128,4,128]{2,1,0:T(4,128)S(1)} all-to-all(f32[128,4,128]{2,1,0:T(4,128)S(1)} %bitcast.10), channel_id=1, replica_groups=mesh['gz'=32,'gx'=4,'core'=2] {'gz','gx'}, dimensions={0} | all-to-all | bytes 524288 | tf_op jit(solution)/shard_map/all_to_all | solution.py:561
  44.1 2.9 %collective-permute-start.4 = (f32[512,128]{1,0:T(8,128)S(1)}, f32[512,128]{1,0:T(8,128)S(1)}, u32[]{:S(2)}, u32[]{:S(2)}) collective-permute-start(f32[512,128]{1,0:T(8,128)S(1)} %bitcast.6), channel_id=1, source_target_pairs={{0,1},{1,0},{2,3},{3,2},{4,5},{5,4},{6,7},{7,6},{8,9},{9,8},{10,11... | collective-permute-start | bytes 786440 | tf_op jit(solution)/shard_map/ppermute | solution.py:550
  47.0 0.8 collective-permute-start.5
  47.9 0.3 collective-permute-done.4.refs_2_
  48.2 3.0 %shard_map.57 = (f32[48,128]{1,0:T(8,128)S(1)}, f32[6,352,128]{2,1,0:T(8,128)S(1)}, f32[6,176,128]{2,1,0:T(8,128)S(1)}, f32[6,96,128]{2,1,0:T(8,128)S(1)}) custom-call(s32[2]{0:T(128)S(1)} %pad_add_fusion.index.refs_0_, f32[512,128]{1,0:T(8,128)S(1)} %bitcast.7, f32[512,128]{1,0:T(8,128)S(1)} %collective-permute-done.4.refs_2_), custom_call_target="tpu_custom_call" | custom-call | tf_op jit(solution)/shard_map/pallas_call | solution.py:475
  51.2 1.5 %shard_map.58 = (f32[16,8,128]{2,1,0:T(8,128)S(1)}, f32[12,8,128]{2,1,0:T(8,128)S(1)}, f32[12,8,128]{2,1,0:T(8,128)S(1)}) custom-call(s32[2]{0:T(128)S(1)} %pad_add_fusion.index.refs_0_, f32[960,128]{1,0:T(8,128)S(1)} %get-tuple-element.34.refs_1_.refs_4_, f32[10,11,24,128]{3,2,1,0:T(8,128)S(1)} %get-tuple-element.35.refs_2_.refs_5_, ...), custom_call_target="tpu_custom_call" | custom-call | tf_op jit(solution)/shard_map/pallas_call | solution.py:475
  52.7 1.1 %collective-permute-start.7 = (f32[12,8,128]{2,1,0:T(8,128)S(1)}, f32[12,8,128]{2,1,0:T(8,128)S(1)}, u32[]{:S(2)}, u32[]{:S(2)}) collective-permute-start(f32[12,8,128]{2,1,0:T(8,128)S(1)} %get-tuple-element.44), channel_id=1, source_target_pairs={{0,248},{8,16},{16,8},{24,32},{32,24},{40,48},{48,40},{56,64},{64,... | collective-permute-start | bytes 147464 | tf_op jit(solution)/shard_map/ppermute | solution.py:550
  53.8 0.3 collective-permute-start.8
  54.2 4.9 %collective-permute-done.7 = f32[12,8,128]{2,1,0:T(8,128)S(1)} collective-permute-done((f32[12,8,128]{2,1,0:T(8,128)S(1)}, f32[12,8,128]{2,1,0:T(8,128)S(1)}, u32[]{:S(2)}, u32[]{:S(2)}) %collective-permute-start.7) | collective-permute-done | bytes 49184 | tf_op jit(solution)/shard_map/ppermute | solution.py:550
  59.1 1.9 %collective-permute-start.10 = (f32[40,8,128]{2,1,0:T(8,128)S(1)}, f32[40,8,128]{2,1,0:T(8,128)S(1)}, u32[]{:S(2)}, u32[]{:S(2)}) collective-permute-start(f32[40,8,128]{2,1,0:T(8,128)S(1)} %pad_maximum_fusion.refs_2_), channel_id=1, source_target_pairs={{0,7},{1,2},{2,1},{3,4},{4,3},{5,6},{6,5},{7,0},{8,15},{9,10},{10,... | collective-permute-start | bytes 491528 | tf_op jit(solution)/shard_map/ppermute | solution.py:550
  61.1 2.9 %collective-permute-done.10.refs_3_ = f32[40,8,128]{2,1,0:T(8,128)S(1)} collective-permute-done((f32[40,8,128]{2,1,0:T(8,128)S(1)}, f32[40,8,128]{2,1,0:T(8,128)S(1)}, u32[]{:S(2)}, u32[]{:S(2)}) %collective-permute-start.10) | collective-permute-done | bytes 163872 | tf_op jit(solution)/shard_map/ppermute | solution.py:550
  64.0 1.9 %shard_map.59 = (f32[256,128]{1,0:T(8,128)S(1)}, f32[80,128]{1,0:T(8,128)S(1)}, f32[480,128]{1,0:T(8,128)S(1)}, f32[320,128]{1,0:T(8,128)S(1)}, f32[352,128]{1,0:T(8,128)S(1)}) custom-call(s32[2]{0:T(128)S(1)} %pad_add_fusion.index.refs_0_, f32[40,8,128]{2,1,0:T(8,128)S(1)} %collective-permute-done.9.refs_1_, f32[40,8,128]{2,1,0:T(8,128)S(1)} %pad_maximum_fusion.refs_2_, ...), custom_call_target="tpu_custom_call" | custom-call | tf_op jit(solution)/shard_map/pallas_call | solution.py:475
  65.9 18.3 %all_to_all.11 = f32[128,2,128]{2,1,0:T(2,128)S(1)} all-to-all(f32[128,2,128]{2,1,0:T(2,128)S(1)} %bitcast.11), channel_id=1, replica_groups=mesh['gz'=32,'gx'=4,'core'=2] {'gz','gx'}, dimensions={0} | all-to-all | bytes 262144 | tf_op jit(solution)/shard_map/all_to_all | solution.py:561
  84.3 2.1 %collective-permute-start.11 = (f32[256,128]{1,0:T(8,128)S(1)}, f32[256,128]{1,0:T(8,128)S(1)}, u32[]{:S(2)}, u32[]{:S(2)}) collective-permute-start(f32[256,128]{1,0:T(8,128)S(1)} %bitcast.8), channel_id=1, source_target_pairs={{0,1},{1,0},{2,3},{3,2},{4,5},{5,4},{6,7},{7,6},{8,9},{9,8},{10,11... | collective-permute-start | bytes 393224 | tf_op jit(solution)/shard_map/ppermute | solution.py:550
  86.5 1.0 %collective-permute-start.12 = (f32[80,128]{1,0:T(8,128)S(1)}, f32[80,128]{1,0:T(8,128)S(1)}, u32[]{:S(2)}, u32[]{:S(2)}) collective-permute-start(f32[80,128]{1,0:T(8,128)S(1)} %get-tuple-element.51), channel_id=1, source_target_pairs={{0,1},{1,0},{2,3},{3,2},{4,5},{5,4},{6,7},{7,6},{8,9},{9,8},{10,11... | collective-permute-start | bytes 122888 | tf_op jit(solution)/shard_map/ppermute | solution.py:550
  87.5 2.7 %shard_map.60.refs_5_ = f32[48,128]{1,0:T(8,128)S(1)} custom-call(s32[2]{0:T(128)S(1)} %pad_add_fusion.index.refs_0_, f32[256,128]{1,0:T(8,128)S(1)} %bitcast.9, f32[256,128]{1,0:T(8,128)S(1)} %collective-permute-done.11.refs_2_, f32[6,352,128]{2,1,0:T(8,128)S(1)} %get-tuple-element.48.refs_3_, f32[6,176,128]{2,1,0:T(8,128)S(1)} %get-tuple-element.49.refs_4_, ...), custom_call_target="tpu_custom_call" | custom-call | tf_op jit(solution)/shard_map/pallas_call | solution.py:475
  90.2 2.2 %shard_map.61 = f32[16,8,128]{2,1,0:T(8,128)} custom-call(s32[2]{0:T(128)S(1)} %pad_add_fusion.index.refs_0_, f32[960,128]{1,0:T(8,128)S(1)} %get-tuple-element.34.refs_1_.refs_4_, f32[10,11,24,128]{3,2,1,0:T(8,128)S(1)} %get-tuple-element.35.refs_2_.refs_5_, f32[11,24,128]{2,1,0:T(8,128)S(1)} %get-tuple-element.36.refs_3_.refs_6_, ...), custom_call_target="tpu_custom_call" | custom-call | tf_op jit(solution)/shard_map/pallas_call | solution.py:475
  (23 shorter events, 0.4 us)
Async XLA Ops:
  1.8 10.6 %collective-permute-start = (f32[15,8,128]{2,1,0:T(8,128)S(1)}, f32[15,8,128]{2,1,0:T(8,128)S(1)}, u32[]{:S(2)}, u32[]{:S(2)}) collective-permute-start(f32[15,8,128]{2,1,0:T(8,128)S(1)} %get-tuple-element.30), channel_id=1, source_target_pairs={{0,248},{8,16},{16,8},{24,32},{32,24},{40,48},{48,40},{56,64},{64,... | collective-permute-start | bytes 184328 | tf_op jit(solution)/shard_map/ppermute | solution.py:550
  10.7 3.1 %collective-permute-start.1 = (f32[15,8,128]{2,1,0:T(8,128)S(1)}, f32[15,8,128]{2,1,0:T(8,128)S(1)}, u32[]{:S(2)}, u32[]{:S(2)}) collective-permute-start(f32[15,8,128]{2,1,0:T(8,128)S(1)} %get-tuple-element.31), channel_id=1, source_target_pairs={{0,8},{8,0},{16,24},{24,16},{32,40},{40,32},{48,56},{56,48},{64,72... | collective-permute-start | bytes 184328 | tf_op jit(solution)/shard_map/ppermute | solution.py:550
  13.9 7.0 %collective-permute-start.3 = (f32[50,8,128]{2,1,0:T(8,128)S(1)}, f32[50,8,128]{2,1,0:T(8,128)S(1)}, u32[]{:S(2)}, u32[]{:S(2)}) collective-permute-start(f32[50,8,128]{2,1,0:T(8,128)S(1)} %constant_dynamic-update-slice_fusion.refs_2_), channel_id=1, source_target_pairs={{0,7},{1,2},{2,1},{3,4},{4,3},{5,6},{6,5},{7,0},{8,15},{9,10},{10,... | collective-permute-start | bytes 614408 | tf_op jit(solution)/shard_map/ppermute | solution.py:550
  17.2 3.7 %collective-permute-start.2 = (f32[50,8,128]{2,1,0:T(8,128)S(1)}, f32[50,8,128]{2,1,0:T(8,128)S(1)}, u32[]{:S(2)}, u32[]{:S(2)}) collective-permute-start(f32[50,8,128]{2,1,0:T(8,128)S(1)} %constant_dynamic-update-slice_fusion.refs_2_), channel_id=1, source_target_pairs={{0,1},{1,0},{2,3},{3,2},{4,5},{5,4},{6,7},{7,6},{8,9},{9,8},{10,11... | collective-permute-start | bytes 614408 | tf_op jit(solution)/shard_map/ppermute | solution.py:550
  44.1 4.1 %collective-permute-start.4 = (f32[512,128]{1,0:T(8,128)S(1)}, f32[512,128]{1,0:T(8,128)S(1)}, u32[]{:S(2)}, u32[]{:S(2)}) collective-permute-start(f32[512,128]{1,0:T(8,128)S(1)} %bitcast.6), channel_id=1, source_target_pairs={{0,1},{1,0},{2,3},{3,2},{4,5},{5,4},{6,7},{7,6},{8,9},{9,8},{10,11... | collective-permute-start | bytes 786440 | tf_op jit(solution)/shard_map/ppermute | solution.py:550
  47.0 4.2 %collective-permute-start.6 = (f32[80,128]{1,0:T(8,128)S(1)}, f32[80,128]{1,0:T(8,128)S(1)}, u32[]{:S(2)}, u32[]{:S(2)}) collective-permute-start(f32[80,128]{1,0:T(8,128)S(1)} %get-tuple-element.40), channel_id=1, source_target_pairs={{0,7},{1,2},{2,1},{3,4},{4,3},{5,6},{6,5},{7,0},{8,15},{9,10},{10,... | collective-permute-start | bytes 122888 | tf_op jit(solution)/shard_map/ppermute | solution.py:550
  47.0 4.1 %collective-permute-start.5 = (f32[80,128]{1,0:T(8,128)S(1)}, f32[80,128]{1,0:T(8,128)S(1)}, u32[]{:S(2)}, u32[]{:S(2)}) collective-permute-start(f32[80,128]{1,0:T(8,128)S(1)} %get-tuple-element.40), channel_id=1, source_target_pairs={{0,1},{1,0},{2,3},{3,2},{4,5},{5,4},{6,7},{7,6},{8,9},{9,8},{10,11... | collective-permute-start | bytes 122888 | tf_op jit(solution)/shard_map/ppermute | solution.py:550
  52.7 6.3 %collective-permute-start.7 = (f32[12,8,128]{2,1,0:T(8,128)S(1)}, f32[12,8,128]{2,1,0:T(8,128)S(1)}, u32[]{:S(2)}, u32[]{:S(2)}) collective-permute-start(f32[12,8,128]{2,1,0:T(8,128)S(1)} %get-tuple-element.44), channel_id=1, source_target_pairs={{0,248},{8,16},{16,8},{24,32},{32,24},{40,48},{48,40},{56,64},{64,... | collective-permute-start | bytes 147464 | tf_op jit(solution)/shard_map/ppermute | solution.py:550
  53.8 5.2 %collective-permute-start.8 = (f32[12,8,128]{2,1,0:T(8,128)S(1)}, f32[12,8,128]{2,1,0:T(8,128)S(1)}, u32[]{:S(2)}, u32[]{:S(2)}) collective-permute-start(f32[12,8,128]{2,1,0:T(8,128)S(1)} %get-tuple-element.45), channel_id=1, source_target_pairs={{0,8},{8,0},{16,24},{24,16},{32,40},{40,32},{48,56},{56,48},{64,72... | collective-permute-start | bytes 147464 | tf_op jit(solution)/shard_map/ppermute | solution.py:550
  59.1 4.9 %collective-permute-start.10 = (f32[40,8,128]{2,1,0:T(8,128)S(1)}, f32[40,8,128]{2,1,0:T(8,128)S(1)}, u32[]{:S(2)}, u32[]{:S(2)}) collective-permute-start(f32[40,8,128]{2,1,0:T(8,128)S(1)} %pad_maximum_fusion.refs_2_), channel_id=1, source_target_pairs={{0,7},{1,2},{2,1},{3,4},{4,3},{5,6},{6,5},{7,0},{8,15},{9,10},{10,... | collective-permute-start | bytes 491528 | tf_op jit(solution)/shard_map/ppermute | solution.py:550
  61.0 3.0 %collective-permute-start.9 = (f32[40,8,128]{2,1,0:T(8,128)S(1)}, f32[40,8,128]{2,1,0:T(8,128)S(1)}, u32[]{:S(2)}, u32[]{:S(2)}) collective-permute-start(f32[40,8,128]{2,1,0:T(8,128)S(1)} %pad_maximum_fusion.refs_2_), channel_id=1, source_target_pairs={{0,1},{1,0},{2,3},{3,2},{4,5},{5,4},{6,7},{7,6},{8,9},{9,8},{10,11... | collective-permute-start | bytes 491528 | tf_op jit(solution)/shard_map/ppermute | solution.py:550
  84.3 3.2 %collective-permute-start.11 = (f32[256,128]{1,0:T(8,128)S(1)}, f32[256,128]{1,0:T(8,128)S(1)}, u32[]{:S(2)}, u32[]{:S(2)}) collective-permute-start(f32[256,128]{1,0:T(8,128)S(1)} %bitcast.8), channel_id=1, source_target_pairs={{0,1},{1,0},{2,3},{3,2},{4,5},{5,4},{6,7},{7,6},{8,9},{9,8},{10,11... | collective-permute-start | bytes 393224 | tf_op jit(solution)/shard_map/ppermute | solution.py:550
  86.4 3.8 %collective-permute-start.13 = (f32[80,128]{1,0:T(8,128)S(1)}, f32[80,128]{1,0:T(8,128)S(1)}, u32[]{:S(2)}, u32[]{:S(2)}) collective-permute-start(f32[80,128]{1,0:T(8,128)S(1)} %get-tuple-element.51), channel_id=1, source_target_pairs={{0,7},{1,2},{2,1},{3,4},{4,3},{5,6},{6,5},{7,0},{8,15},{9,10},{10,... | collective-permute-start | bytes 122888 | tf_op jit(solution)/shard_map/ppermute | solution.py:550
  86.5 3.7 %collective-permute-start.12 = (f32[80,128]{1,0:T(8,128)S(1)}, f32[80,128]{1,0:T(8,128)S(1)}, u32[]{:S(2)}, u32[]{:S(2)}) collective-permute-start(f32[80,128]{1,0:T(8,128)S(1)} %get-tuple-element.51), channel_id=1, source_target_pairs={{0,1},{1,0},{2,3},{3,2},{4,5},{5,4},{6,7},{7,6},{8,9},{9,8},{10,11... | collective-permute-start | bytes 122888 | tf_op jit(solution)/shard_map/ppermute | solution.py:550

commit v4 on v3

--- a/solution.py
+++ b/solution.py
@@ -19,14 +19,7 @@
 
 
 def dot(left, right):
-    right = right.astype(jnp.bfloat16)
-    total = None
-    for _ in range(3):
-        part = left.astype(jnp.bfloat16)
-        left = left - part.astype(jnp.float32)
-        product = jnp.dot(part, right, preferred_element_type=jnp.float32)
-        total = product if total is None else total + product
-    return total
+    return jnp.dot(left, right, precision=lax.Precision.HIGHEST, preferred_element_type=jnp.float32)
 
 
 def iota(rows, dim, lanes=128):
@@ -42,8 +35,8 @@
 
 
 class Level:
-    def __init__(self, planes, ny, nx, zl, pad, y_start, y_total, chunk):
-        self.planes, self.ny, self.nx, self.zl, self.pad = planes, ny, nx, zl, pad
+    def __init__(self, planes, ny, zl, step, span, pad, y_start, y_total, chunk):
+        self.planes, self.ny, self.zl, self.step, self.span, self.pad = planes, ny, zl, step, span, pad
         self.y_start, self.y_total = y_start, y_total
         self.rows = planes * ny
         self.chunk = min(chunk, self.rows)
@@ -62,9 +55,10 @@
         below = ref[base - self.ny : base - self.ny + size]
         above = ref[base + self.ny : base + self.ny + size]
         if self.zl > 1:
-            cell = iota(size, 1) & (self.zl * self.nx - 1)
-            below = pltpu.roll(jnp.where(cell >= (self.zl - 1) * self.nx, below, here), self.nx, 1)
-            above = pltpu.roll(jnp.where(cell < self.nx, above, here), 128 - self.nx, 1)
+            width = 128 // self.zl
+            lane = iota(size, 1)
+            below = pltpu.roll(jnp.where(lane >= 128 - width, below, here), width, 1)
+            above = pltpu.roll(jnp.where(lane < width, above, here), 128 - width, 1)
         return (
             here,
             (
@@ -72,7 +66,7 @@
                 above,
                 ref[base - 1 : base - 1 + size],
                 ref[base + 1 : base + 1 + size],
-                pltpu.roll(here, 1, 1),
+                pltpu.roll(here, self.step, 1),
             ),
         )
 
@@ -90,18 +84,18 @@
         for at, size in self.chunks():
             here, around = self.neighbours(kappa, at, size)
             y = (iota(size, 0) & (self.ny - 1)) + self.y_start
-            x = iota(size, 1) & (self.nx - 1)
+            x = iota(size, 1) & (self.span - 1)
             rows = slice(self.pad + at, self.pad + at + size)
             faces[0, rows] = harmonic(here, around[0])
             faces[2, rows] = jnp.where((y != 0) & (y != self.y_total), harmonic(here, around[2]), 0.0)
-            faces[3, rows] = jnp.where(x != 0, harmonic(here, around[4]), 0.0)
+            faces[3, rows] = jnp.where(x >= self.step, harmonic(here, around[4]), 0.0)
         for at, size in self.chunks():
             rows = slice(self.pad + at, self.pad + at + size)
             z_low, around = self.neighbours(faces.at[0], at, size)
             z_high = around[1]
             y_high = faces[2, self.pad + at + 1 : self.pad + at + 1 + size]
             x_low = faces[3, rows]
-            total = 1.0 + z_low + z_high + faces[2, rows] + y_high + x_low + pltpu.roll(x_low, 127, 1)
+            total = 1.0 + z_low + z_high + faces[2, rows] + y_high + x_low + pltpu.roll(x_low, 128 - self.step, 1)
             faces[1, rows] = z_high
             faces[4, rows] = 0.8 / total
             faces[5, rows] = total
@@ -118,7 +112,7 @@
             + faces[2, rows] * around[2]
             + faces[2, next_rows] * around[3]
             + x_low * around[4]
-            + pltpu.roll(x_low * here, 127, 1)
+            + pltpu.roll(x_low * here, 128 - self.step, 1)
         )
         return here, total
 
@@ -142,6 +136,16 @@
     def pairs(self, ref):
         half = self.rows // 2
         return ref[pl.ds(0, half, stride=2), :] + ref[pl.ds(1, half, stride=2), :]
+
+
+def coarsen(value, step, zl=1):
+    lane = iota(value.shape[0], 1)
+    value = value + jnp.where((lane & step) == 0, pltpu.roll(value, 128 - step, 1), pltpu.roll(value, step, 1))
+    if zl == 4:
+        value = value + jnp.where((lane & 32) == 0, pltpu.roll(value, 96, 1), pltpu.roll(value, 32, 1))
+    if zl == 2:
+        value = value + pltpu.roll(value, 64, 1)
+    return 0.125 * value
 
 
 def parities(index):
@@ -236,15 +240,14 @@
 
 
 def level_one(y_device):
-    return Level(20, 16, 64, 1, 16, y_device * 4 - 4, 32, 160)
+    return Level(20, 16, 1, 2, 128, 16, y_device * 4 - 4, 32, 160)
 
 
 def build_one(level, kappa, spread, packed, kappa_one, faces):
     for block in range(BLOCKS):
         spread[block * 32 : block * 32 + WY] = kappa[8 + block * WY : 8 + (block + 1) * WY]
         spread[block * 32 + WY : block * 32 + 32] = jnp.ones((32 - WY, 128), jnp.float32)
-    pick = lane_map(lambda r, c: matrix(r == 2 * (c & 63), 0.5))
-    packed[...] = dot(spread[pl.ds(0, BLOCKS * 16, stride=2), :], pick)
+    packed[...] = 0.5 * spread[pl.ds(0, BLOCKS * 16, stride=2), :]
     level.close(kappa_one, 1.0)
     for block in range(BLOCKS):
         value = packed[block * 16 : block * 16 + 16]
@@ -311,8 +314,7 @@
             rs[plane * 32 + WY : plane * 32 + 32] = jnp.zeros((32 - WY, 128), jnp.float32)
         else:
             rs[plane * 32 : plane * 32 + 32] = jnp.zeros((32, 128), jnp.float32)
-    mean_x = lane_map(lambda r, c: matrix(r >> 1 == (c & 63), 0.125))
-    source_one[...] = dot(rs[pl.ds(0, 320, stride=2), :] + rs[pl.ds(1, 320, stride=2), :], mean_x)
+    source_one[...] = coarsen(rs[pl.ds(0, 320, stride=2), :] + rs[pl.ds(1, 320, stride=2), :], 1)
     for ref in (oa, kept_one):
         level.close(ref, 0.0)
     level.start(oa, source_one, faces)
@@ -321,10 +323,10 @@
     for z in range(4):
         tmp[z * 16 : z * 16 + 16] = tmp[z * 32 : z * 32 + 16] + tmp[z * 32 + 16 : z * 32 + 32]
     halves = tmp[pl.ds(0, 32, stride=2), :] + tmp[pl.ds(1, 32, stride=2), :]
-    mean_two = lane_map(lambda r, c: matrix((r < 64) & (r >> 1 == (c & 31)), 0.125))
+    mean_two = lane_map(lambda r, c: matrix(((r & 1) == 0) & (r >> 2 == (c & 31)), 0.125))
     values = [to_chunk(dot(halves, mean_two))[2:4]]
     if first:
-        pick_two = lane_map(lambda r, c: matrix((r < 64) & (r == 2 * (c & 31)), 0.5))
+        pick_two = lane_map(lambda r, c: matrix(r == 4 * (c & 31), 0.5))
         values.append(to_chunk(dot(packed[pl.ds(48, 32, stride=2), :], pick_two))[2:4])
     repeats = 4 // len(values)
     tile = jnp.concatenate(values * repeats, axis=0)
@@ -336,9 +338,9 @@
 
 def coarse_levels():
     return (
-        Level(SPAN, 16, 32, 4, 16, 0, 16, 160),
-        Level(SPAN, 8, 16, 2, 8, 0, 8, 160),
-        Level(SPAN, 4, 8, 1, 8, 0, 4, 128),
+        Level(SPAN, 16, 4, 1, 32, 16, 0, 16, 160),
+        Level(SPAN, 8, 2, 2, 32, 8, 0, 8, 160),
+        Level(SPAN, 4, 1, 4, 32, 8, 0, 4, 128),
     )
 
 
@@ -369,19 +371,17 @@
             target[pl.ds(start + 2 + y, 4 * SPAN, stride=4), :] = jnp.where(even, two_, one)
 
     interleave(g2, 0, 0)
-    mean_three = lane_map(lambda r, c: matrix((c & 31) == (r >> 6) * 16 + ((r & 31) >> 1), 0.125))
-    mean_four = lane_map(lambda r, c: matrix((r < 32) & ((c & 7) == (r & 15) >> 1), 0.125))
     if first:
         k2, k3, k4 = refs[17:]
         interleave(k2, two.pad, 2)
         two.close(k2, 1.0)
         two.build(k2, f2)
         r2[...] = k2[two.pad : two.pad + two.rows]
-        k3[three.pad : three.pad + three.rows] = 0.5 * dot(two.pairs(r2), mean_three)
+        k3[three.pad : three.pad + three.rows] = 0.5 * coarsen(two.pairs(r2), 1, 4)
         three.close(k3, 1.0)
         three.build(k3, f3)
         r3[...] = k3[three.pad : three.pad + three.rows]
-        k4[four.pad : four.pad + four.rows] = 0.5 * dot(three.pairs(r3), mean_four)
+        k4[four.pad : four.pad + four.rows] = 0.5 * coarsen(three.pairs(r3), 2, 2)
         four.close(k4, 1.0)
         four.build(k4, f4)
     for level, fields in ((two, (a2, b2)), (three, (a3, b3)), (four, (a4, b4))):
@@ -391,32 +391,29 @@
     two.start(a2, g2, f2)
     two.relax(a2, b2, g2, f2)
     two.defect(b2, g2, f2, r2)
-    g3[...] = dot(two.pairs(r2), mean_three)
+    g3[...] = coarsen(two.pairs(r2), 1, 4)
     three.start(a3, g3, f3)
     three.relax(a3, b3, g3, f3)
     three.defect(b3, g3, f3, r3)
-    g4[...] = dot(three.pairs(r3), mean_four)
+    g4[...] = coarsen(three.pairs(r3), 2, 2)
     four.start(a4, g4, f4)
     for _ in range(2):
         four.relax(a4, b4, g4, f4)
         four.relax(b4, a4, g4, f4)
     four.relax(a4, b4, g4, f4)
 
-    def correct(level, field, start, count, coarse, tmp, spread_lanes):
-        value = dot(coarse, spread_lanes)
+    def correct(level, field, start, count, value, tmp):
         tmp[pl.ds(0, count // 2, stride=2), :] = value
         tmp[pl.ds(1, count // 2, stride=2), :] = value
         inner = slice(level.pad + start, level.pad + start + count)
         field[inner] = field[inner] + tmp[0:count]
 
-    from_four = lane_map(lambda r, c: matrix((r < 8) & (r == (c & 15) >> 1), 1.0))
-    from_three = lane_map(lambda r, c: matrix((r < 32) & (r == (c >> 6) * 16 + ((c & 31) >> 1)), 1.0))
     low = NEAR - 3
-    correct(three, b3, 8 * low, 48, b4[four.pad + 4 * low : four.pad + 4 * low + 24], r3, from_four)
+    correct(three, b3, 8 * low, 48, b4[four.pad + 4 * low : four.pad + 4 * low + 24], r3)
     three.relax(b3, a3, g3, f3, 8 * low, 48)
     low = NEAR - 1
     three.relax(a3, b3, g3, f3, 8 * low, 24)
-    correct(two, b2, 16 * low, 48, b3[three.pad + 8 * low : three.pad + 8 * low + 24], r2, from_three)
+    correct(two, b2, 16 * low, 48, b3[three.pad + 8 * low : three.pad + 8 * low + 24], r2)
     two.relax(b2, a2, g2, f2, 16 * low, 48)
     two.relax(a2, b2, g2, f2, 16 * low, 48)
     near[...] = b2[two.pad + 16 * low : two.pad + 16 * low + 48]
@@ -434,7 +431,7 @@
     rows = matrix(iota(16, 1, 16) == y_device * 2 - 2 + (iota(16, 0, 16) >> 1), 1.0)
     spread_y = jnp.concatenate([dot(rows, near[16 * part : 16 * part + 16]) for part in range(3)], axis=0)
     by_z = [
-        dot(spread_y, lane_map(lambda r, c, z=z: matrix(r == z * 32 + ((c & 63) >> 1), 1.0))) for z in range(4)
+        dot(spread_y, lane_map(lambda r, c, z=z: matrix(r == z * 32 + (c >> 2), 1.0))) for z in range(4)
     ]
     for plane in range(20):
         part, z = divmod(plane // 2 + 1, 4)
@@ -447,8 +444,7 @@
         oa[at : at + 16] = field + by_z[z][16 * part : 16 * part + 16]
     level.relax(oa, ob, source_one, faces, 4 * 16, 12 * 16)
     level.relax(ob, oa, source_one, faces, 5 * 16, 10 * 16)
-    from_one = lane_map(lambda r, c: matrix((r < 64) & (r == c >> 1), 1.0))
-    value = dot(oa[16 + 80 : 16 + 240], from_one)
+    value = oa[16 + 80 : 16 + 240]
     spread[pl.ds(0, 160, stride=2), :] = value
     spread[pl.ds(1, 160, stride=2), :] = value
     for z in range(10, 30):

time: 92.6 us -> 92.1 us (level)
  transfers between devices with their start and end apart: 14 -> 14, of which waited for: 6 -> 7; matrix products, arithmetic and copies ran while one was open for 0% -> 0% of each run, Pallas kernels for 6% -> 6%
where the time goes in v4:
time: 92.1 us; the launch traced here: 91.9 us
  blocking collectives  39.4 us (43%)
  starting transfers between devices  22.6 us (25%)
  waiting for transfers between devices  15.3 us (17%)
  Pallas kernels  14.3 us (16%)
    all_to_all x2, blocking collectives, to_all(): out = lax.all_to_all(copies, ('gz', 'gx'), 0, 0)  39.4 us
    ppermute x14, starting transfers between devices, swap(): lax.ppermute(array, axis, [(i, partner(i) % count) for i in range(count)])  22.6 us
    ppermute x14, waiting for transfers between devices, swap(): lax.ppermute(array, axis, [(i, partner(i) % count) for i in range(count)])  15.3 us
    pallas_call x7, Pallas kernels, call(): pl.pallas_call(body, out_shape=outs, in_specs=[pl.BlockSpec(memory_space=...  14.3 us
  transfers between devices with their start and end apart: 14, of which 7 were waited for; matrix products, arithmetic and copies ran while one was open for 0% of the time, Pallas kernels for 6%

profile of v4, /device:TPU:1, one launch (start us, length us, event | category | flops | bytes accessed | tf_op | source)
XLA Modules:
  0.0 91.9 jit_solution(8949038375516831109)
XLA Ops:
  0.1 1.7 %shard_map.55 = (f32[4,8,128]{2,1,0:T(8,128)S(1)}, f32[16,8,128]{2,1,0:T(8,128)S(1)}, f32[15,8,128]{2,1,0:T(8,128)S(1)}, f32[15,8,128]{2,1,0:T(8,128)S(1)}) custom-call(s32[2]{0:T(128)S(1)} %pad_add_fusion.index.refs_0_, s32[64]{0:T(128)} %class_hbm.1, f32[3,4]{1,0:T(4,128)} %diff_hbm.1, s32[16,8,128]{2,1,0:T(8,128)} %phases_hbm.1, ...), custom_call_target="tpu_custom_call" | custom-call | tf_op jit(solution)/shard_map/pallas_call | solution.py:471
  1.8 8.9 %collective-permute-start = (f32[15,8,128]{2,1,0:T(8,128)S(1)}, f32[15,8,128]{2,1,0:T(8,128)S(1)}, u32[]{:S(2)}, u32[]{:S(2)}) collective-permute-start(f32[15,8,128]{2,1,0:T(8,128)S(1)} %get-tuple-element.30), channel_id=1, source_target_pairs={{0,248},{8,16},{16,8},{24,32},{32,24},{40,48},{48,40},{56,64},{64,... | collective-permute-start | bytes 184328 | tf_op jit(solution)/shard_map/ppermute | solution.py:546
  10.7 1.6 %collective-permute-done = f32[15,8,128]{2,1,0:T(8,128)S(1)} collective-permute-done((f32[15,8,128]{2,1,0:T(8,128)S(1)}, f32[15,8,128]{2,1,0:T(8,128)S(1)}, u32[]{:S(2)}, u32[]{:S(2)}) %collective-permute-start) | collective-permute-done | bytes 61472 | tf_op jit(solution)/shard_map/ppermute | solution.py:546
  12.3 1.5 %collective-permute-done.1 = f32[15,8,128]{2,1,0:T(8,128)S(1)} collective-permute-done((f32[15,8,128]{2,1,0:T(8,128)S(1)}, f32[15,8,128]{2,1,0:T(8,128)S(1)}, u32[]{:S(2)}, u32[]{:S(2)}) %collective-permute-start.1) | collective-permute-done | bytes 61472 | tf_op jit(solution)/shard_map/ppermute | solution.py:546
  13.9 3.3 %collective-permute-start.3 = (f32[50,8,128]{2,1,0:T(8,128)S(1)}, f32[50,8,128]{2,1,0:T(8,128)S(1)}, u32[]{:S(2)}, u32[]{:S(2)}) collective-permute-start(f32[50,8,128]{2,1,0:T(8,128)S(1)} %constant_dynamic-update-slice_fusion.refs_2_), channel_id=1, source_target_pairs={{0,7},{1,2},{2,1},{3,4},{4,3},{5,6},{6,5},{7,0},{8,15},{9,10},{10,... | collective-permute-start | bytes 614408 | tf_op jit(solution)/shard_map/ppermute | solution.py:546
  17.2 3.7 %collective-permute-done.3.refs_3_ = f32[50,8,128]{2,1,0:T(8,128)S(1)} collective-permute-done((f32[50,8,128]{2,1,0:T(8,128)S(1)}, f32[50,8,128]{2,1,0:T(8,128)S(1)}, u32[]{:S(2)}, u32[]{:S(2)}) %collective-permute-start.3) | collective-permute-done | bytes 204832 | tf_op jit(solution)/shard_map/ppermute | solution.py:546
  20.9 2.0 %shard_map.56 = (f32[512,128]{1,0:T(8,128)S(1)}, f32[80,128]{1,0:T(8,128)S(1)}, f32[480,128]{1,0:T(8,128)S(1)}, f32[320,128]{1,0:T(8,128)S(1)}, f32[352,128]{1,0...) custom-call(s32[2]{0:T(128)S(1)} %pad_add_fusion.index.refs_0_, ...), custom_call_target="tpu_custom_call" | custom-call | tf_op jit(solution)/shard_map/pallas_call | solution.py:471
  22.9 21.1 %all_to_all.10 = f32[128,4,128]{2,1,0:T(4,128)S(1)} all-to-all(f32[128,4,128]{2,1,0:T(4,128)S(1)} %bitcast.10), channel_id=1, replica_groups=mesh['gz'=32,'gx'=4,'core'=2] {'gz','gx'}, dimensions={0} | all-to-all | bytes 524288 | tf_op jit(solution)/shard_map/all_to_all | solution.py:557
  43.9 3.0 %collective-permute-start.4 = (f32[512,128]{1,0:T(8,128)S(1)}, f32[512,128]{1,0:T(8,128)S(1)}, u32[]{:S(2)}, u32[]{:S(2)}) collective-permute-start(f32[512,128]{1,0:T(8,128)S(1)} %bitcast.6), channel_id=1, source_target_pairs={{0,1},{1,0},{2,3},{3,2},{4,5},{5,4},{6,7},{7,6},{8,9},{9,8},{10,11... | collective-permute-start | bytes 786440 | tf_op jit(solution)/shard_map/ppermute | solution.py:546
  46.9 0.8 collective-permute-start.5
  48.0 3.1 %shard_map.57 = (f32[48,128]{1,0:T(8,128)S(1)}, f32[6,352,128]{2,1,0:T(8,128)S(1)}, f32[6,176,128]{2,1,0:T(8,128)S(1)}, f32[6,96,128]{2,1,0:T(8,128)S(1)}) custom-call(s32[2]{0:T(128)S(1)} %pad_add_fusion.index.refs_0_, f32[512,128]{1,0:T(8,128)S(1)} %bitcast.7, f32[512,128]{1,0:T(8,128)S(1)} %collective-permute-done.4.refs_2_), custom_call_target="tpu_custom_call" | custom-call | tf_op jit(solution)/shard_map/pallas_call | solution.py:471
  51.1 1.4 %shard_map.58 = (f32[16,8,128]{2,1,0:T(8,128)S(1)}, f32[12,8,128]{2,1,0:T(8,128)S(1)}, f32[12,8,128]{2,1,0:T(8,128)S(1)}) custom-call(s32[2]{0:T(128)S(1)} %pad_add_fusion.index.refs_0_, f32[960,128]{1,0:T(8,128)S(1)} %get-tuple-element.34.refs_1_.refs_4_, f32[10,11,24,128]{3,2,1,0:T(8,128)S(1)} %get-tuple-element.35.refs_2_.refs_5_, ...), custom_call_target="tpu_custom_call" | custom-call | tf_op jit(solution)/shard_map/pallas_call | solution.py:471
  52.6 1.1 %collective-permute-start.7 = (f32[12,8,128]{2,1,0:T(8,128)S(1)}, f32[12,8,128]{2,1,0:T(8,128)S(1)}, u32[]{:S(2)}, u32[]{:S(2)}) collective-permute-start(f32[12,8,128]{2,1,0:T(8,128)S(1)} %get-tuple-element.44), channel_id=1, source_target_pairs={{0,248},{8,16},{16,8},{24,32},{32,24},{40,48},{48,40},{56,64},{64,... | collective-permute-start | bytes 147464 | tf_op jit(solution)/shard_map/ppermute | solution.py:546
  53.7 0.3 collective-permute-start.8
  54.1 4.9 %collective-permute-done.7 = f32[12,8,128]{2,1,0:T(8,128)S(1)} collective-permute-done((f32[12,8,128]{2,1,0:T(8,128)S(1)}, f32[12,8,128]{2,1,0:T(8,128)S(1)}, u32[]{:S(2)}, u32[]{:S(2)}) %collective-permute-start.7) | collective-permute-done | bytes 49184 | tf_op jit(solution)/shard_map/ppermute | solution.py:546
  59.0 1.9 %collective-permute-start.10 = (f32[40,8,128]{2,1,0:T(8,128)S(1)}, f32[40,8,128]{2,1,0:T(8,128)S(1)}, u32[]{:S(2)}, u32[]{:S(2)}) collective-permute-start(f32[40,8,128]{2,1,0:T(8,128)S(1)} %pad_maximum_fusion.refs_2_), channel_id=1, source_target_pairs={{0,7},{1,2},{2,1},{3,4},{4,3},{5,6},{6,5},{7,0},{8,15},{9,10},{10,... | collective-permute-start | bytes 491528 | tf_op jit(solution)/shard_map/ppermute | solution.py:546
  60.9 3.0 %collective-permute-done.10.refs_3_ = f32[40,8,128]{2,1,0:T(8,128)S(1)} collective-permute-done((f32[40,8,128]{2,1,0:T(8,128)S(1)}, f32[40,8,128]{2,1,0:T(8,128)S(1)}, u32[]{:S(2)}, u32[]{:S(2)}) %collective-permute-start.10) | collective-permute-done | bytes 163872 | tf_op jit(solution)/shard_map/ppermute | solution.py:546
  63.9 1.8 %shard_map.59 = (f32[256,128]{1,0:T(8,128)S(1)}, f32[80,128]{1,0:T(8,128)S(1)}, f32[480,128]{1,0:T(8,128)S(1)}, f32[320,128]{1,0:T(8,128)S(1)}, f32[352,128]{1,0:T(8,128)S(1)}) custom-call(s32[2]{0:T(128)S(1)} %pad_add_fusion.index.refs_0_, f32[40,8,128]{2,1,0:T(8,128)S(1)} %collective-permute-done.9.refs_1_, f32[40,8,128]{2,1,0:T(8,128)S(1)} %pad_maximum_fusion.refs_2_, ...), custom_call_target="tpu_custom_call" | custom-call | tf_op jit(solution)/shard_map/pallas_call | solution.py:471
  65.7 18.3 %all_to_all.11 = f32[128,2,128]{2,1,0:T(2,128)S(1)} all-to-all(f32[128,2,128]{2,1,0:T(2,128)S(1)} %bitcast.11), channel_id=1, replica_groups=mesh['gz'=32,'gx'=4,'core'=2] {'gz','gx'}, dimensions={0} | all-to-all | bytes 262144 | tf_op jit(solution)/shard_map/all_to_all | solution.py:557
  84.0 2.1 %collective-permute-start.11 = (f32[256,128]{1,0:T(8,128)S(1)}, f32[256,128]{1,0:T(8,128)S(1)}, u32[]{:S(2)}, u32[]{:S(2)}) collective-permute-start(f32[256,128]{1,0:T(8,128)S(1)} %bitcast.8), channel_id=1, source_target_pairs={{0,1},{1,0},{2,3},{3,2},{4,5},{5,4},{6,7},{7,6},{8,9},{9,8},{10,11... | collective-permute-start | bytes 393224 | tf_op jit(solution)/shard_map/ppermute | solution.py:546
  86.2 1.0 %collective-permute-start.12 = (f32[80,128]{1,0:T(8,128)S(1)}, f32[80,128]{1,0:T(8,128)S(1)}, u32[]{:S(2)}, u32[]{:S(2)}) collective-permute-start(f32[80,128]{1,0:T(8,128)S(1)} %get-tuple-element.51), channel_id=1, source_target_pairs={{0,1},{1,0},{2,3},{3,2},{4,5},{5,4},{6,7},{7,6},{8,9},{9,8},{10,11... | collective-permute-start | bytes 122888 | tf_op jit(solution)/shard_map/ppermute | solution.py:546
  87.2 2.3 %shard_map.60.refs_5_ = f32[48,128]{1,0:T(8,128)S(1)} custom-call(s32[2]{0:T(128)S(1)} %pad_add_fusion.index.refs_0_, f32[256,128]{1,0:T(8,128)S(1)} %bitcast.9, f32[256,128]{1,0:T(8,128)S(1)} %collective-permute-done.11.refs_2_, f32[6,352,128]{2,1,0:T(8,128)S(1)} %get-tuple-element.48.refs_3_, f32[6,176,128]{2,1,0:T(8,128)S(1)} %get-tuple-element.49.refs_4_, ...), custom_call_target="tpu_custom_call" | custom-call | tf_op jit(solution)/shard_map/pallas_call | solution.py:471
  89.5 0.3 collective-permute-done.13.refs_7_
  89.8 2.1 %shard_map.61 = f32[16,8,128]{2,1,0:T(8,128)} custom-call(s32[2]{0:T(128)S(1)} %pad_add_fusion.index.refs_0_, f32[960,128]{1,0:T(8,128)S(1)} %get-tuple-element.34.refs_1_.refs_4_, f32[10,11,24,128]{3,2,1,0:T(8,128)S(1)} %get-tuple-element.35.refs_2_.refs_5_, f32[11,24,128]{2,1,0:T(8,128)S(1)} %get-tuple-element.36.refs_3_.refs_6_, ...), custom_call_target="tpu_custom_call" | custom-call | tf_op jit(solution)/shard_map/pallas_call | solution.py:471
  (23 shorter events, 0.6 us)
Async XLA Ops:
  1.8 10.6 %collective-permute-start = (f32[15,8,128]{2,1,0:T(8,128)S(1)}, f32[15,8,128]{2,1,0:T(8,128)S(1)}, u32[]{:S(2)}, u32[]{:S(2)}) collective-permute-start(f32[15,8,128]{2,1,0:T(8,128)S(1)} %get-tuple-element.30), channel_id=1, source_target_pairs={{0,248},{8,16},{16,8},{24,32},{32,24},{40,48},{48,40},{56,64},{64,... | collective-permute-start | bytes 184328 | tf_op jit(solution)/shard_map/ppermute | solution.py:546
  10.7 3.1 %collective-permute-start.1 = (f32[15,8,128]{2,1,0:T(8,128)S(1)}, f32[15,8,128]{2,1,0:T(8,128)S(1)}, u32[]{:S(2)}, u32[]{:S(2)}) collective-permute-start(f32[15,8,128]{2,1,0:T(8,128)S(1)} %get-tuple-element.31), channel_id=1, source_target_pairs={{0,8},{8,0},{16,24},{24,16},{32,40},{40,32},{48,56},{56,48},{64,72... | collective-permute-start | bytes 184328 | tf_op jit(solution)/shard_map/ppermute | solution.py:546
  13.9 7.0 %collective-permute-start.3 = (f32[50,8,128]{2,1,0:T(8,128)S(1)}, f32[50,8,128]{2,1,0:T(8,128)S(1)}, u32[]{:S(2)}, u32[]{:S(2)}) collective-permute-start(f32[50,8,128]{2,1,0:T(8,128)S(1)} %constant_dynamic-update-slice_fusion.refs_2_), channel_id=1, source_target_pairs={{0,7},{1,2},{2,1},{3,4},{4,3},{5,6},{6,5},{7,0},{8,15},{9,10},{10,... | collective-permute-start | bytes 614408 | tf_op jit(solution)/shard_map/ppermute | solution.py:546
  17.2 3.7 %collective-permute-start.2 = (f32[50,8,128]{2,1,0:T(8,128)S(1)}, f32[50,8,128]{2,1,0:T(8,128)S(1)}, u32[]{:S(2)}, u32[]{:S(2)}) collective-permute-start(f32[50,8,128]{2,1,0:T(8,128)S(1)} %constant_dynamic-update-slice_fusion.refs_2_), channel_id=1, source_target_pairs={{0,1},{1,0},{2,3},{3,2},{4,5},{5,4},{6,7},{7,6},{8,9},{9,8},{10,11... | collective-permute-start | bytes 614408 | tf_op jit(solution)/shard_map/ppermute | solution.py:546
  43.9 4.1 %collective-permute-start.4 = (f32[512,128]{1,0:T(8,128)S(1)}, f32[512,128]{1,0:T(8,128)S(1)}, u32[]{:S(2)}, u32[]{:S(2)}) collective-permute-start(f32[512,128]{1,0:T(8,128)S(1)} %bitcast.6), channel_id=1, source_target_pairs={{0,1},{1,0},{2,3},{3,2},{4,5},{5,4},{6,7},{7,6},{8,9},{9,8},{10,11... | collective-permute-start | bytes 786440 | tf_op jit(solution)/shard_map/ppermute | solution.py:546
  46.9 4.2 %collective-permute-start.6 = (f32[80,128]{1,0:T(8,128)S(1)}, f32[80,128]{1,0:T(8,128)S(1)}, u32[]{:S(2)}, u32[]{:S(2)}) collective-permute-start(f32[80,128]{1,0:T(8,128)S(1)} %get-tuple-element.40), channel_id=1, source_target_pairs={{0,7},{1,2},{2,1},{3,4},{4,3},{5,6},{6,5},{7,0},{8,15},{9,10},{10,... | collective-permute-start | bytes 122888 | tf_op jit(solution)/shard_map/ppermute | solution.py:546
  46.9 4.2 %collective-permute-start.5 = (f32[80,128]{1,0:T(8,128)S(1)}, f32[80,128]{1,0:T(8,128)S(1)}, u32[]{:S(2)}, u32[]{:S(2)}) collective-permute-start(f32[80,128]{1,0:T(8,128)S(1)} %get-tuple-element.40), channel_id=1, source_target_pairs={{0,1},{1,0},{2,3},{3,2},{4,5},{5,4},{6,7},{7,6},{8,9},{9,8},{10,11... | collective-permute-start | bytes 122888 | tf_op jit(solution)/shard_map/ppermute | solution.py:546
  52.6 6.3 %collective-permute-start.7 = (f32[12,8,128]{2,1,0:T(8,128)S(1)}, f32[12,8,128]{2,1,0:T(8,128)S(1)}, u32[]{:S(2)}, u32[]{:S(2)}) collective-permute-start(f32[12,8,128]{2,1,0:T(8,128)S(1)} %get-tuple-element.44), channel_id=1, source_target_pairs={{0,248},{8,16},{16,8},{24,32},{32,24},{40,48},{48,40},{56,64},{64,... | collective-permute-start | bytes 147464 | tf_op jit(solution)/shard_map/ppermute | solution.py:546
  53.7 5.2 %collective-permute-start.8 = (f32[12,8,128]{2,1,0:T(8,128)S(1)}, f32[12,8,128]{2,1,0:T(8,128)S(1)}, u32[]{:S(2)}, u32[]{:S(2)}) collective-permute-start(f32[12,8,128]{2,1,0:T(8,128)S(1)} %get-tuple-element.45), channel_id=1, source_target_pairs={{0,8},{8,0},{16,24},{24,16},{32,40},{40,32},{48,56},{56,48},{64,72... | collective-permute-start | bytes 147464 | tf_op jit(solution)/shard_map/ppermute | solution.py:546
  59.0 4.9 %collective-permute-start.10 = (f32[40,8,128]{2,1,0:T(8,128)S(1)}, f32[40,8,128]{2,1,0:T(8,128)S(1)}, u32[]{:S(2)}, u32[]{:S(2)}) collective-permute-start(f32[40,8,128]{2,1,0:T(8,128)S(1)} %pad_maximum_fusion.refs_2_), channel_id=1, source_target_pairs={{0,7},{1,2},{2,1},{3,4},{4,3},{5,6},{6,5},{7,0},{8,15},{9,10},{10,... | collective-permute-start | bytes 491528 | tf_op jit(solution)/shard_map/ppermute | solution.py:546
  60.9 3.0 %collective-permute-start.9 = (f32[40,8,128]{2,1,0:T(8,128)S(1)}, f32[40,8,128]{2,1,0:T(8,128)S(1)}, u32[]{:S(2)}, u32[]{:S(2)}) collective-permute-start(f32[40,8,128]{2,1,0:T(8,128)S(1)} %pad_maximum_fusion.refs_2_), channel_id=1, source_target_pairs={{0,1},{1,0},{2,3},{3,2},{4,5},{5,4},{6,7},{7,6},{8,9},{9,8},{10,11... | collective-permute-start | bytes 491528 | tf_op jit(solution)/shard_map/ppermute | solution.py:546
  84.0 3.2 %collective-permute-start.11 = (f32[256,128]{1,0:T(8,128)S(1)}, f32[256,128]{1,0:T(8,128)S(1)}, u32[]{:S(2)}, u32[]{:S(2)}) collective-permute-start(f32[256,128]{1,0:T(8,128)S(1)} %bitcast.8), channel_id=1, source_target_pairs={{0,1},{1,0},{2,3},{3,2},{4,5},{5,4},{6,7},{7,6},{8,9},{9,8},{10,11... | collective-permute-start | bytes 393224 | tf_op jit(solution)/shard_map/ppermute | solution.py:546
  86.1 3.7 %collective-permute-start.13 = (f32[80,128]{1,0:T(8,128)S(1)}, f32[80,128]{1,0:T(8,128)S(1)}, u32[]{:S(2)}, u32[]{:S(2)}) collective-permute-start(f32[80,128]{1,0:T(8,128)S(1)} %get-tuple-element.51), channel_id=1, source_target_pairs={{0,7},{1,2},{2,1},{3,4},{4,3},{5,6},{6,5},{7,0},{8,15},{9,10},{10,... | collective-permute-start | bytes 122888 | tf_op jit(solution)/shard_map/ppermute | solution.py:546
  86.2 3.6 %collective-permute-start.12 = (f32[80,128]{1,0:T(8,128)S(1)}, f32[80,128]{1,0:T(8,128)S(1)}, u32[]{:S(2)}, u32[]{:S(2)}) collective-permute-start(f32[80,128]{1,0:T(8,128)S(1)} %get-tuple-element.51), channel_id=1, source_target_pairs={{0,1},{1,0},{2,3},{3,2},{4,5},{5,4},{6,7},{7,6},{8,9},{9,8},{10,11... | collective-permute-start | bytes 122888 | tf_op jit(solution)/shard_map/ppermute | solution.py:546

commit v5 on v4

--- a/solution.py
+++ b/solution.py
@@ -5,7 +5,8 @@
 from jax.experimental.pallas import tpu as pltpu
 from jax.sharding import PartitionSpec as P
 
-HALO = 12
+HALO = 10
+FIELD_HALO = 11
 WZ = 40
 BLOCKS = 10
 WY = 24
@@ -178,9 +179,10 @@
     for p in range(num_phases):
         for c in range(num_classes):
             value = jnp.where((phase == p) & (cls == c), diff[p, c], value)
-    kappa_ref[...] = value
-    mate_ref[HALO:] = jnp.where(even, value[1:], value[:3])
-    other_ref[HALO:] = jnp.where(even, value[:3], value[1:])
+    rows = jnp.concatenate([value[block, 4 * half : 4 * half + 1] for block in range(4) for half in range(2)], axis=0)
+    kappa_ref[0] = rows
+    mate_ref[HALO] = rows
+    other_ref[HALO] = rows
     for copy in copies[-3:]:
         copy.wait()
 
@@ -194,7 +196,13 @@
     kappa[0:8] = jnp.ones((8, 128), jnp.float32)
     kappa[8 + BLOCKS * WY : 16 + BLOCKS * WY] = jnp.ones((8, 128), jnp.float32)
     for block in range(BLOCKS):
-        kappa[8 + block * WY : 8 + (block + 1) * WY] = window(sources, WZ + block, even)
+        plane, number = divmod(block + 1, 4)
+        two = slice(2 * number, 2 * number + 2)
+        mate, own, other = (ref[16 + 2 * HALO + plane, two] for ref in sources)
+        rows = (jnp.where(even, other, mate), own, jnp.where(even, mate, other))
+        kappa[8 + block * WY : 8 + (block + 1) * WY] = jnp.concatenate(
+            [jnp.broadcast_to(pair[half : half + 1], (4, 128)) for pair in rows for half in range(2)], axis=0
+        )
     y = iota(WY, 0) + y_device * 8 - 8
     x = iota(WY, 1)
     for block in range(BLOCKS + 1):
@@ -289,16 +297,17 @@
     if first:
         for z in range(WZ):
             kind = (0, 1, 1, 2)[z % 4]
-            value = window(sources, z, even)
+            inside = 0 <= z + HALO - 12 < 16 + 2 * HALO
+            value = window(sources, z + HALO - 12, even) if inside else zero
             source[z * WY : (z + 1) * WY] = value
             va[(z + 1) * WY : (z + 2) * WY] = coefs[z // 4, 5 + kind] * value
     else:
-        for z in range(WZ):
-            vb[(z + 1) * WY : (z + 2) * WY] = window(fields, z, even)
-        for z in range(WZ):
+        for z in range(1, WZ - 1):
+            vb[(z + 1) * WY : (z + 2) * WY] = window(fields, z - 1, even)
+        for z in range(2, WZ - 2):
             here, total, weight, _ = fine_plane(vb, source, coefs, z_faces, z)
             va[(z + 1) * WY : (z + 2) * WY] = 0.2 * here + weight * total
-    for z in range(2, WZ - 2):
+    for z in range(3, WZ - 3):
         here, total, weight, _ = fine_plane(va, source, coefs, z_faces, z)
         value = 0.2 * here + weight * total
         vb[(z + 1) * WY : (z + 2) * WY] = value
@@ -422,7 +431,13 @@
 def up_body(last, *refs):
     index, source, coefs, z_faces, faces, near, edge_mate, edge_other, kept, source_one, kept_one, out = refs[:12]
     refs = refs[12:]
-    if not last:
+    if last:
+        out_hbm, (out, sems), refs = out, refs[-2:], refs[:-2]
+        halves = (slice(0, 8), slice(8, 16))
+        copies = [
+            pltpu.make_async_copy(out.at[half], out_hbm.at[half], sems.at[i]) for i, half in enumerate(halves)
+        ]
+    else:
         (mate, other), refs = refs[:2], refs[2:]
     va, vb, spread, oa, ob = refs
     even_z, even = parities(index)
@@ -456,23 +471,27 @@
     for z in range(12, 28):
         here, total, weight, _ = fine_plane(vb, source, coefs, z_faces, z, 8, 8)
         out[z - 12] = 0.2 * here + weight * total
-    if not last:
-        top = 16 - HALO
-        mate[...] = out[pl.ds(jnp.where(even_z, top, 0), HALO)]
-        other[...] = out[pl.ds(jnp.where(even_z, 0, top), HALO)]
+        if last and z in (19, 27):
+            copies[z // 27].start()
+    if last:
+        for copy in copies:
+            copy.wait()
+    else:
+        top = 16 - FIELD_HALO
+        mate[...] = out[pl.ds(jnp.where(even_z, top, 0), FIELD_HALO)]
+        other[...] = out[pl.ds(jnp.where(even_z, 0, top), FIELD_HALO)]
 
 
 def floats(*shape):
     return jax.ShapeDtypeStruct(shape, jnp.float32)
 
 
-def call(body, outs, scratch, args, inputs=pltpu.VMEM):
-    vmem = pl.BlockSpec(memory_space=pltpu.VMEM)
+def call(body, outs, scratch, args, inputs=pltpu.VMEM, outputs=pltpu.VMEM):
     return pl.pallas_call(
         body,
         out_shape=outs,
         in_specs=[pl.BlockSpec(memory_space=pltpu.SMEM)] + [pl.BlockSpec(memory_space=inputs)] * (len(args) - 1),
-        out_specs=[vmem] * len(outs),
+        out_specs=[pl.BlockSpec(memory_space=outputs)] * len(outs),
         scratch_shapes=[pltpu.VMEM(s, jnp.float32) if isinstance(s, tuple) else s for s in scratch],
         compiler_params=pltpu.CompilerParams(vmem_limit_bytes=VMEM_BYTES),
     )(*args)
@@ -524,10 +543,13 @@
 
 
 def up(index, shared, near, edges, kept, last):
-    outs = [floats(16, 8, 128)] + ([] if last else [floats(HALO, 8, 128)] * 2)
+    outs = [floats(16, 8, 128)] + ([] if last else [floats(FIELD_HALO, 8, 128)] * 2)
     scratch = [FIELD, FIELD, (320, 128), (352, 128), (352, 128)]
+    if last:
+        scratch += [(16, 8, 128), pltpu.SemaphoreType.DMA((2,))]
+    args = [index, *shared, near, *edges, *kept]
     return call(
-        lambda *refs: up_body(last, *refs), outs, scratch, [index, *shared, near, *edges, *kept]
+        lambda *refs: up_body(last, *refs), outs, scratch, args, outputs=pltpu.HBM if last else pltpu.VMEM
     )
 
 
@@ -559,13 +581,13 @@
     return out, swap(out, Y_AXIS, mate_of)
 
 
-def stack(index, parts, own):
+def stack(index, parts, own, halo):
     even = index[0] % 2 == 0
     mate, other = parts
     before, after = jnp.where(even, other, mate), jnp.where(even, mate, other)
-    pieces = [before[:HALO], own[0], after[:HALO]]
+    pieces = [before[:halo], own[0], after[:halo]]
     if len(own) > 1:
-        pieces += [before[HALO:], own[1], after[HALO:]]
+        pieces += [before[halo:], own[1], after[halo:]]
     return jnp.concatenate(pieces, axis=0)
 
 
@@ -581,10 +603,10 @@
     y_device = lax.axis_index("gx") * lax.axis_size("core") + lax.axis_index("core")
     index = jnp.stack([lax.axis_index("gz"), y_device]).astype(jnp.int32)
     plane = (4,) + phases.shape[1:]
-    part = floats(HALO + 3, 8, 128)
+    part = floats(HALO + 1, 8, 128)
     kappa, block, *parts = call(
         kappa_body,
-        [floats(*plane), floats(*phases.shape), part, part],
+        [floats(1, 8, 128), floats(*phases.shape), part, part],
         [
             pltpu.SMEM(grain_class.shape, jnp.int32),
             pltpu.SMEM(diffusivity.shape, jnp.float32),
@@ -598,11 +620,11 @@
         ],
         pltpu.HBM,
     )
-    own = stack(index, swaps(*parts, Z_AXIS), (block, kappa))
+    own = stack(index, swaps(*parts, Z_AXIS), (block, kappa), HALO)
     mate, other = swaps(own, own, Y_AXIS)
     (field, *parts), shared, faces = cycle(index, (mate, own, other), None, None, False)
 
-    own = stack(index, swaps(*parts, Z_AXIS), (field,))
+    own = stack(index, swaps(*parts, Z_AXIS), (field,), FIELD_HALO)
     mate, other = swaps(own, own, Y_AXIS)
     return cycle(index, (mate, own, other), shared, faces, True)[0][0]
 

time: 92.1 us -> 91.6 us (level)
  no operation moved by 1% of the time
where the time goes in v5:
time: 91.6 us; the launch traced here: 91.4 us
  blocking collectives  39.4 us (43%)
  starting transfers between devices  22.6 us (25%)
  waiting for transfers between devices  14.5 us (16%)
  Pallas kernels  14.4 us (16%)
    all_to_all x2, blocking collectives, to_all(): out = lax.all_to_all(copies, ('gz', 'gx'), 0, 0)  39.4 us
    ppermute x14, starting transfers between devices, swap(): lax.ppermute(array, axis, [(i, partner(i) % count) for i in range(count)])  22.6 us
    ppermute x14, waiting for transfers between devices, swap(): lax.ppermute(array, axis, [(i, partner(i) % count) for i in range(count)])  14.5 us
    pallas_call x7, Pallas kernels, call(): pl.pallas_call(body, out_shape=outs, in_specs=[pl.BlockSpec(memory_space=...  14.4 us
  transfers between devices with their start and end apart: 14, of which 7 were waited for; matrix products, arithmetic and copies ran while one was open for 0% of the time, Pallas kernels for 6%

profile of v5, /device:TPU:1, one launch (start us, length us, event | category | flops | bytes accessed | tf_op | source)
XLA Modules:
  0.0 91.4 jit_solution(15234283692598235009)
XLA Ops:
  0.1 1.7 %shard_map.55 = (f32[1,8,128]{2,1,0:T(8,128)S(1)}, f32[16,8,128]{2,1,0:T(8,128)S(1)}, f32[11,8,128]{2,1,0:T(8,128)S(1)}, f32[11,8,128]{2,1,0:T(8,128)S(1)}) custom-call(s32[2]{0:T(128)S(1)} %pad_add_fusion.index.refs_0_, s32[64]{0:T(128)} %class_hbm.1, f32[3,4]{1,0:T(4,128)} %diff_hbm.1, s32[16,8,128]{2,1,0:T(8,128)} %phases_hbm.1, ...), custom_call_target="tpu_custom_call" | custom-call | tf_op jit(solution)/shard_map/pallas_call | solution.py:490
  1.7 8.9 %collective-permute-start = (f32[11,8,128]{2,1,0:T(8,128)S(1)}, f32[11,8,128]{2,1,0:T(8,128)S(1)}, u32[]{:S(2)}, u32[]{:S(2)}) collective-permute-start(f32[11,8,128]{2,1,0:T(8,128)S(1)} %get-tuple-element.30), channel_id=1, source_target_pairs={{0,248},{8,16},{16,8},{24,32},{32,24},{40,48},{48,40},{56,64},{64,... | collective-permute-start | bytes 135176 | tf_op jit(solution)/shard_map/ppermute | solution.py:568
  10.7 1.4 %collective-permute-done = f32[11,8,128]{2,1,0:T(8,128)S(1)} collective-permute-done((f32[11,8,128]{2,1,0:T(8,128)S(1)}, f32[11,8,128]{2,1,0:T(8,128)S(1)}, u32[]{:S(2)}, u32[]{:S(2)}) %collective-permute-start) | collective-permute-done | bytes 45088 | tf_op jit(solution)/shard_map/ppermute | solution.py:568
  12.1 1.5 %collective-permute-done.1 = f32[11,8,128]{2,1,0:T(8,128)S(1)} collective-permute-done((f32[11,8,128]{2,1,0:T(8,128)S(1)}, f32[11,8,128]{2,1,0:T(8,128)S(1)}, u32[]{:S(2)}, u32[]{:S(2)}) %collective-permute-start.1) | collective-permute-done | bytes 45088 | tf_op jit(solution)/shard_map/ppermute | solution.py:568
  13.7 3.3 %collective-permute-start.3 = (f32[39,8,128]{2,1,0:T(8,128)S(1)}, f32[39,8,128]{2,1,0:T(8,128)S(1)}, u32[]{:S(2)}, u32[]{:S(2)}) collective-permute-start(f32[39,8,128]{2,1,0:T(8,128)S(1)} %constant_dynamic-update-slice_fusion.refs_2_), channel_id=1, source_target_pairs={{0,7},{1,2},{2,1},{3,4},{4,3},{5,6},{6,5},{7,0},{8,15},{9,10},{10,... | collective-permute-start | bytes 479240 | tf_op jit(solution)/shard_map/ppermute | solution.py:568
  17.0 3.3 %collective-permute-done.3.refs_3_ = f32[39,8,128]{2,1,0:T(8,128)S(1)} collective-permute-done((f32[39,8,128]{2,1,0:T(8,128)S(1)}, f32[39,8,128]{2,1,0:T(8,128)S(1)}, u32[]{:S(2)}, u32[]{:S(2)}) %collective-permute-start.3) | collective-permute-done | bytes 159776 | tf_op jit(solution)/shard_map/ppermute | solution.py:568
  20.2 2.0 %shard_map.56 = (f32[512,128]{1,0:T(8,128)S(1)}, f32[80,128]{1,0:T(8,128)S(1)}, f32[480,128]{1,0:T(8,128)S(1)}, f32[320,128]{1,0:T(8,128)S(1)}, f32[352,128]{1,0...) custom-call(s32[2]{0:T(128)S(1)} %pad_add_fusion.index.refs_0_, ...), custom_call_target="tpu_custom_call" | custom-call | tf_op jit(solution)/shard_map/pallas_call | solution.py:490
  22.2 21.1 %all_to_all.10 = f32[128,4,128]{2,1,0:T(4,128)S(1)} all-to-all(f32[128,4,128]{2,1,0:T(4,128)S(1)} %bitcast.10), channel_id=1, replica_groups=mesh['gz'=32,'gx'=4,'core'=2] {'gz','gx'}, dimensions={0} | all-to-all | bytes 524288 | tf_op jit(solution)/shard_map/all_to_all | solution.py:579
  43.3 3.0 %collective-permute-start.4 = (f32[512,128]{1,0:T(8,128)S(1)}, f32[512,128]{1,0:T(8,128)S(1)}, u32[]{:S(2)}, u32[]{:S(2)}) collective-permute-start(f32[512,128]{1,0:T(8,128)S(1)} %bitcast.6), channel_id=1, source_target_pairs={{0,1},{1,0},{2,3},{3,2},{4,5},{5,4},{6,7},{7,6},{8,9},{9,8},{10,11... | collective-permute-start | bytes 786440 | tf_op jit(solution)/shard_map/ppermute | solution.py:568
  46.3 0.8 collective-permute-start.5
  47.4 3.0 %shard_map.57 = (f32[48,128]{1,0:T(8,128)S(1)}, f32[6,352,128]{2,1,0:T(8,128)S(1)}, f32[6,176,128]{2,1,0:T(8,128)S(1)}, f32[6,96,128]{2,1,0:T(8,128)S(1)}) custom-call(s32[2]{0:T(128)S(1)} %pad_add_fusion.index.refs_0_, f32[512,128]{1,0:T(8,128)S(1)} %bitcast.7, f32[512,128]{1,0:T(8,128)S(1)} %collective-permute-done.4.refs_2_), custom_call_target="tpu_custom_call" | custom-call | tf_op jit(solution)/shard_map/pallas_call | solution.py:490
  50.5 1.5 %shard_map.58 = (f32[16,8,128]{2,1,0:T(8,128)S(1)}, f32[11,8,128]{2,1,0:T(8,128)S(1)}, f32[11,8,128]{2,1,0:T(8,128)S(1)}) custom-call(s32[2]{0:T(128)S(1)} %pad_add_fusion.index.refs_0_, f32[960,128]{1,0:T(8,128)S(1)} %get-tuple-element.34.refs_1_.refs_4_, f32[10,11,24,128]{3,2,1,0:T(8,128)S(1)} %get-tuple-element.35.refs_2_.refs_5_, ...), custom_call_target="tpu_custom_call" | custom-call | tf_op jit(solution)/shard_map/pallas_call | solution.py:490
  51.9 1.1 %collective-permute-start.7 = (f32[11,8,128]{2,1,0:T(8,128)S(1)}, f32[11,8,128]{2,1,0:T(8,128)S(1)}, u32[]{:S(2)}, u32[]{:S(2)}) collective-permute-start(f32[11,8,128]{2,1,0:T(8,128)S(1)} %get-tuple-element.44), channel_id=1, source_target_pairs={{0,248},{8,16},{16,8},{24,32},{32,24},{40,48},{48,40},{56,64},{64,... | collective-permute-start | bytes 135176 | tf_op jit(solution)/shard_map/ppermute | solution.py:568
  53.1 0.3 collective-permute-start.8
  53.4 4.8 %collective-permute-done.7 = f32[11,8,128]{2,1,0:T(8,128)S(1)} collective-permute-done((f32[11,8,128]{2,1,0:T(8,128)S(1)}, f32[11,8,128]{2,1,0:T(8,128)S(1)}, u32[]{:S(2)}, u32[]{:S(2)}) %collective-permute-start.7) | collective-permute-done | bytes 45088 | tf_op jit(solution)/shard_map/ppermute | solution.py:568
  58.3 1.8 %collective-permute-start.10 = (f32[38,8,128]{2,1,0:T(8,128)S(1)}, f32[38,8,128]{2,1,0:T(8,128)S(1)}, u32[]{:S(2)}, u32[]{:S(2)}) collective-permute-start(f32[38,8,128]{2,1,0:T(8,128)S(1)} %pad_maximum_fusion.refs_2_), channel_id=1, source_target_pairs={{0,7},{1,2},{2,1},{3,4},{4,3},{5,6},{6,5},{7,0},{8,15},{9,10},{10,... | collective-permute-start | bytes 466952 | tf_op jit(solution)/shard_map/ppermute | solution.py:568
  60.2 2.8 %collective-permute-done.10.refs_3_ = f32[38,8,128]{2,1,0:T(8,128)S(1)} collective-permute-done((f32[38,8,128]{2,1,0:T(8,128)S(1)}, f32[38,8,128]{2,1,0:T(8,128)S(1)}, u32[]{:S(2)}, u32[]{:S(2)}) %collective-permute-start.10) | collective-permute-done | bytes 155680 | tf_op jit(solution)/shard_map/ppermute | solution.py:568
  63.0 1.9 %shard_map.59 = (f32[256,128]{1,0:T(8,128)S(1)}, f32[80,128]{1,0:T(8,128)S(1)}, f32[480,128]{1,0:T(8,128)S(1)}, f32[320,128]{1,0:T(8,128)S(1)}, f32[352,128]{1,0:T(8,128)S(1)}) custom-call(s32[2]{0:T(128)S(1)} %pad_add_fusion.index.refs_0_, f32[38,8,128]{2,1,0:T(8,128)S(1)} %collective-permute-done.9.refs_1_, f32[38,8,128]{2,1,0:T(8,128)S(1)} %pad_maximum_fusion.refs_2_, ...), custom_call_target="tpu_custom_call" | custom-call | tf_op jit(solution)/shard_map/pallas_call | solution.py:490
  64.9 18.4 %all_to_all.11 = f32[128,2,128]{2,1,0:T(2,128)S(1)} all-to-all(f32[128,2,128]{2,1,0:T(2,128)S(1)} %bitcast.11), channel_id=1, replica_groups=mesh['gz'=32,'gx'=4,'core'=2] {'gz','gx'}, dimensions={0} | all-to-all | bytes 262144 | tf_op jit(solution)/shard_map/all_to_all | solution.py:579
  83.3 2.1 %collective-permute-start.11 = (f32[256,128]{1,0:T(8,128)S(1)}, f32[256,128]{1,0:T(8,128)S(1)}, u32[]{:S(2)}, u32[]{:S(2)}) collective-permute-start(f32[256,128]{1,0:T(8,128)S(1)} %bitcast.8), channel_id=1, source_target_pairs={{0,1},{1,0},{2,3},{3,2},{4,5},{5,4},{6,7},{7,6},{8,9},{9,8},{10,11... | collective-permute-start | bytes 393224 | tf_op jit(solution)/shard_map/ppermute | solution.py:568
  85.5 1.0 %collective-permute-start.12 = (f32[80,128]{1,0:T(8,128)S(1)}, f32[80,128]{1,0:T(8,128)S(1)}, u32[]{:S(2)}, u32[]{:S(2)}) collective-permute-start(f32[80,128]{1,0:T(8,128)S(1)} %get-tuple-element.51), channel_id=1, source_target_pairs={{0,1},{1,0},{2,3},{3,2},{4,5},{5,4},{6,7},{7,6},{8,9},{9,8},{10,11... | collective-permute-start | bytes 122888 | tf_op jit(solution)/shard_map/ppermute | solution.py:568
  86.5 2.3 %shard_map.60.refs_5_ = f32[48,128]{1,0:T(8,128)S(1)} custom-call(s32[2]{0:T(128)S(1)} %pad_add_fusion.index.refs_0_, f32[256,128]{1,0:T(8,128)S(1)} %bitcast.9, f32[256,128]{1,0:T(8,128)S(1)} %collective-permute-done.11.refs_2_, f32[6,352,128]{2,1,0:T(8,128)S(1)} %get-tuple-element.48.refs_3_, f32[6,176,128]{2,1,0:T(8,128)S(1)} %get-tuple-element.49.refs_4_, ...), custom_call_target="tpu_custom_call" | custom-call | tf_op jit(solution)/shard_map/pallas_call | solution.py:490
  88.8 0.3 collective-permute-done.13.refs_7_
  89.1 2.1 %shard_map.61 = f32[16,8,128]{2,1,0:T(8,128)} custom-call(s32[2]{0:T(128)S(1)} %pad_add_fusion.index.refs_0_, f32[960,128]{1,0:T(8,128)S(1)} %get-tuple-element.34.refs_1_.refs_4_, f32[10,11,24,128]{3,2,1,0:T(8,128)S(1)} %get-tuple-element.35.refs_2_.refs_5_, f32[11,24,128]{2,1,0:T(8,128)S(1)} %get-tuple-element.36.refs_3_.refs_6_, ...), custom_call_target="tpu_custom_call" | custom-call | tf_op jit(solution)/shard_map/pallas_call | solution.py:490
  (23 shorter events, 0.7 us)
Async XLA Ops:
  1.7 10.4 %collective-permute-start = (f32[11,8,128]{2,1,0:T(8,128)S(1)}, f32[11,8,128]{2,1,0:T(8,128)S(1)}, u32[]{:S(2)}, u32[]{:S(2)}) collective-permute-start(f32[11,8,128]{2,1,0:T(8,128)S(1)} %get-tuple-element.30), channel_id=1, source_target_pairs={{0,248},{8,16},{16,8},{24,32},{32,24},{40,48},{48,40},{56,64},{64,... | collective-permute-start | bytes 135176 | tf_op jit(solution)/shard_map/ppermute | solution.py:568
  10.7 2.9 %collective-permute-start.1 = (f32[11,8,128]{2,1,0:T(8,128)S(1)}, f32[11,8,128]{2,1,0:T(8,128)S(1)}, u32[]{:S(2)}, u32[]{:S(2)}) collective-permute-start(f32[11,8,128]{2,1,0:T(8,128)S(1)} %get-tuple-element.31), channel_id=1, source_target_pairs={{0,8},{8,0},{16,24},{24,16},{32,40},{40,32},{48,56},{56,48},{64,72... | collective-permute-start | bytes 135176 | tf_op jit(solution)/shard_map/ppermute | solution.py:568
  13.7 6.5 %collective-permute-start.3 = (f32[39,8,128]{2,1,0:T(8,128)S(1)}, f32[39,8,128]{2,1,0:T(8,128)S(1)}, u32[]{:S(2)}, u32[]{:S(2)}) collective-permute-start(f32[39,8,128]{2,1,0:T(8,128)S(1)} %constant_dynamic-update-slice_fusion.refs_2_), channel_id=1, source_target_pairs={{0,7},{1,2},{2,1},{3,4},{4,3},{5,6},{6,5},{7,0},{8,15},{9,10},{10,... | collective-permute-start | bytes 479240 | tf_op jit(solution)/shard_map/ppermute | solution.py:568
  17.0 3.3 %collective-permute-start.2 = (f32[39,8,128]{2,1,0:T(8,128)S(1)}, f32[39,8,128]{2,1,0:T(8,128)S(1)}, u32[]{:S(2)}, u32[]{:S(2)}) collective-permute-start(f32[39,8,128]{2,1,0:T(8,128)S(1)} %constant_dynamic-update-slice_fusion.refs_2_), channel_id=1, source_target_pairs={{0,1},{1,0},{2,3},{3,2},{4,5},{5,4},{6,7},{7,6},{8,9},{9,8},{10,11... | collective-permute-start | bytes 479240 | tf_op jit(solution)/shard_map/ppermute | solution.py:568
  43.3 4.1 %collective-permute-start.4 = (f32[512,128]{1,0:T(8,128)S(1)}, f32[512,128]{1,0:T(8,128)S(1)}, u32[]{:S(2)}, u32[]{:S(2)}) collective-permute-start(f32[512,128]{1,0:T(8,128)S(1)} %bitcast.6), channel_id=1, source_target_pairs={{0,1},{1,0},{2,3},{3,2},{4,5},{5,4},{6,7},{7,6},{8,9},{9,8},{10,11... | collective-permute-start | bytes 786440 | tf_op jit(solution)/shard_map/ppermute | solution.py:568
  46.2 4.2 %collective-permute-start.6 = (f32[80,128]{1,0:T(8,128)S(1)}, f32[80,128]{1,0:T(8,128)S(1)}, u32[]{:S(2)}, u32[]{:S(2)}) collective-permute-start(f32[80,128]{1,0:T(8,128)S(1)} %get-tuple-element.40), channel_id=1, source_target_pairs={{0,7},{1,2},{2,1},{3,4},{4,3},{5,6},{6,5},{7,0},{8,15},{9,10},{10,... | collective-permute-start | bytes 122888 | tf_op jit(solution)/shard_map/ppermute | solution.py:568
  46.3 4.2 %collective-permute-start.5 = (f32[80,128]{1,0:T(8,128)S(1)}, f32[80,128]{1,0:T(8,128)S(1)}, u32[]{:S(2)}, u32[]{:S(2)}) collective-permute-start(f32[80,128]{1,0:T(8,128)S(1)} %get-tuple-element.40), channel_id=1, source_target_pairs={{0,1},{1,0},{2,3},{3,2},{4,5},{5,4},{6,7},{7,6},{8,9},{9,8},{10,11... | collective-permute-start | bytes 122888 | tf_op jit(solution)/shard_map/ppermute | solution.py:568
  51.9 6.3 %collective-permute-start.7 = (f32[11,8,128]{2,1,0:T(8,128)S(1)}, f32[11,8,128]{2,1,0:T(8,128)S(1)}, u32[]{:S(2)}, u32[]{:S(2)}) collective-permute-start(f32[11,8,128]{2,1,0:T(8,128)S(1)} %get-tuple-element.44), channel_id=1, source_target_pairs={{0,248},{8,16},{16,8},{24,32},{32,24},{40,48},{48,40},{56,64},{64,... | collective-permute-start | bytes 135176 | tf_op jit(solution)/shard_map/ppermute | solution.py:568
  53.1 5.2 %collective-permute-start.8 = (f32[11,8,128]{2,1,0:T(8,128)S(1)}, f32[11,8,128]{2,1,0:T(8,128)S(1)}, u32[]{:S(2)}, u32[]{:S(2)}) collective-permute-start(f32[11,8,128]{2,1,0:T(8,128)S(1)} %get-tuple-element.45), channel_id=1, source_target_pairs={{0,8},{8,0},{16,24},{24,16},{32,40},{40,32},{48,56},{56,48},{64,72... | collective-permute-start | bytes 135176 | tf_op jit(solution)/shard_map/ppermute | solution.py:568
  58.3 4.8 %collective-permute-start.10 = (f32[38,8,128]{2,1,0:T(8,128)S(1)}, f32[38,8,128]{2,1,0:T(8,128)S(1)}, u32[]{:S(2)}, u32[]{:S(2)}) collective-permute-start(f32[38,8,128]{2,1,0:T(8,128)S(1)} %pad_maximum_fusion.refs_2_), channel_id=1, source_target_pairs={{0,7},{1,2},{2,1},{3,4},{4,3},{5,6},{6,5},{7,0},{8,15},{9,10},{10,... | collective-permute-start | bytes 466952 | tf_op jit(solution)/shard_map/ppermute | solution.py:568
  60.1 2.9 %collective-permute-start.9 = (f32[38,8,128]{2,1,0:T(8,128)S(1)}, f32[38,8,128]{2,1,0:T(8,128)S(1)}, u32[]{:S(2)}, u32[]{:S(2)}) collective-permute-start(f32[38,8,128]{2,1,0:T(8,128)S(1)} %pad_maximum_fusion.refs_2_), channel_id=1, source_target_pairs={{0,1},{1,0},{2,3},{3,2},{4,5},{5,4},{6,7},{7,6},{8,9},{9,8},{10,11... | collective-permute-start | bytes 466952 | tf_op jit(solution)/shard_map/ppermute | solution.py:568
  83.3 3.2 %collective-permute-start.11 = (f32[256,128]{1,0:T(8,128)S(1)}, f32[256,128]{1,0:T(8,128)S(1)}, u32[]{:S(2)}, u32[]{:S(2)}) collective-permute-start(f32[256,128]{1,0:T(8,128)S(1)} %bitcast.8), channel_id=1, source_target_pairs={{0,1},{1,0},{2,3},{3,2},{4,5},{5,4},{6,7},{7,6},{8,9},{9,8},{10,11... | collective-permute-start | bytes 393224 | tf_op jit(solution)/shard_map/ppermute | solution.py:568
  85.4 3.7 %collective-permute-start.13 = (f32[80,128]{1,0:T(8,128)S(1)}, f32[80,128]{1,0:T(8,128)S(1)}, u32[]{:S(2)}, u32[]{:S(2)}) collective-permute-start(f32[80,128]{1,0:T(8,128)S(1)} %get-tuple-element.51), channel_id=1, source_target_pairs={{0,7},{1,2},{2,1},{3,4},{4,3},{5,6},{6,5},{7,0},{8,15},{9,10},{10,... | collective-permute-start | bytes 122888 | tf_op jit(solution)/shard_map/ppermute | solution.py:568
  85.5 3.6 %collective-permute-start.12 = (f32[80,128]{1,0:T(8,128)S(1)}, f32[80,128]{1,0:T(8,128)S(1)}, u32[]{:S(2)}, u32[]{:S(2)}) collective-permute-start(f32[80,128]{1,0:T(8,128)S(1)} %get-tuple-element.51), channel_id=1, source_target_pairs={{0,1},{1,0},{2,3},{3,2},{4,5},{5,4},{6,7},{7,6},{8,9},{9,8},{10,11... | collective-permute-start | bytes 122888 | tf_op jit(solution)/shard_map/ppermute | solution.py:568

commit v6 on v5

--- a/solution.py
+++ b/solution.py
@@ -565,7 +565,10 @@
     count = 1
     for name in axis:
         count *= lax.axis_size(name)
-    return lax.ppermute(array, axis, [(i, partner(i) % count) for i in range(count)])
+    pairs = [(i, partner(i)) for i in range(count)]
+    if axis == Y_AXIS:
+        pairs = [(i, j if 0 <= j < count else i) for i, j in pairs]
+    return lax.ppermute(array, axis, [(i, j % count) for i, j in pairs])
 
 
 def swaps(mate, other, axis):

time: 91.6 us -> 98.1 us (1.071)
  starting transfers between devices: 22.6 us -> 29.5 us
    ppermute x14, starting transfers between devices: 22.6 us -> 29.5 us  [swap(): return lax.ppermute(array, axis, [(i, j % count) for i, j in pairs])]
  transfers between devices with their start and end apart: 14 -> 14, of which waited for: 7 -> 7; matrix products, arithmetic and copies ran while one was open for 0% -> 0% of each run, Pallas kernels for 6% -> 5%
where the time goes in v6:
time: 98.1 us; the launch traced here: 97.8 us
  blocking collectives  38.8 us (40%)
  starting transfers between devices  29.5 us (30%)
  waiting for transfers between devices  14.7 us (15%)
  Pallas kernels  14.4 us (15%)
    all_to_all x2, blocking collectives, to_all(): out = lax.all_to_all(copies, ('gz', 'gx'), 0, 0)  38.8 us
    ppermute x14, starting transfers between devices, swap(): return lax.ppermute(array, axis, [(i, j % count) for i, j in pairs])  29.5 us
    ppermute x14, waiting for transfers between devices, swap(): return lax.ppermute(array, axis, [(i, j % count) for i, j in pairs])  14.7 us
    pallas_call x7, Pallas kernels, call(): pl.pallas_call(body, out_shape=outs, in_specs=[pl.BlockSpec(memory_space=...  14.4 us
  transfers between devices with their start and end apart: 14, of which 7 were waited for; matrix products, arithmetic and copies ran while one was open for 0% of the time, Pallas kernels for 5%

profile of v6, /device:TPU:1, one launch (start us, length us, event | category | flops | bytes accessed | tf_op | source)
XLA Modules:
  0.0 97.8 jit_solution(1337371316740172287)
XLA Ops:
  0.1 1.7 %shard_map.55 = (f32[1,8,128]{2,1,0:T(8,128)S(1)}, f32[16,8,128]{2,1,0:T(8,128)S(1)}, f32[11,8,128]{2,1,0:T(8,128)S(1)}, f32[11,8,128]{2,1,0:T(8,128)S(1)}) custom-call(s32[2]{0:T(128)S(1)} %pad_add_fusion.index.refs_0_, s32[64]{0:T(128)} %class_hbm.1, f32[3,4]{1,0:T(4,128)} %diff_hbm.1, s32[16,8,128]{2,1,0:T(8,128)} %phases_hbm.1, ...), custom_call_target="tpu_custom_call" | custom-call | tf_op jit(solution)/shard_map/pallas_call | solution.py:490
  1.7 8.9 %collective-permute-start = (f32[11,8,128]{2,1,0:T(8,128)S(1)}, f32[11,8,128]{2,1,0:T(8,128)S(1)}, u32[]{:S(2)}, u32[]{:S(2)}) collective-permute-start(f32[11,8,128]{2,1,0:T(8,128)S(1)} %get-tuple-element.30), channel_id=1, source_target_pairs={{0,248},{8,16},{16,8},{24,32},{32,24},{40,48},{48,40},{56,64},{64,... | collective-permute-start | bytes 135176 | tf_op jit(solution)/shard_map/ppermute | solution.py:571
  10.7 1.4 %collective-permute-done = f32[11,8,128]{2,1,0:T(8,128)S(1)} collective-permute-done((f32[11,8,128]{2,1,0:T(8,128)S(1)}, f32[11,8,128]{2,1,0:T(8,128)S(1)}, u32[]{:S(2)}, u32[]{:S(2)}) %collective-permute-start) | collective-permute-done | bytes 45088 | tf_op jit(solution)/shard_map/ppermute | solution.py:571
  12.1 1.5 %collective-permute-done.1 = f32[11,8,128]{2,1,0:T(8,128)S(1)} collective-permute-done((f32[11,8,128]{2,1,0:T(8,128)S(1)}, f32[11,8,128]{2,1,0:T(8,128)S(1)}, u32[]{:S(2)}, u32[]{:S(2)}) %collective-permute-start.1) | collective-permute-done | bytes 45088 | tf_op jit(solution)/shard_map/ppermute | solution.py:571
  13.7 5.1 %collective-permute-start.3 = (f32[39,8,128]{2,1,0:T(8,128)S(1)}, f32[39,8,128]{2,1,0:T(8,128)S(1)}, u32[]{:S(2)}, u32[]{:S(2)}) collective-permute-start(f32[39,8,128]{2,1,0:T(8,128)S(1)} %constant_dynamic-update-slice_fusion.refs_2_), channel_id=1, source_target_pairs={{0,0},{1,2},{2,1},{3,4},{4,3},{5,6},{6,5},{7,7},{8,8},{9,10},{10,9... | collective-permute-start | bytes 479240 | tf_op jit(solution)/shard_map/ppermute | solution.py:571
  18.9 2.8 %collective-permute-done.3.refs_3_ = f32[39,8,128]{2,1,0:T(8,128)S(1)} collective-permute-done((f32[39,8,128]{2,1,0:T(8,128)S(1)}, f32[39,8,128]{2,1,0:T(8,128)S(1)}, u32[]{:S(2)}, u32[]{:S(2)}) %collective-permute-start.3) | collective-permute-done | bytes 159776 | tf_op jit(solution)/shard_map/ppermute | solution.py:571
  21.7 2.0 %shard_map.56 = (f32[512,128]{1,0:T(8,128)S(1)}, f32[80,128]{1,0:T(8,128)S(1)}, f32[480,128]{1,0:T(8,128)S(1)}, f32[320,128]{1,0:T(8,128)S(1)}, f32[352,128]{1,0...) custom-call(s32[2]{0:T(128)S(1)} %pad_add_fusion.index.refs_0_, ...), custom_call_target="tpu_custom_call" | custom-call | tf_op jit(solution)/shard_map/pallas_call | solution.py:490
  23.7 21.4 %all_to_all.10 = f32[128,4,128]{2,1,0:T(4,128)S(1)} all-to-all(f32[128,4,128]{2,1,0:T(4,128)S(1)} %bitcast.10), channel_id=1, replica_groups=mesh['gz'=32,'gx'=4,'core'=2] {'gz','gx'}, dimensions={0} | all-to-all | bytes 524288 | tf_op jit(solution)/shard_map/all_to_all | solution.py:582
  45.1 2.9 %collective-permute-start.4 = (f32[512,128]{1,0:T(8,128)S(1)}, f32[512,128]{1,0:T(8,128)S(1)}, u32[]{:S(2)}, u32[]{:S(2)}) collective-permute-start(f32[512,128]{1,0:T(8,128)S(1)} %bitcast.6), channel_id=1, source_target_pairs={{0,1},{1,0},{2,3},{3,2},{4,5},{5,4},{6,7},{7,6},{8,9},{9,8},{10,11... | collective-permute-start | bytes 786440 | tf_op jit(solution)/shard_map/ppermute | solution.py:571
  48.1 1.9 %collective-permute-start.6 = (f32[80,128]{1,0:T(8,128)S(1)}, f32[80,128]{1,0:T(8,128)S(1)}, u32[]{:S(2)}, u32[]{:S(2)}) collective-permute-start(f32[80,128]{1,0:T(8,128)S(1)} %get-tuple-element.40), channel_id=1, source_target_pairs={{0,0},{1,2},{2,1},{3,4},{4,3},{5,6},{6,5},{7,7},{8,8},{9,10},{10,9... | collective-permute-start | bytes 122888 | tf_op jit(solution)/shard_map/ppermute | solution.py:571
  50.1 3.0 %shard_map.57 = (f32[48,128]{1,0:T(8,128)S(1)}, f32[6,352,128]{2,1,0:T(8,128)S(1)}, f32[6,176,128]{2,1,0:T(8,128)S(1)}, f32[6,96,128]{2,1,0:T(8,128)S(1)}) custom-call(s32[2]{0:T(128)S(1)} %pad_add_fusion.index.refs_0_, f32[512,128]{1,0:T(8,128)S(1)} %bitcast.7, f32[512,128]{1,0:T(8,128)S(1)} %collective-permute-done.4.refs_2_), custom_call_target="tpu_custom_call" | custom-call | tf_op jit(solution)/shard_map/pallas_call | solution.py:490
  53.1 0.2 collective-permute-done.6.refs_7_
  53.4 1.5 %shard_map.58 = (f32[16,8,128]{2,1,0:T(8,128)S(1)}, f32[11,8,128]{2,1,0:T(8,128)S(1)}, f32[11,8,128]{2,1,0:T(8,128)S(1)}) custom-call(s32[2]{0:T(128)S(1)} %pad_add_fusion.index.refs_0_, f32[960,128]{1,0:T(8,128)S(1)} %get-tuple-element.34.refs_1_.refs_4_, f32[10,11,24,128]{3,2,1,0:T(8,128)S(1)} %get-tuple-element.35.refs_2_.refs_5_, ...), custom_call_target="tpu_custom_call" | custom-call | tf_op jit(solution)/shard_map/pallas_call | solution.py:490
  54.8 1.1 %collective-permute-start.7 = (f32[11,8,128]{2,1,0:T(8,128)S(1)}, f32[11,8,128]{2,1,0:T(8,128)S(1)}, u32[]{:S(2)}, u32[]{:S(2)}) collective-permute-start(f32[11,8,128]{2,1,0:T(8,128)S(1)} %get-tuple-element.44), channel_id=1, source_target_pairs={{0,248},{8,16},{16,8},{24,32},{32,24},{40,48},{48,40},{56,64},{64,... | collective-permute-start | bytes 135176 | tf_op jit(solution)/shard_map/ppermute | solution.py:571
  56.1 5.0 %collective-permute-done.7 = f32[11,8,128]{2,1,0:T(8,128)S(1)} collective-permute-done((f32[11,8,128]{2,1,0:T(8,128)S(1)}, f32[11,8,128]{2,1,0:T(8,128)S(1)}, u32[]{:S(2)}, u32[]{:S(2)}) %collective-permute-start.7) | collective-permute-done | bytes 45088 | tf_op jit(solution)/shard_map/ppermute | solution.py:571
  61.2 4.6 %collective-permute-start.10 = (f32[38,8,128]{2,1,0:T(8,128)S(1)}, f32[38,8,128]{2,1,0:T(8,128)S(1)}, u32[]{:S(2)}, u32[]{:S(2)}) collective-permute-start(f32[38,8,128]{2,1,0:T(8,128)S(1)} %pad_maximum_fusion.refs_2_), channel_id=1, source_target_pairs={{0,0},{1,2},{2,1},{3,4},{4,3},{5,6},{6,5},{7,7},{8,8},{9,10},{10,9... | collective-permute-start | bytes 466952 | tf_op jit(solution)/shard_map/ppermute | solution.py:571
  65.9 2.8 %collective-permute-done.10.refs_3_ = f32[38,8,128]{2,1,0:T(8,128)S(1)} collective-permute-done((f32[38,8,128]{2,1,0:T(8,128)S(1)}, f32[38,8,128]{2,1,0:T(8,128)S(1)}, u32[]{:S(2)}, u32[]{:S(2)}) %collective-permute-start.10) | collective-permute-done | bytes 155680 | tf_op jit(solution)/shard_map/ppermute | solution.py:571
  68.7 1.9 %shard_map.59 = (f32[256,128]{1,0:T(8,128)S(1)}, f32[80,128]{1,0:T(8,128)S(1)}, f32[480,128]{1,0:T(8,128)S(1)}, f32[320,128]{1,0:T(8,128)S(1)}, f32[352,128]{1,0:T(8,128)S(1)}) custom-call(s32[2]{0:T(128)S(1)} %pad_add_fusion.index.refs_0_, f32[38,8,128]{2,1,0:T(8,128)S(1)} %collective-permute-done.9.refs_1_, f32[38,8,128]{2,1,0:T(8,128)S(1)} %pad_maximum_fusion.refs_2_, ...), custom_call_target="tpu_custom_call" | custom-call | tf_op jit(solution)/shard_map/pallas_call | solution.py:490
  70.6 17.4 %all_to_all.11 = f32[128,2,128]{2,1,0:T(2,128)S(1)} all-to-all(f32[128,2,128]{2,1,0:T(2,128)S(1)} %bitcast.11), channel_id=1, replica_groups=mesh['gz'=32,'gx'=4,'core'=2] {'gz','gx'}, dimensions={0} | all-to-all | bytes 262144 | tf_op jit(solution)/shard_map/all_to_all | solution.py:582
  87.9 2.3 %collective-permute-start.11 = (f32[256,128]{1,0:T(8,128)S(1)}, f32[256,128]{1,0:T(8,128)S(1)}, u32[]{:S(2)}, u32[]{:S(2)}) collective-permute-start(f32[256,128]{1,0:T(8,128)S(1)} %bitcast.8), channel_id=1, source_target_pairs={{0,1},{1,0},{2,3},{3,2},{4,5},{5,4},{6,7},{7,6},{8,9},{9,8},{10,11... | collective-permute-start | bytes 393224 | tf_op jit(solution)/shard_map/ppermute | solution.py:571
  90.2 2.0 %collective-permute-start.13 = (f32[80,128]{1,0:T(8,128)S(1)}, f32[80,128]{1,0:T(8,128)S(1)}, u32[]{:S(2)}, u32[]{:S(2)}) collective-permute-start(f32[80,128]{1,0:T(8,128)S(1)} %get-tuple-element.51), channel_id=1, source_target_pairs={{0,0},{1,2},{2,1},{3,4},{4,3},{5,6},{6,5},{7,7},{8,8},{9,10},{10,9... | collective-permute-start | bytes 122888 | tf_op jit(solution)/shard_map/ppermute | solution.py:571
  92.4 2.3 %shard_map.60.refs_5_ = f32[48,128]{1,0:T(8,128)S(1)} custom-call(s32[2]{0:T(128)S(1)} %pad_add_fusion.index.refs_0_, f32[256,128]{1,0:T(8,128)S(1)} %bitcast.9, f32[256,128]{1,0:T(8,128)S(1)} %collective-permute-done.11.refs_2_, f32[6,352,128]{2,1,0:T(8,128)S(1)} %get-tuple-element.48.refs_3_, f32[6,176,128]{2,1,0:T(8,128)S(1)} %get-tuple-element.49.refs_4_, ...), custom_call_target="tpu_custom_call" | custom-call | tf_op jit(solution)/shard_map/pallas_call | solution.py:490
  94.7 0.9 collective-permute-done.13.refs_7_
  95.5 2.1 %shard_map.61 = f32[16,8,128]{2,1,0:T(8,128)} custom-call(s32[2]{0:T(128)S(1)} %pad_add_fusion.index.refs_0_, f32[960,128]{1,0:T(8,128)S(1)} %get-tuple-element.34.refs_1_.refs_4_, f32[10,11,24,128]{3,2,1,0:T(8,128)S(1)} %get-tuple-element.35.refs_2_.refs_5_, f32[11,24,128]{2,1,0:T(8,128)S(1)} %get-tuple-element.36.refs_3_.refs_6_, ...), custom_call_target="tpu_custom_call" | custom-call | tf_op jit(solution)/shard_map/pallas_call | solution.py:490
  (23 shorter events, 0.7 us)
Async XLA Ops:
  1.7 10.4 %collective-permute-start = (f32[11,8,128]{2,1,0:T(8,128)S(1)}, f32[11,8,128]{2,1,0:T(8,128)S(1)}, u32[]{:S(2)}, u32[]{:S(2)}) collective-permute-start(f32[11,8,128]{2,1,0:T(8,128)S(1)} %get-tuple-element.30), channel_id=1, source_target_pairs={{0,248},{8,16},{16,8},{24,32},{32,24},{40,48},{48,40},{56,64},{64,... | collective-permute-start | bytes 135176 | tf_op jit(solution)/shard_map/ppermute | solution.py:571
  10.7 2.9 %collective-permute-start.1 = (f32[11,8,128]{2,1,0:T(8,128)S(1)}, f32[11,8,128]{2,1,0:T(8,128)S(1)}, u32[]{:S(2)}, u32[]{:S(2)}) collective-permute-start(f32[11,8,128]{2,1,0:T(8,128)S(1)} %get-tuple-element.31), channel_id=1, source_target_pairs={{0,8},{8,0},{16,24},{24,16},{32,40},{40,32},{48,56},{56,48},{64,72... | collective-permute-start | bytes 135176 | tf_op jit(solution)/shard_map/ppermute | solution.py:571
  13.7 8.1 %collective-permute-start.3 = (f32[39,8,128]{2,1,0:T(8,128)S(1)}, f32[39,8,128]{2,1,0:T(8,128)S(1)}, u32[]{:S(2)}, u32[]{:S(2)}) collective-permute-start(f32[39,8,128]{2,1,0:T(8,128)S(1)} %constant_dynamic-update-slice_fusion.refs_2_), channel_id=1, source_target_pairs={{0,0},{1,2},{2,1},{3,4},{4,3},{5,6},{6,5},{7,7},{8,8},{9,10},{10,9... | collective-permute-start | bytes 479240 | tf_op jit(solution)/shard_map/ppermute | solution.py:571
  18.8 2.9 %collective-permute-start.2 = (f32[39,8,128]{2,1,0:T(8,128)S(1)}, f32[39,8,128]{2,1,0:T(8,128)S(1)}, u32[]{:S(2)}, u32[]{:S(2)}) collective-permute-start(f32[39,8,128]{2,1,0:T(8,128)S(1)} %constant_dynamic-update-slice_fusion.refs_2_), channel_id=1, source_target_pairs={{0,1},{1,0},{2,3},{3,2},{4,5},{5,4},{6,7},{7,6},{8,9},{9,8},{10,11... | collective-permute-start | bytes 479240 | tf_op jit(solution)/shard_map/ppermute | solution.py:571
  45.1 5.0 %collective-permute-start.4 = (f32[512,128]{1,0:T(8,128)S(1)}, f32[512,128]{1,0:T(8,128)S(1)}, u32[]{:S(2)}, u32[]{:S(2)}) collective-permute-start(f32[512,128]{1,0:T(8,128)S(1)} %bitcast.6), channel_id=1, source_target_pairs={{0,1},{1,0},{2,3},{3,2},{4,5},{5,4},{6,7},{7,6},{8,9},{9,8},{10,11... | collective-permute-start | bytes 786440 | tf_op jit(solution)/shard_map/ppermute | solution.py:571
  48.1 5.3 %collective-permute-start.6 = (f32[80,128]{1,0:T(8,128)S(1)}, f32[80,128]{1,0:T(8,128)S(1)}, u32[]{:S(2)}, u32[]{:S(2)}) collective-permute-start(f32[80,128]{1,0:T(8,128)S(1)} %get-tuple-element.40), channel_id=1, source_target_pairs={{0,0},{1,2},{2,1},{3,4},{4,3},{5,6},{6,5},{7,7},{8,8},{9,10},{10,9... | collective-permute-start | bytes 122888 | tf_op jit(solution)/shard_map/ppermute | solution.py:571
  50.0 3.4 %collective-permute-start.5 = (f32[80,128]{1,0:T(8,128)S(1)}, f32[80,128]{1,0:T(8,128)S(1)}, u32[]{:S(2)}, u32[]{:S(2)}) collective-permute-start(f32[80,128]{1,0:T(8,128)S(1)} %get-tuple-element.40), channel_id=1, source_target_pairs={{0,1},{1,0},{2,3},{3,2},{4,5},{5,4},{6,7},{7,6},{8,9},{9,8},{10,11... | collective-permute-start | bytes 122888 | tf_op jit(solution)/shard_map/ppermute | solution.py:571
  54.8 6.3 %collective-permute-start.7 = (f32[11,8,128]{2,1,0:T(8,128)S(1)}, f32[11,8,128]{2,1,0:T(8,128)S(1)}, u32[]{:S(2)}, u32[]{:S(2)}) collective-permute-start(f32[11,8,128]{2,1,0:T(8,128)S(1)} %get-tuple-element.44), channel_id=1, source_target_pairs={{0,248},{8,16},{16,8},{24,32},{32,24},{40,48},{48,40},{56,64},{64,... | collective-permute-start | bytes 135176 | tf_op jit(solution)/shard_map/ppermute | solution.py:571
  56.0 5.2 %collective-permute-start.8 = (f32[11,8,128]{2,1,0:T(8,128)S(1)}, f32[11,8,128]{2,1,0:T(8,128)S(1)}, u32[]{:S(2)}, u32[]{:S(2)}) collective-permute-start(f32[11,8,128]{2,1,0:T(8,128)S(1)} %get-tuple-element.45), channel_id=1, source_target_pairs={{0,8},{8,0},{16,24},{24,16},{32,40},{40,32},{48,56},{56,48},{64,72... | collective-permute-start | bytes 135176 | tf_op jit(solution)/shard_map/ppermute | solution.py:571
  61.2 7.5 %collective-permute-start.10 = (f32[38,8,128]{2,1,0:T(8,128)S(1)}, f32[38,8,128]{2,1,0:T(8,128)S(1)}, u32[]{:S(2)}, u32[]{:S(2)}) collective-permute-start(f32[38,8,128]{2,1,0:T(8,128)S(1)} %pad_maximum_fusion.refs_2_), channel_id=1, source_target_pairs={{0,0},{1,2},{2,1},{3,4},{4,3},{5,6},{6,5},{7,7},{8,8},{9,10},{10,9... | collective-permute-start | bytes 466952 | tf_op jit(solution)/shard_map/ppermute | solution.py:571
  65.8 2.9 %collective-permute-start.9 = (f32[38,8,128]{2,1,0:T(8,128)S(1)}, f32[38,8,128]{2,1,0:T(8,128)S(1)}, u32[]{:S(2)}, u32[]{:S(2)}) collective-permute-start(f32[38,8,128]{2,1,0:T(8,128)S(1)} %pad_maximum_fusion.refs_2_), channel_id=1, source_target_pairs={{0,1},{1,0},{2,3},{3,2},{4,5},{5,4},{6,7},{7,6},{8,9},{9,8},{10,11... | collective-permute-start | bytes 466952 | tf_op jit(solution)/shard_map/ppermute | solution.py:571
  87.9 4.4 %collective-permute-start.11 = (f32[256,128]{1,0:T(8,128)S(1)}, f32[256,128]{1,0:T(8,128)S(1)}, u32[]{:S(2)}, u32[]{:S(2)}) collective-permute-start(f32[256,128]{1,0:T(8,128)S(1)} %bitcast.8), channel_id=1, source_target_pairs={{0,1},{1,0},{2,3},{3,2},{4,5},{5,4},{6,7},{7,6},{8,9},{9,8},{10,11... | collective-permute-start | bytes 393224 | tf_op jit(solution)/shard_map/ppermute | solution.py:571
  90.2 5.3 %collective-permute-start.13 = (f32[80,128]{1,0:T(8,128)S(1)}, f32[80,128]{1,0:T(8,128)S(1)}, u32[]{:S(2)}, u32[]{:S(2)}) collective-permute-start(f32[80,128]{1,0:T(8,128)S(1)} %get-tuple-element.51), channel_id=1, source_target_pairs={{0,0},{1,2},{2,1},{3,4},{4,3},{5,6},{6,5},{7,7},{8,8},{9,10},{10,9... | collective-permute-start | bytes 122888 | tf_op jit(solution)/shard_map/ppermute | solution.py:571
  92.3 3.3 %collective-permute-start.12 = (f32[80,128]{1,0:T(8,128)S(1)}, f32[80,128]{1,0:T(8,128)S(1)}, u32[]{:S(2)}, u32[]{:S(2)}) collective-permute-start(f32[80,128]{1,0:T(8,128)S(1)} %get-tuple-element.51), channel_id=1, source_target_pairs={{0,1},{1,0},{2,3},{3,2},{4,5},{5,4},{6,7},{7,6},{8,9},{9,8},{10,11... | collective-permute-start | bytes 122888 | tf_op jit(solution)/shard_map/ppermute | solution.py:571

commit v7 on v5

--- a/solution.py
+++ b/solution.py
@@ -569,8 +569,19 @@
 
 
 def swaps(mate, other, axis):
-    far = swap(other, axis, other_of)
+    far = far_in_y(other) if axis == Y_AXIS else swap(other, axis, other_of)
     return swap(mate, axis, mate_of), far
+
+
+def far_in_y(array):
+    y_devices = lax.axis_size("gx") * lax.axis_size("core")
+    pairs = []
+    for z in range(lax.axis_size("gz")):
+        for y in range(y_devices):
+            at = other_of(y)
+            target = z * y_devices + at if 0 <= at < y_devices else mate_of(z) * y_devices + y
+            pairs.append((z * y_devices + y, target))
+    return lax.ppermute(array, ("gz", "gx", "core"), pairs)
 
 
 def to_all(copies):

time: 91.6 us -> 90.8 us (level)
  blocking collectives: 39.4 us -> 38.3 us
    ppermute x0 -> x4, waiting for transfers between devices: none -> 6.75 us  [far_in_y(): return lax.ppermute(array, ('gz', 'gx', 'core'), pairs)]
    ppermute x14 -> x10, starting transfers between devices: 22.6 us -> 16.8 us  [swap(): lax.ppermute(array, axis, [(i, partner(i) % count) for i in range(count)])]
    ppermute x14 -> x10, waiting for transfers between devices: 14.5 us -> 8.64 us  [swap(): lax.ppermute(array, axis, [(i, partner(i) % count) for i in range(count)])]
    ppermute x0 -> x4, starting transfers between devices: none -> 5.28 us  [far_in_y(): return lax.ppermute(array, ('gz', 'gx', 'core'), pairs)]
    all_to_all x2, blocking collectives: 39.4 us -> 38.3 us  [to_all(): out = lax.all_to_all(copies, ('gz', 'gx'), 0, 0)]
  transfers between devices with their start and end apart: 14 -> 14, of which waited for: 7 -> 8; matrix products, arithmetic and copies ran while one was open for 0% -> 0% of each run, Pallas kernels for 6% -> 6%
where the time goes in v7:
time: 90.8 us; the launch traced here: 90.6 us
  blocking collectives  38.3 us (42%)
  starting transfers between devices  22 us (24%)
  waiting for transfers between devices  15.4 us (17%)
  Pallas kernels  14.4 us (16%)
    all_to_all x2, blocking collectives, to_all(): out = lax.all_to_all(copies, ('gz', 'gx'), 0, 0)  38.3 us
    ppermute x10, starting transfers between devices, swap(): lax.ppermute(array, axis, [(i, partner(i) % count) for i in range(count)])  16.8 us
    pallas_call x7, Pallas kernels, call(): pl.pallas_call(body, out_shape=outs, in_specs=[pl.BlockSpec(memory_space=...  14.4 us
    ppermute x10, waiting for transfers between devices, swap(): lax.ppermute(array, axis, [(i, partner(i) % count) for i in range(count)])  8.64 us
    ppermute x4, waiting for transfers between devices, far_in_y(): return lax.ppermute(array, ('gz', 'gx', 'core'), pairs)  6.75 us
    ppermute x4, starting transfers between devices, far_in_y(): return lax.ppermute(array, ('gz', 'gx', 'core'), pairs)  5.28 us
  transfers between devices with their start and end apart: 14, of which 8 were waited for; matrix products, arithmetic and copies ran while one was open for 0% of the time, Pallas kernels for 6%

profile of v7, /device:TPU:1, one launch (start us, length us, event | category | flops | bytes accessed | tf_op | source)
XLA Modules:
  0.0 90.6 jit_solution(11375495230976457215)
XLA Ops:
  0.1 1.7 %shard_map.55 = (f32[1,8,128]{2,1,0:T(8,128)S(1)}, f32[16,8,128]{2,1,0:T(8,128)S(1)}, f32[11,8,128]{2,1,0:T(8,128)S(1)}, f32[11,8,128]{2,1,0:T(8,128)S(1)}) custom-call(s32[2]{0:T(128)S(1)} %pad_add_fusion.index.refs_0_, s32[64]{0:T(128)} %class_hbm.1, f32[3,4]{1,0:T(4,128)} %diff_hbm.1, s32[16,8,128]{2,1,0:T(8,128)} %phases_hbm.1, ...), custom_call_target="tpu_custom_call" | custom-call | tf_op jit(solution)/shard_map/pallas_call | solution.py:490
  1.7 8.9 %collective-permute-start = (f32[11,8,128]{2,1,0:T(8,128)S(1)}, f32[11,8,128]{2,1,0:T(8,128)S(1)}, u32[]{:S(2)}, u32[]{:S(2)}) collective-permute-start(f32[11,8,128]{2,1,0:T(8,128)S(1)} %get-tuple-element.30), channel_id=1, source_target_pairs={{0,248},{8,16},{16,8},{24,32},{32,24},{40,48},{48,40},{56,64},{64,... | collective-permute-start | bytes 135176 | tf_op jit(solution)/shard_map/ppermute | solution.py:568
  10.7 1.4 %collective-permute-done = f32[11,8,128]{2,1,0:T(8,128)S(1)} collective-permute-done((f32[11,8,128]{2,1,0:T(8,128)S(1)}, f32[11,8,128]{2,1,0:T(8,128)S(1)}, u32[]{:S(2)}, u32[]{:S(2)}) %collective-permute-start) | collective-permute-done | bytes 45088 | tf_op jit(solution)/shard_map/ppermute | solution.py:568
  12.1 1.5 %collective-permute-done.1 = f32[11,8,128]{2,1,0:T(8,128)S(1)} collective-permute-done((f32[11,8,128]{2,1,0:T(8,128)S(1)}, f32[11,8,128]{2,1,0:T(8,128)S(1)}, u32[]{:S(2)}, u32[]{:S(2)}) %collective-permute-start.1) | collective-permute-done | bytes 45088 | tf_op jit(solution)/shard_map/ppermute | solution.py:568
  13.7 3.3 %collective-permute-start.3 = (f32[39,8,128]{2,1,0:T(8,128)S(1)}, f32[39,8,128]{2,1,0:T(8,128)S(1)}, u32[]{:S(2)}, u32[]{:S(2)}) collective-permute-start(f32[39,8,128]{2,1,0:T(8,128)S(1)} %constant_dynamic-update-slice_fusion.refs_2_), channel_id=1, source_target_pairs={{0,8},{1,2},{2,1},{3,4},{4,3},{5,6},{6,5},{7,15},{8,0},{9,10},{10,... | collective-permute-start | bytes 479240 | tf_op jit(solution)/shard_map/ppermute | solution.py:584
  17.0 3.3 %collective-permute-done.3.refs_3_ = f32[39,8,128]{2,1,0:T(8,128)S(1)} collective-permute-done((f32[39,8,128]{2,1,0:T(8,128)S(1)}, f32[39,8,128]{2,1,0:T(8,128)S(1)}, u32[]{:S(2)}, u32[]{:S(2)}) %collective-permute-start.3) | collective-permute-done | bytes 159776 | tf_op jit(solution)/shard_map/ppermute | solution.py:584
  20.2 2.0 %shard_map.56 = (f32[512,128]{1,0:T(8,128)S(1)}, f32[80,128]{1,0:T(8,128)S(1)}, f32[480,128]{1,0:T(8,128)S(1)}, f32[320,128]{1,0:T(8,128)S(1)}, f32[352,128]{1,0...) custom-call(s32[2]{0:T(128)S(1)} %pad_add_fusion.index.refs_0_, ...), custom_call_target="tpu_custom_call" | custom-call | tf_op jit(solution)/shard_map/pallas_call | solution.py:490
  22.2 21.1 %all_to_all.10 = f32[128,4,128]{2,1,0:T(4,128)S(1)} all-to-all(f32[128,4,128]{2,1,0:T(4,128)S(1)} %bitcast.10), channel_id=1, replica_groups=mesh['gz'=32,'gx'=4,'core'=2] {'gz','gx'}, dimensions={0} | all-to-all | bytes 524288 | tf_op jit(solution)/shard_map/all_to_all | solution.py:590
  43.3 3.0 %collective-permute-start.4 = (f32[512,128]{1,0:T(8,128)S(1)}, f32[512,128]{1,0:T(8,128)S(1)}, u32[]{:S(2)}, u32[]{:S(2)}) collective-permute-start(f32[512,128]{1,0:T(8,128)S(1)} %bitcast.6), channel_id=1, source_target_pairs={{0,1},{1,0},{2,3},{3,2},{4,5},{5,4},{6,7},{7,6},{8,9},{9,8},{10,11... | collective-permute-start | bytes 786440 | tf_op jit(solution)/shard_map/ppermute | solution.py:568
  46.3 0.8 collective-permute-start.5
  47.0 0.4 collective-permute-done.4.refs_2_
  47.4 3.0 %shard_map.57 = (f32[48,128]{1,0:T(8,128)S(1)}, f32[6,352,128]{2,1,0:T(8,128)S(1)}, f32[6,176,128]{2,1,0:T(8,128)S(1)}, f32[6,96,128]{2,1,0:T(8,128)S(1)}) custom-call(s32[2]{0:T(128)S(1)} %pad_add_fusion.index.refs_0_, f32[512,128]{1,0:T(8,128)S(1)} %bitcast.7, f32[512,128]{1,0:T(8,128)S(1)} %collective-permute-done.4.refs_2_), custom_call_target="tpu_custom_call" | custom-call | tf_op jit(solution)/shard_map/pallas_call | solution.py:490
  50.5 1.5 %shard_map.58 = (f32[16,8,128]{2,1,0:T(8,128)S(1)}, f32[11,8,128]{2,1,0:T(8,128)S(1)}, f32[11,8,128]{2,1,0:T(8,128)S(1)}) custom-call(s32[2]{0:T(128)S(1)} %pad_add_fusion.index.refs_0_, f32[960,128]{1,0:T(8,128)S(1)} %get-tuple-element.34.refs_1_.refs_4_, f32[10,11,24,128]{3,2,1,0:T(8,128)S(1)} %get-tuple-element.35.refs_2_.refs_5_, ...), custom_call_target="tpu_custom_call" | custom-call | tf_op jit(solution)/shard_map/pallas_call | solution.py:490
  51.9 1.1 %collective-permute-start.7 = (f32[11,8,128]{2,1,0:T(8,128)S(1)}, f32[11,8,128]{2,1,0:T(8,128)S(1)}, u32[]{:S(2)}, u32[]{:S(2)}) collective-permute-start(f32[11,8,128]{2,1,0:T(8,128)S(1)} %get-tuple-element.44), channel_id=1, source_target_pairs={{0,248},{8,16},{16,8},{24,32},{32,24},{40,48},{48,40},{56,64},{64,... | collective-permute-start | bytes 135176 | tf_op jit(solution)/shard_map/ppermute | solution.py:568
  53.2 5.0 %collective-permute-done.7 = f32[11,8,128]{2,1,0:T(8,128)S(1)} collective-permute-done((f32[11,8,128]{2,1,0:T(8,128)S(1)}, f32[11,8,128]{2,1,0:T(8,128)S(1)}, u32[]{:S(2)}, u32[]{:S(2)}) %collective-permute-start.7) | collective-permute-done | bytes 45088 | tf_op jit(solution)/shard_map/ppermute | solution.py:568
  58.3 1.8 %collective-permute-start.10 = (f32[38,8,128]{2,1,0:T(8,128)S(1)}, f32[38,8,128]{2,1,0:T(8,128)S(1)}, u32[]{:S(2)}, u32[]{:S(2)}) collective-permute-start(f32[38,8,128]{2,1,0:T(8,128)S(1)} %pad_maximum_fusion.refs_2_), channel_id=1, source_target_pairs={{0,8},{1,2},{2,1},{3,4},{4,3},{5,6},{6,5},{7,15},{8,0},{9,10},{10,... | collective-permute-start | bytes 466952 | tf_op jit(solution)/shard_map/ppermute | solution.py:584
  60.2 3.2 %collective-permute-done.10.refs_3_ = f32[38,8,128]{2,1,0:T(8,128)S(1)} collective-permute-done((f32[38,8,128]{2,1,0:T(8,128)S(1)}, f32[38,8,128]{2,1,0:T(8,128)S(1)}, u32[]{:S(2)}, u32[]{:S(2)}) %collective-permute-start.10) | collective-permute-done | bytes 155680 | tf_op jit(solution)/shard_map/ppermute | solution.py:584
  63.3 1.9 %shard_map.59 = (f32[256,128]{1,0:T(8,128)S(1)}, f32[80,128]{1,0:T(8,128)S(1)}, f32[480,128]{1,0:T(8,128)S(1)}, f32[320,128]{1,0:T(8,128)S(1)}, f32[352,128]{1,0:T(8,128)S(1)}) custom-call(s32[2]{0:T(128)S(1)} %pad_add_fusion.index.refs_0_, f32[38,8,128]{2,1,0:T(8,128)S(1)} %collective-permute-done.9.refs_1_, f32[38,8,128]{2,1,0:T(8,128)S(1)} %pad_maximum_fusion.refs_2_, ...), custom_call_target="tpu_custom_call" | custom-call | tf_op jit(solution)/shard_map/pallas_call | solution.py:490
  65.2 17.2 %all_to_all.11 = f32[128,2,128]{2,1,0:T(2,128)S(1)} all-to-all(f32[128,2,128]{2,1,0:T(2,128)S(1)} %bitcast.11), channel_id=1, replica_groups=mesh['gz'=32,'gx'=4,'core'=2] {'gz','gx'}, dimensions={0} | all-to-all | bytes 262144 | tf_op jit(solution)/shard_map/all_to_all | solution.py:590
  82.4 2.2 %collective-permute-start.11 = (f32[256,128]{1,0:T(8,128)S(1)}, f32[256,128]{1,0:T(8,128)S(1)}, u32[]{:S(2)}, u32[]{:S(2)}) collective-permute-start(f32[256,128]{1,0:T(8,128)S(1)} %bitcast.8), channel_id=1, source_target_pairs={{0,1},{1,0},{2,3},{3,2},{4,5},{5,4},{6,7},{7,6},{8,9},{9,8},{10,11... | collective-permute-start | bytes 393224 | tf_op jit(solution)/shard_map/ppermute | solution.py:568
  84.8 0.5 collective-permute-start.12
  85.3 0.4 collective-permute-done.11.refs_2_
  85.7 2.3 %shard_map.60.refs_5_ = f32[48,128]{1,0:T(8,128)S(1)} custom-call(s32[2]{0:T(128)S(1)} %pad_add_fusion.index.refs_0_, f32[256,128]{1,0:T(8,128)S(1)} %bitcast.9, f32[256,128]{1,0:T(8,128)S(1)} %collective-permute-done.11.refs_2_, f32[6,352,128]{2,1,0:T(8,128)S(1)} %get-tuple-element.48.refs_3_, f32[6,176,128]{2,1,0:T(8,128)S(1)} %get-tuple-element.49.refs_4_, ...), custom_call_target="tpu_custom_call" | custom-call | tf_op jit(solution)/shard_map/pallas_call | solution.py:490
  88.3 2.1 %shard_map.61 = f32[16,8,128]{2,1,0:T(8,128)} custom-call(s32[2]{0:T(128)S(1)} %pad_add_fusion.index.refs_0_, f32[960,128]{1,0:T(8,128)S(1)} %get-tuple-element.34.refs_1_.refs_4_, f32[10,11,24,128]{3,2,1,0:T(8,128)S(1)} %get-tuple-element.35.refs_2_.refs_5_, f32[11,24,128]{2,1,0:T(8,128)S(1)} %get-tuple-element.36.refs_3_.refs_6_, ...), custom_call_target="tpu_custom_call" | custom-call | tf_op jit(solution)/shard_map/pallas_call | solution.py:490
  (23 shorter events, 0.8 us)
Async XLA Ops:
  1.7 10.4 %collective-permute-start = (f32[11,8,128]{2,1,0:T(8,128)S(1)}, f32[11,8,128]{2,1,0:T(8,128)S(1)}, u32[]{:S(2)}, u32[]{:S(2)}) collective-permute-start(f32[11,8,128]{2,1,0:T(8,128)S(1)} %get-tuple-element.30), channel_id=1, source_target_pairs={{0,248},{8,16},{16,8},{24,32},{32,24},{40,48},{48,40},{56,64},{64,... | collective-permute-start | bytes 135176 | tf_op jit(solution)/shard_map/ppermute | solution.py:568
  10.7 2.9 %collective-permute-start.1 = (f32[11,8,128]{2,1,0:T(8,128)S(1)}, f32[11,8,128]{2,1,0:T(8,128)S(1)}, u32[]{:S(2)}, u32[]{:S(2)}) collective-permute-start(f32[11,8,128]{2,1,0:T(8,128)S(1)} %get-tuple-element.31), channel_id=1, source_target_pairs={{0,8},{8,0},{16,24},{24,16},{32,40},{40,32},{48,56},{56,48},{64,72... | collective-permute-start | bytes 135176 | tf_op jit(solution)/shard_map/ppermute | solution.py:568
  13.7 6.5 %collective-permute-start.3 = (f32[39,8,128]{2,1,0:T(8,128)S(1)}, f32[39,8,128]{2,1,0:T(8,128)S(1)}, u32[]{:S(2)}, u32[]{:S(2)}) collective-permute-start(f32[39,8,128]{2,1,0:T(8,128)S(1)} %constant_dynamic-update-slice_fusion.refs_2_), channel_id=1, source_target_pairs={{0,8},{1,2},{2,1},{3,4},{4,3},{5,6},{6,5},{7,15},{8,0},{9,10},{10,... | collective-permute-start | bytes 479240 | tf_op jit(solution)/shard_map/ppermute | solution.py:584
  17.0 3.3 %collective-permute-start.2 = (f32[39,8,128]{2,1,0:T(8,128)S(1)}, f32[39,8,128]{2,1,0:T(8,128)S(1)}, u32[]{:S(2)}, u32[]{:S(2)}) collective-permute-start(f32[39,8,128]{2,1,0:T(8,128)S(1)} %constant_dynamic-update-slice_fusion.refs_2_), channel_id=1, source_target_pairs={{0,1},{1,0},{2,3},{3,2},{4,5},{5,4},{6,7},{7,6},{8,9},{9,8},{10,11... | collective-permute-start | bytes 479240 | tf_op jit(solution)/shard_map/ppermute | solution.py:568
  43.3 4.1 %collective-permute-start.4 = (f32[512,128]{1,0:T(8,128)S(1)}, f32[512,128]{1,0:T(8,128)S(1)}, u32[]{:S(2)}, u32[]{:S(2)}) collective-permute-start(f32[512,128]{1,0:T(8,128)S(1)} %bitcast.6), channel_id=1, source_target_pairs={{0,1},{1,0},{2,3},{3,2},{4,5},{5,4},{6,7},{7,6},{8,9},{9,8},{10,11... | collective-permute-start | bytes 786440 | tf_op jit(solution)/shard_map/ppermute | solution.py:568
  46.2 4.2 %collective-permute-start.6 = (f32[80,128]{1,0:T(8,128)S(1)}, f32[80,128]{1,0:T(8,128)S(1)}, u32[]{:S(2)}, u32[]{:S(2)}) collective-permute-start(f32[80,128]{1,0:T(8,128)S(1)} %get-tuple-element.40), channel_id=1, source_target_pairs={{0,8},{1,2},{2,1},{3,4},{4,3},{5,6},{6,5},{7,15},{8,0},{9,10},{10,... | collective-permute-start | bytes 122888 | tf_op jit(solution)/shard_map/ppermute | solution.py:584
  46.3 4.2 %collective-permute-start.5 = (f32[80,128]{1,0:T(8,128)S(1)}, f32[80,128]{1,0:T(8,128)S(1)}, u32[]{:S(2)}, u32[]{:S(2)}) collective-permute-start(f32[80,128]{1,0:T(8,128)S(1)} %get-tuple-element.40), channel_id=1, source_target_pairs={{0,1},{1,0},{2,3},{3,2},{4,5},{5,4},{6,7},{7,6},{8,9},{9,8},{10,11... | collective-permute-start | bytes 122888 | tf_op jit(solution)/shard_map/ppermute | solution.py:568
  51.9 6.3 %collective-permute-start.7 = (f32[11,8,128]{2,1,0:T(8,128)S(1)}, f32[11,8,128]{2,1,0:T(8,128)S(1)}, u32[]{:S(2)}, u32[]{:S(2)}) collective-permute-start(f32[11,8,128]{2,1,0:T(8,128)S(1)} %get-tuple-element.44), channel_id=1, source_target_pairs={{0,248},{8,16},{16,8},{24,32},{32,24},{40,48},{48,40},{56,64},{64,... | collective-permute-start | bytes 135176 | tf_op jit(solution)/shard_map/ppermute | solution.py:568
  53.1 5.2 %collective-permute-start.8 = (f32[11,8,128]{2,1,0:T(8,128)S(1)}, f32[11,8,128]{2,1,0:T(8,128)S(1)}, u32[]{:S(2)}, u32[]{:S(2)}) collective-permute-start(f32[11,8,128]{2,1,0:T(8,128)S(1)} %get-tuple-element.45), channel_id=1, source_target_pairs={{0,8},{8,0},{16,24},{24,16},{32,40},{40,32},{48,56},{56,48},{64,72... | collective-permute-start | bytes 135176 | tf_op jit(solution)/shard_map/ppermute | solution.py:568
  58.3 5.1 %collective-permute-start.10 = (f32[38,8,128]{2,1,0:T(8,128)S(1)}, f32[38,8,128]{2,1,0:T(8,128)S(1)}, u32[]{:S(2)}, u32[]{:S(2)}) collective-permute-start(f32[38,8,128]{2,1,0:T(8,128)S(1)} %pad_maximum_fusion.refs_2_), channel_id=1, source_target_pairs={{0,8},{1,2},{2,1},{3,4},{4,3},{5,6},{6,5},{7,15},{8,0},{9,10},{10,... | collective-permute-start | bytes 466952 | tf_op jit(solution)/shard_map/ppermute | solution.py:584
  60.1 3.2 %collective-permute-start.9 = (f32[38,8,128]{2,1,0:T(8,128)S(1)}, f32[38,8,128]{2,1,0:T(8,128)S(1)}, u32[]{:S(2)}, u32[]{:S(2)}) collective-permute-start(f32[38,8,128]{2,1,0:T(8,128)S(1)} %pad_maximum_fusion.refs_2_), channel_id=1, source_target_pairs={{0,1},{1,0},{2,3},{3,2},{4,5},{5,4},{6,7},{7,6},{8,9},{9,8},{10,11... | collective-permute-start | bytes 466952 | tf_op jit(solution)/shard_map/ppermute | solution.py:568
  82.4 3.2 %collective-permute-start.11 = (f32[256,128]{1,0:T(8,128)S(1)}, f32[256,128]{1,0:T(8,128)S(1)}, u32[]{:S(2)}, u32[]{:S(2)}) collective-permute-start(f32[256,128]{1,0:T(8,128)S(1)} %bitcast.8), channel_id=1, source_target_pairs={{0,1},{1,0},{2,3},{3,2},{4,5},{5,4},{6,7},{7,6},{8,9},{9,8},{10,11... | collective-permute-start | bytes 393224 | tf_op jit(solution)/shard_map/ppermute | solution.py:568
  84.7 3.6 %collective-permute-start.13 = (f32[80,128]{1,0:T(8,128)S(1)}, f32[80,128]{1,0:T(8,128)S(1)}, u32[]{:S(2)}, u32[]{:S(2)}) collective-permute-start(f32[80,128]{1,0:T(8,128)S(1)} %get-tuple-element.51), channel_id=1, source_target_pairs={{0,8},{1,2},{2,1},{3,4},{4,3},{5,6},{6,5},{7,15},{8,0},{9,10},{10,... | collective-permute-start | bytes 122888 | tf_op jit(solution)/shard_map/ppermute | solution.py:584
  84.8 3.5 %collective-permute-start.12 = (f32[80,128]{1,0:T(8,128)S(1)}, f32[80,128]{1,0:T(8,128)S(1)}, u32[]{:S(2)}, u32[]{:S(2)}) collective-permute-start(f32[80,128]{1,0:T(8,128)S(1)} %get-tuple-element.51), channel_id=1, source_target_pairs={{0,1},{1,0},{2,3},{3,2},{4,5},{5,4},{6,7},{7,6},{8,9},{9,8},{10,11... | collective-permute-start | bytes 122888 | tf_op jit(solution)/shard_map/ppermute | solution.py:568

commit v8 on v7

--- a/solution.py
+++ b/solution.py
@@ -157,8 +157,7 @@
     even, _ = parities(index)
     num_phases, num_classes = diff.shape
     pairs = [(class_hbm, classes), (diff_hbm, diff)]
-    for block in range(4):
-        pairs += [(phases_hbm.at[4 * block], phases.at[block]), (grains_hbm.at[4 * block], grains.at[block])]
+    pairs += [(phases_hbm.at[:, 0], phases), (grains_hbm.at[:, 0], grains)]
     top = 16 - HALO
     pairs += [
         (conc_hbm.at[pl.ds(jnp.where(even, top, 0), HALO)], mate_ref.at[0:HALO]),
@@ -614,6 +613,7 @@
     y_device = lax.axis_index("gx") * lax.axis_size("core") + lax.axis_index("core")
     index = jnp.stack([lax.axis_index("gz"), y_device]).astype(jnp.int32)
     plane = (4,) + phases.shape[1:]
+    blocks = (4, 4) + phases.shape[1:]
     part = floats(HALO + 1, 8, 128)
     kappa, block, *parts = call(
         kappa_body,
@@ -623,11 +623,11 @@
             pltpu.SMEM(diffusivity.shape, jnp.float32),
             pltpu.VMEM(plane, jnp.int32),
             pltpu.VMEM(plane, jnp.int32),
-            pltpu.SemaphoreType.DMA((13,)),
+            pltpu.SemaphoreType.DMA((7,)),
         ],
         [index] + [
             pltpu.with_memory_space_constraint(array, pltpu.HBM)
-            for array in (grain_class, diffusivity, phases, grains, concentration)
+            for array in (grain_class, diffusivity, phases.reshape(blocks), grains.reshape(blocks), concentration)
         ],
         pltpu.HBM,
     )

time: 90.8 us -> 90.7 us (level)
  no operation moved by 1% of the time
where the time goes in v8:
time: 90.7 us; the launch traced here: 90.5 us
  blocking collectives  38.3 us (42%)
  starting transfers between devices  22 us (24%)
  waiting for transfers between devices  15.4 us (17%)
  Pallas kernels  14.3 us (16%)
    all_to_all x2, blocking collectives, to_all(): out = lax.all_to_all(copies, ('gz', 'gx'), 0, 0)  38.3 us
    ppermute x10, starting transfers between devices, swap(): lax.ppermute(array, axis, [(i, partner(i) % count) for i in range(count)])  16.8 us
    pallas_call x7, Pallas kernels, call(): pl.pallas_call(body, out_shape=outs, in_specs=[pl.BlockSpec(memory_space=...  14.3 us
    ppermute x10, waiting for transfers between devices, swap(): lax.ppermute(array, axis, [(i, partner(i) % count) for i in range(count)])  8.64 us
    ppermute x4, waiting for transfers between devices, far_in_y(): return lax.ppermute(array, ('gz', 'gx', 'core'), pairs)  6.75 us
    ppermute x4, starting transfers between devices, far_in_y(): return lax.ppermute(array, ('gz', 'gx', 'core'), pairs)  5.28 us
  transfers between devices with their start and end apart: 14, of which 8 were waited for; matrix products, arithmetic and copies ran while one was open for 0% of the time, Pallas kernels for 6%

profile of v8, /device:TPU:1, one launch (start us, length us, event | category | flops | bytes accessed | tf_op | source)
XLA Modules:
  0.0 90.5 jit_solution(15954003034158809797)
XLA Ops:
  0.1 1.6 %shard_map.55 = (f32[1,8,128]{2,1,0:T(8,128)S(1)}, f32[16,8,128]{2,1,0:T(8,128)S(1)}, f32[11,8,128]{2,1,0:T(8,128)S(1)}, f32[11,8,128]{2,1,0:T(8,128)S(1)}) custom-call(s32[2]{0:T(128)S(1)} %pad_add_fusion.index.refs_0_, s32[64]{0:T(128)} %class_hbm.1, f32[3,4]{1,0:T(4,128)} %diff_hbm.1, s32[4,4,8,128]{3,2,1,0:T(8,128)} %bitcast.14, ...), custom_call_target="tpu_custom_call" | custom-call | tf_op jit(solution)/shard_map/pallas_call | solution.py:489
  1.7 8.9 %collective-permute-start = (f32[11,8,128]{2,1,0:T(8,128)S(1)}, f32[11,8,128]{2,1,0:T(8,128)S(1)}, u32[]{:S(2)}, u32[]{:S(2)}) collective-permute-start(f32[11,8,128]{2,1,0:T(8,128)S(1)} %get-tuple-element.30), channel_id=1, source_target_pairs={{0,248},{8,16},{16,8},{24,32},{32,24},{40,48},{48,40},{56,64},{64,... | collective-permute-start | bytes 135176 | tf_op jit(solution)/shard_map/ppermute | solution.py:567
  10.6 1.4 %collective-permute-done = f32[11,8,128]{2,1,0:T(8,128)S(1)} collective-permute-done((f32[11,8,128]{2,1,0:T(8,128)S(1)}, f32[11,8,128]{2,1,0:T(8,128)S(1)}, u32[]{:S(2)}, u32[]{:S(2)}) %collective-permute-start) | collective-permute-done | bytes 45088 | tf_op jit(solution)/shard_map/ppermute | solution.py:567
  12.0 1.5 %collective-permute-done.1 = f32[11,8,128]{2,1,0:T(8,128)S(1)} collective-permute-done((f32[11,8,128]{2,1,0:T(8,128)S(1)}, f32[11,8,128]{2,1,0:T(8,128)S(1)}, u32[]{:S(2)}, u32[]{:S(2)}) %collective-permute-start.1) | collective-permute-done | bytes 45088 | tf_op jit(solution)/shard_map/ppermute | solution.py:567
  13.6 3.3 %collective-permute-start.3 = (f32[39,8,128]{2,1,0:T(8,128)S(1)}, f32[39,8,128]{2,1,0:T(8,128)S(1)}, u32[]{:S(2)}, u32[]{:S(2)}) collective-permute-start(f32[39,8,128]{2,1,0:T(8,128)S(1)} %constant_dynamic-update-slice_fusion.refs_2_), channel_id=1, source_target_pairs={{0,8},{1,2},{2,1},{3,4},{4,3},{5,6},{6,5},{7,15},{8,0},{9,10},{10,... | collective-permute-start | bytes 479240 | tf_op jit(solution)/shard_map/ppermute | solution.py:583
  16.9 3.3 %collective-permute-done.3.refs_3_ = f32[39,8,128]{2,1,0:T(8,128)S(1)} collective-permute-done((f32[39,8,128]{2,1,0:T(8,128)S(1)}, f32[39,8,128]{2,1,0:T(8,128)S(1)}, u32[]{:S(2)}, u32[]{:S(2)}) %collective-permute-start.3) | collective-permute-done | bytes 159776 | tf_op jit(solution)/shard_map/ppermute | solution.py:583
  20.1 2.0 %shard_map.56 = (f32[512,128]{1,0:T(8,128)S(1)}, f32[80,128]{1,0:T(8,128)S(1)}, f32[480,128]{1,0:T(8,128)S(1)}, f32[320,128]{1,0:T(8,128)S(1)}, f32[352,128]{1,0...) custom-call(s32[2]{0:T(128)S(1)} %pad_add_fusion.index.refs_0_, ...), custom_call_target="tpu_custom_call" | custom-call | tf_op jit(solution)/shard_map/pallas_call | solution.py:489
  22.1 21.1 %all_to_all.10 = f32[128,4,128]{2,1,0:T(4,128)S(1)} all-to-all(f32[128,4,128]{2,1,0:T(4,128)S(1)} %bitcast.12), channel_id=1, replica_groups=mesh['gz'=32,'gx'=4,'core'=2] {'gz','gx'}, dimensions={0} | all-to-all | bytes 524288 | tf_op jit(solution)/shard_map/all_to_all | solution.py:589
  43.2 3.0 %collective-permute-start.4 = (f32[512,128]{1,0:T(8,128)S(1)}, f32[512,128]{1,0:T(8,128)S(1)}, u32[]{:S(2)}, u32[]{:S(2)}) collective-permute-start(f32[512,128]{1,0:T(8,128)S(1)} %bitcast.8), channel_id=1, source_target_pairs={{0,1},{1,0},{2,3},{3,2},{4,5},{5,4},{6,7},{7,6},{8,9},{9,8},{10,11... | collective-permute-start | bytes 786440 | tf_op jit(solution)/shard_map/ppermute | solution.py:567
  46.2 0.8 collective-permute-start.5
  47.0 0.4 collective-permute-done.4.refs_2_
  47.3 3.0 %shard_map.57 = (f32[48,128]{1,0:T(8,128)S(1)}, f32[6,352,128]{2,1,0:T(8,128)S(1)}, f32[6,176,128]{2,1,0:T(8,128)S(1)}, f32[6,96,128]{2,1,0:T(8,128)S(1)}) custom-call(s32[2]{0:T(128)S(1)} %pad_add_fusion.index.refs_0_, f32[512,128]{1,0:T(8,128)S(1)} %bitcast.9, f32[512,128]{1,0:T(8,128)S(1)} %collective-permute-done.4.refs_2_), custom_call_target="tpu_custom_call" | custom-call | tf_op jit(solution)/shard_map/pallas_call | solution.py:489
  50.4 1.5 %shard_map.58 = (f32[16,8,128]{2,1,0:T(8,128)S(1)}, f32[11,8,128]{2,1,0:T(8,128)S(1)}, f32[11,8,128]{2,1,0:T(8,128)S(1)}) custom-call(s32[2]{0:T(128)S(1)} %pad_add_fusion.index.refs_0_, f32[960,128]{1,0:T(8,128)S(1)} %get-tuple-element.34.refs_1_.refs_4_, f32[10,11,24,128]{3,2,1,0:T(8,128)S(1)} %get-tuple-element.35.refs_2_.refs_5_, ...), custom_call_target="tpu_custom_call" | custom-call | tf_op jit(solution)/shard_map/pallas_call | solution.py:489
  51.8 1.1 %collective-permute-start.7 = (f32[11,8,128]{2,1,0:T(8,128)S(1)}, f32[11,8,128]{2,1,0:T(8,128)S(1)}, u32[]{:S(2)}, u32[]{:S(2)}) collective-permute-start(f32[11,8,128]{2,1,0:T(8,128)S(1)} %get-tuple-element.44), channel_id=1, source_target_pairs={{0,248},{8,16},{16,8},{24,32},{32,24},{40,48},{48,40},{56,64},{64,... | collective-permute-start | bytes 135176 | tf_op jit(solution)/shard_map/ppermute | solution.py:567
  53.1 5.0 %collective-permute-done.7 = f32[11,8,128]{2,1,0:T(8,128)S(1)} collective-permute-done((f32[11,8,128]{2,1,0:T(8,128)S(1)}, f32[11,8,128]{2,1,0:T(8,128)S(1)}, u32[]{:S(2)}, u32[]{:S(2)}) %collective-permute-start.7) | collective-permute-done | bytes 45088 | tf_op jit(solution)/shard_map/ppermute | solution.py:567
  58.2 1.8 %collective-permute-start.10 = (f32[38,8,128]{2,1,0:T(8,128)S(1)}, f32[38,8,128]{2,1,0:T(8,128)S(1)}, u32[]{:S(2)}, u32[]{:S(2)}) collective-permute-start(f32[38,8,128]{2,1,0:T(8,128)S(1)} %pad_maximum_fusion.refs_2_), channel_id=1, source_target_pairs={{0,8},{1,2},{2,1},{3,4},{4,3},{5,6},{6,5},{7,15},{8,0},{9,10},{10,... | collective-permute-start | bytes 466952 | tf_op jit(solution)/shard_map/ppermute | solution.py:583
  60.1 3.2 %collective-permute-done.10.refs_3_ = f32[38,8,128]{2,1,0:T(8,128)S(1)} collective-permute-done((f32[38,8,128]{2,1,0:T(8,128)S(1)}, f32[38,8,128]{2,1,0:T(8,128)S(1)}, u32[]{:S(2)}, u32[]{:S(2)}) %collective-permute-start.10) | collective-permute-done | bytes 155680 | tf_op jit(solution)/shard_map/ppermute | solution.py:583
  63.2 1.9 %shard_map.59 = (f32[256,128]{1,0:T(8,128)S(1)}, f32[80,128]{1,0:T(8,128)S(1)}, f32[480,128]{1,0:T(8,128)S(1)}, f32[320,128]{1,0:T(8,128)S(1)}, f32[352,128]{1,0:T(8,128)S(1)}) custom-call(s32[2]{0:T(128)S(1)} %pad_add_fusion.index.refs_0_, f32[38,8,128]{2,1,0:T(8,128)S(1)} %collective-permute-done.9.refs_1_, f32[38,8,128]{2,1,0:T(8,128)S(1)} %pad_maximum_fusion.refs_2_, ...), custom_call_target="tpu_custom_call" | custom-call | tf_op jit(solution)/shard_map/pallas_call | solution.py:489
  65.1 17.2 %all_to_all.11 = f32[128,2,128]{2,1,0:T(2,128)S(1)} all-to-all(f32[128,2,128]{2,1,0:T(2,128)S(1)} %bitcast.13), channel_id=1, replica_groups=mesh['gz'=32,'gx'=4,'core'=2] {'gz','gx'}, dimensions={0} | all-to-all | bytes 262144 | tf_op jit(solution)/shard_map/all_to_all | solution.py:589
  82.4 2.2 %collective-permute-start.11 = (f32[256,128]{1,0:T(8,128)S(1)}, f32[256,128]{1,0:T(8,128)S(1)}, u32[]{:S(2)}, u32[]{:S(2)}) collective-permute-start(f32[256,128]{1,0:T(8,128)S(1)} %bitcast.10), channel_id=1, source_target_pairs={{0,1},{1,0},{2,3},{3,2},{4,5},{5,4},{6,7},{7,6},{8,9},{9,8},{10,11... | collective-permute-start | bytes 393224 | tf_op jit(solution)/shard_map/ppermute | solution.py:567
  84.7 0.5 collective-permute-start.12
  85.2 0.4 collective-permute-done.11.refs_2_
  85.6 2.3 %shard_map.60.refs_5_ = f32[48,128]{1,0:T(8,128)S(1)} custom-call(s32[2]{0:T(128)S(1)} %pad_add_fusion.index.refs_0_, f32[256,128]{1,0:T(8,128)S(1)} %bitcast.11, f32[256,128]{1,0:T(8,128)S(1)} %collective-permute-done.11.refs_2_, f32[6,352,128]{2,1,0:T(8,128)S(1)} %get-tuple-element.48.refs_3_, f32[6,176,128]{2,1,0:T(8,128)S(1)} %get-tuple-element.49.refs_4_, ...), custom_call_target="tpu_custom_call" | custom-call | tf_op jit(solution)/shard_map/pallas_call | solution.py:489
  88.2 2.1 %shard_map.61 = f32[16,8,128]{2,1,0:T(8,128)} custom-call(s32[2]{0:T(128)S(1)} %pad_add_fusion.index.refs_0_, f32[960,128]{1,0:T(8,128)S(1)} %get-tuple-element.34.refs_1_.refs_4_, f32[10,11,24,128]{3,2,1,0:T(8,128)S(1)} %get-tuple-element.35.refs_2_.refs_5_, f32[11,24,128]{2,1,0:T(8,128)S(1)} %get-tuple-element.36.refs_3_.refs_6_, ...), custom_call_target="tpu_custom_call" | custom-call | tf_op jit(solution)/shard_map/pallas_call | solution.py:489
  (23 shorter events, 0.8 us)
Async XLA Ops:
  1.7 10.4 %collective-permute-start = (f32[11,8,128]{2,1,0:T(8,128)S(1)}, f32[11,8,128]{2,1,0:T(8,128)S(1)}, u32[]{:S(2)}, u32[]{:S(2)}) collective-permute-start(f32[11,8,128]{2,1,0:T(8,128)S(1)} %get-tuple-element.30), channel_id=1, source_target_pairs={{0,248},{8,16},{16,8},{24,32},{32,24},{40,48},{48,40},{56,64},{64,... | collective-permute-start | bytes 135176 | tf_op jit(solution)/shard_map/ppermute | solution.py:567
  10.6 2.9 %collective-permute-start.1 = (f32[11,8,128]{2,1,0:T(8,128)S(1)}, f32[11,8,128]{2,1,0:T(8,128)S(1)}, u32[]{:S(2)}, u32[]{:S(2)}) collective-permute-start(f32[11,8,128]{2,1,0:T(8,128)S(1)} %get-tuple-element.31), channel_id=1, source_target_pairs={{0,8},{8,0},{16,24},{24,16},{32,40},{40,32},{48,56},{56,48},{64,72... | collective-permute-start | bytes 135176 | tf_op jit(solution)/shard_map/ppermute | solution.py:567
  13.6 6.5 %collective-permute-start.3 = (f32[39,8,128]{2,1,0:T(8,128)S(1)}, f32[39,8,128]{2,1,0:T(8,128)S(1)}, u32[]{:S(2)}, u32[]{:S(2)}) collective-permute-start(f32[39,8,128]{2,1,0:T(8,128)S(1)} %constant_dynamic-update-slice_fusion.refs_2_), channel_id=1, source_target_pairs={{0,8},{1,2},{2,1},{3,4},{4,3},{5,6},{6,5},{7,15},{8,0},{9,10},{10,... | collective-permute-start | bytes 479240 | tf_op jit(solution)/shard_map/ppermute | solution.py:583
  16.9 3.3 %collective-permute-start.2 = (f32[39,8,128]{2,1,0:T(8,128)S(1)}, f32[39,8,128]{2,1,0:T(8,128)S(1)}, u32[]{:S(2)}, u32[]{:S(2)}) collective-permute-start(f32[39,8,128]{2,1,0:T(8,128)S(1)} %constant_dynamic-update-slice_fusion.refs_2_), channel_id=1, source_target_pairs={{0,1},{1,0},{2,3},{3,2},{4,5},{5,4},{6,7},{7,6},{8,9},{9,8},{10,11... | collective-permute-start | bytes 479240 | tf_op jit(solution)/shard_map/ppermute | solution.py:567
  43.2 4.1 %collective-permute-start.4 = (f32[512,128]{1,0:T(8,128)S(1)}, f32[512,128]{1,0:T(8,128)S(1)}, u32[]{:S(2)}, u32[]{:S(2)}) collective-permute-start(f32[512,128]{1,0:T(8,128)S(1)} %bitcast.8), channel_id=1, source_target_pairs={{0,1},{1,0},{2,3},{3,2},{4,5},{5,4},{6,7},{7,6},{8,9},{9,8},{10,11... | collective-permute-start | bytes 786440 | tf_op jit(solution)/shard_map/ppermute | solution.py:567
  46.1 4.2 %collective-permute-start.6 = (f32[80,128]{1,0:T(8,128)S(1)}, f32[80,128]{1,0:T(8,128)S(1)}, u32[]{:S(2)}, u32[]{:S(2)}) collective-permute-start(f32[80,128]{1,0:T(8,128)S(1)} %get-tuple-element.40), channel_id=1, source_target_pairs={{0,8},{1,2},{2,1},{3,4},{4,3},{5,6},{6,5},{7,15},{8,0},{9,10},{10,... | collective-permute-start | bytes 122888 | tf_op jit(solution)/shard_map/ppermute | solution.py:583
  46.2 4.2 %collective-permute-start.5 = (f32[80,128]{1,0:T(8,128)S(1)}, f32[80,128]{1,0:T(8,128)S(1)}, u32[]{:S(2)}, u32[]{:S(2)}) collective-permute-start(f32[80,128]{1,0:T(8,128)S(1)} %get-tuple-element.40), channel_id=1, source_target_pairs={{0,1},{1,0},{2,3},{3,2},{4,5},{5,4},{6,7},{7,6},{8,9},{9,8},{10,11... | collective-permute-start | bytes 122888 | tf_op jit(solution)/shard_map/ppermute | solution.py:567
  51.8 6.3 %collective-permute-start.7 = (f32[11,8,128]{2,1,0:T(8,128)S(1)}, f32[11,8,128]{2,1,0:T(8,128)S(1)}, u32[]{:S(2)}, u32[]{:S(2)}) collective-permute-start(f32[11,8,128]{2,1,0:T(8,128)S(1)} %get-tuple-element.44), channel_id=1, source_target_pairs={{0,248},{8,16},{16,8},{24,32},{32,24},{40,48},{48,40},{56,64},{64,... | collective-permute-start | bytes 135176 | tf_op jit(solution)/shard_map/ppermute | solution.py:567
  53.0 5.2 %collective-permute-start.8 = (f32[11,8,128]{2,1,0:T(8,128)S(1)}, f32[11,8,128]{2,1,0:T(8,128)S(1)}, u32[]{:S(2)}, u32[]{:S(2)}) collective-permute-start(f32[11,8,128]{2,1,0:T(8,128)S(1)} %get-tuple-element.45), channel_id=1, source_target_pairs={{0,8},{8,0},{16,24},{24,16},{32,40},{40,32},{48,56},{56,48},{64,72... | collective-permute-start | bytes 135176 | tf_op jit(solution)/shard_map/ppermute | solution.py:567
  58.2 5.1 %collective-permute-start.10 = (f32[38,8,128]{2,1,0:T(8,128)S(1)}, f32[38,8,128]{2,1,0:T(8,128)S(1)}, u32[]{:S(2)}, u32[]{:S(2)}) collective-permute-start(f32[38,8,128]{2,1,0:T(8,128)S(1)} %pad_maximum_fusion.refs_2_), channel_id=1, source_target_pairs={{0,8},{1,2},{2,1},{3,4},{4,3},{5,6},{6,5},{7,15},{8,0},{9,10},{10,... | collective-permute-start | bytes 466952 | tf_op jit(solution)/shard_map/ppermute | solution.py:583
  60.0 3.2 %collective-permute-start.9 = (f32[38,8,128]{2,1,0:T(8,128)S(1)}, f32[38,8,128]{2,1,0:T(8,128)S(1)}, u32[]{:S(2)}, u32[]{:S(2)}) collective-permute-start(f32[38,8,128]{2,1,0:T(8,128)S(1)} %pad_maximum_fusion.refs_2_), channel_id=1, source_target_pairs={{0,1},{1,0},{2,3},{3,2},{4,5},{5,4},{6,7},{7,6},{8,9},{9,8},{10,11... | collective-permute-start | bytes 466952 | tf_op jit(solution)/shard_map/ppermute | solution.py:567
  82.4 3.2 %collective-permute-start.11 = (f32[256,128]{1,0:T(8,128)S(1)}, f32[256,128]{1,0:T(8,128)S(1)}, u32[]{:S(2)}, u32[]{:S(2)}) collective-permute-start(f32[256,128]{1,0:T(8,128)S(1)} %bitcast.10), channel_id=1, source_target_pairs={{0,1},{1,0},{2,3},{3,2},{4,5},{5,4},{6,7},{7,6},{8,9},{9,8},{10,11... | collective-permute-start | bytes 393224 | tf_op jit(solution)/shard_map/ppermute | solution.py:567
  84.6 3.6 %collective-permute-start.13 = (f32[80,128]{1,0:T(8,128)S(1)}, f32[80,128]{1,0:T(8,128)S(1)}, u32[]{:S(2)}, u32[]{:S(2)}) collective-permute-start(f32[80,128]{1,0:T(8,128)S(1)} %get-tuple-element.51), channel_id=1, source_target_pairs={{0,8},{1,2},{2,1},{3,4},{4,3},{5,6},{6,5},{7,15},{8,0},{9,10},{10,... | collective-permute-start | bytes 122888 | tf_op jit(solution)/shard_map/ppermute | solution.py:583
  84.7 3.5 %collective-permute-start.12 = (f32[80,128]{1,0:T(8,128)S(1)}, f32[80,128]{1,0:T(8,128)S(1)}, u32[]{:S(2)}, u32[]{:S(2)}) collective-permute-start(f32[80,128]{1,0:T(8,128)S(1)} %get-tuple-element.51), channel_id=1, source_target_pairs={{0,1},{1,0},{2,3},{3,2},{4,5},{5,4},{6,7},{7,6},{8,9},{9,8},{10,11... | collective-permute-start | bytes 122888 | tf_op jit(solution)/shard_map/ppermute | solution.py:567

commit v9 on v8

--- a/solution.py
+++ b/solution.py
@@ -169,8 +169,9 @@
         copy.start()
     for copy in copies[:-3]:
         copy.wait()
-    grain = grains[...]
-    phase = phases[...]
+    halves = [(block, slice(4 * half, 4 * half + 1)) for block in range(4) for half in range(2)]
+    grain = jnp.concatenate([grains[at] for at in halves], axis=0)
+    phase = jnp.concatenate([phases[at] for at in halves], axis=0)
     cls = jnp.zeros(grain.shape, jnp.int32)
     for number in range(classes.shape[0]):
         cls = jnp.where(grain == number, classes[number], cls)
@@ -178,10 +179,9 @@
     for p in range(num_phases):
         for c in range(num_classes):
             value = jnp.where((phase == p) & (cls == c), diff[p, c], value)
-    rows = jnp.concatenate([value[block, 4 * half : 4 * half + 1] for block in range(4) for half in range(2)], axis=0)
-    kappa_ref[0] = rows
-    mate_ref[HALO] = rows
-    other_ref[HALO] = rows
+    kappa_ref[0] = value
+    mate_ref[HALO] = value
+    other_ref[HALO] = value
     for copy in copies[-3:]:
         copy.wait()
 
@@ -432,9 +432,9 @@
     refs = refs[12:]
     if last:
         out_hbm, (out, sems), refs = out, refs[-2:], refs[:-2]
-        halves = (slice(0, 8), slice(8, 16))
+        quarters = [slice(4 * i, 4 * i + 4) for i in range(4)]
         copies = [
-            pltpu.make_async_copy(out.at[half], out_hbm.at[half], sems.at[i]) for i, half in enumerate(halves)
+            pltpu.make_async_copy(out.at[part], out_hbm.at[part], sems.at[i]) for i, part in enumerate(quarters)
         ]
     else:
         (mate, other), refs = refs[:2], refs[2:]
@@ -470,8 +470,8 @@
     for z in range(12, 28):
         here, total, weight, _ = fine_plane(vb, source, coefs, z_faces, z, 8, 8)
         out[z - 12] = 0.2 * here + weight * total
-        if last and z in (19, 27):
-            copies[z // 27].start()
+        if last and z % 4 == 3:
+            copies[(z - 12) // 4].start()
     if last:
         for copy in copies:
             copy.wait()
@@ -545,7 +545,7 @@
     outs = [floats(16, 8, 128)] + ([] if last else [floats(FIELD_HALO, 8, 128)] * 2)
     scratch = [FIELD, FIELD, (320, 128), (352, 128), (352, 128)]
     if last:
-        scratch += [(16, 8, 128), pltpu.SemaphoreType.DMA((2,))]
+        scratch += [(16, 8, 128), pltpu.SemaphoreType.DMA((4,))]
     args = [index, *shared, near, *edges, *kept]
     return call(
         lambda *refs: up_body(last, *refs), outs, scratch, args, outputs=pltpu.HBM if last else pltpu.VMEM

time: 90.7 us -> 90.7 us (level)
  no operation moved by 1% of the time
where the time goes in v9:
time: 90.7 us; the launch traced here: 90.5 us
  blocking collectives  38.3 us (42%)
  starting transfers between devices  22 us (24%)
  waiting for transfers between devices  15.4 us (17%)
  Pallas kernels  14.3 us (16%)
    all_to_all x2, blocking collectives, to_all(): out = lax.all_to_all(copies, ('gz', 'gx'), 0, 0)  38.3 us
    ppermute x10, starting transfers between devices, swap(): lax.ppermute(array, axis, [(i, partner(i) % count) for i in range(count)])  16.8 us
    pallas_call x7, Pallas kernels, call(): pl.pallas_call(body, out_shape=outs, in_specs=[pl.BlockSpec(memory_space=...  14.3 us
    ppermute x10, waiting for transfers between devices, swap(): lax.ppermute(array, axis, [(i, partner(i) % count) for i in range(count)])  8.64 us
    ppermute x4, waiting for transfers between devices, far_in_y(): return lax.ppermute(array, ('gz', 'gx', 'core'), pairs)  6.75 us
    ppermute x4, starting transfers between devices, far_in_y(): return lax.ppermute(array, ('gz', 'gx', 'core'), pairs)  5.28 us
  transfers between devices with their start and end apart: 14, of which 8 were waited for; matrix products, arithmetic and copies ran while one was open for 0% of the time, Pallas kernels for 6%

profile of v9, /device:TPU:1, one launch (start us, length us, event | category | flops | bytes accessed | tf_op | source)
XLA Modules:
  0.0 90.5 jit_solution(10685117389677142874)
XLA Ops:
  0.1 1.6 %shard_map.55 = (f32[1,8,128]{2,1,0:T(8,128)S(1)}, f32[16,8,128]{2,1,0:T(8,128)S(1)}, f32[11,8,128]{2,1,0:T(8,128)S(1)}, f32[11,8,128]{2,1,0:T(8,128)S(1)}) custom-call(s32[2]{0:T(128)S(1)} %pad_add_fusion.index.refs_0_, s32[64]{0:T(128)} %class_hbm.1, f32[3,4]{1,0:T(4,128)} %diff_hbm.1, s32[4,4,8,128]{3,2,1,0:T(8,128)} %bitcast.14, ...), custom_call_target="tpu_custom_call" | custom-call | tf_op jit(solution)/shard_map/pallas_call | solution.py:489
  1.7 8.9 %collective-permute-start = (f32[11,8,128]{2,1,0:T(8,128)S(1)}, f32[11,8,128]{2,1,0:T(8,128)S(1)}, u32[]{:S(2)}, u32[]{:S(2)}) collective-permute-start(f32[11,8,128]{2,1,0:T(8,128)S(1)} %get-tuple-element.30), channel_id=1, source_target_pairs={{0,248},{8,16},{16,8},{24,32},{32,24},{40,48},{48,40},{56,64},{64,... | collective-permute-start | bytes 135176 | tf_op jit(solution)/shard_map/ppermute | solution.py:567
  10.6 1.4 %collective-permute-done = f32[11,8,128]{2,1,0:T(8,128)S(1)} collective-permute-done((f32[11,8,128]{2,1,0:T(8,128)S(1)}, f32[11,8,128]{2,1,0:T(8,128)S(1)}, u32[]{:S(2)}, u32[]{:S(2)}) %collective-permute-start) | collective-permute-done | bytes 45088 | tf_op jit(solution)/shard_map/ppermute | solution.py:567
  12.0 1.5 %collective-permute-done.1 = f32[11,8,128]{2,1,0:T(8,128)S(1)} collective-permute-done((f32[11,8,128]{2,1,0:T(8,128)S(1)}, f32[11,8,128]{2,1,0:T(8,128)S(1)}, u32[]{:S(2)}, u32[]{:S(2)}) %collective-permute-start.1) | collective-permute-done | bytes 45088 | tf_op jit(solution)/shard_map/ppermute | solution.py:567
  13.6 3.3 %collective-permute-start.3 = (f32[39,8,128]{2,1,0:T(8,128)S(1)}, f32[39,8,128]{2,1,0:T(8,128)S(1)}, u32[]{:S(2)}, u32[]{:S(2)}) collective-permute-start(f32[39,8,128]{2,1,0:T(8,128)S(1)} %constant_dynamic-update-slice_fusion.refs_2_), channel_id=1, source_target_pairs={{0,8},{1,2},{2,1},{3,4},{4,3},{5,6},{6,5},{7,15},{8,0},{9,10},{10,... | collective-permute-start | bytes 479240 | tf_op jit(solution)/shard_map/ppermute | solution.py:583
  16.9 3.3 %collective-permute-done.3.refs_3_ = f32[39,8,128]{2,1,0:T(8,128)S(1)} collective-permute-done((f32[39,8,128]{2,1,0:T(8,128)S(1)}, f32[39,8,128]{2,1,0:T(8,128)S(1)}, u32[]{:S(2)}, u32[]{:S(2)}) %collective-permute-start.3) | collective-permute-done | bytes 159776 | tf_op jit(solution)/shard_map/ppermute | solution.py:583
  20.1 2.0 %shard_map.56 = (f32[512,128]{1,0:T(8,128)S(1)}, f32[80,128]{1,0:T(8,128)S(1)}, f32[480,128]{1,0:T(8,128)S(1)}, f32[320,128]{1,0:T(8,128)S(1)}, f32[352,128]{1,0...) custom-call(s32[2]{0:T(128)S(1)} %pad_add_fusion.index.refs_0_, ...), custom_call_target="tpu_custom_call" | custom-call | tf_op jit(solution)/shard_map/pallas_call | solution.py:489
  22.1 21.1 %all_to_all.10 = f32[128,4,128]{2,1,0:T(4,128)S(1)} all-to-all(f32[128,4,128]{2,1,0:T(4,128)S(1)} %bitcast.12), channel_id=1, replica_groups=mesh['gz'=32,'gx'=4,'core'=2] {'gz','gx'}, dimensions={0} | all-to-all | bytes 524288 | tf_op jit(solution)/shard_map/all_to_all | solution.py:589
  43.2 3.0 %collective-permute-start.4 = (f32[512,128]{1,0:T(8,128)S(1)}, f32[512,128]{1,0:T(8,128)S(1)}, u32[]{:S(2)}, u32[]{:S(2)}) collective-permute-start(f32[512,128]{1,0:T(8,128)S(1)} %bitcast.8), channel_id=1, source_target_pairs={{0,1},{1,0},{2,3},{3,2},{4,5},{5,4},{6,7},{7,6},{8,9},{9,8},{10,11... | collective-permute-start | bytes 786440 | tf_op jit(solution)/shard_map/ppermute | solution.py:567
  46.2 0.8 collective-permute-start.5
  47.0 0.4 collective-permute-done.4.refs_2_
  47.3 3.0 %shard_map.57 = (f32[48,128]{1,0:T(8,128)S(1)}, f32[6,352,128]{2,1,0:T(8,128)S(1)}, f32[6,176,128]{2,1,0:T(8,128)S(1)}, f32[6,96,128]{2,1,0:T(8,128)S(1)}) custom-call(s32[2]{0:T(128)S(1)} %pad_add_fusion.index.refs_0_, f32[512,128]{1,0:T(8,128)S(1)} %bitcast.9, f32[512,128]{1,0:T(8,128)S(1)} %collective-permute-done.4.refs_2_), custom_call_target="tpu_custom_call" | custom-call | tf_op jit(solution)/shard_map/pallas_call | solution.py:489
  50.4 1.5 %shard_map.58 = (f32[16,8,128]{2,1,0:T(8,128)S(1)}, f32[11,8,128]{2,1,0:T(8,128)S(1)}, f32[11,8,128]{2,1,0:T(8,128)S(1)}) custom-call(s32[2]{0:T(128)S(1)} %pad_add_fusion.index.refs_0_, f32[960,128]{1,0:T(8,128)S(1)} %get-tuple-element.34.refs_1_.refs_4_, f32[10,11,24,128]{3,2,1,0:T(8,128)S(1)} %get-tuple-element.35.refs_2_.refs_5_, ...), custom_call_target="tpu_custom_call" | custom-call | tf_op jit(solution)/shard_map/pallas_call | solution.py:489
  51.8 1.1 %collective-permute-start.7 = (f32[11,8,128]{2,1,0:T(8,128)S(1)}, f32[11,8,128]{2,1,0:T(8,128)S(1)}, u32[]{:S(2)}, u32[]{:S(2)}) collective-permute-start(f32[11,8,128]{2,1,0:T(8,128)S(1)} %get-tuple-element.44), channel_id=1, source_target_pairs={{0,248},{8,16},{16,8},{24,32},{32,24},{40,48},{48,40},{56,64},{64,... | collective-permute-start | bytes 135176 | tf_op jit(solution)/shard_map/ppermute | solution.py:567
  53.1 5.0 %collective-permute-done.7 = f32[11,8,128]{2,1,0:T(8,128)S(1)} collective-permute-done((f32[11,8,128]{2,1,0:T(8,128)S(1)}, f32[11,8,128]{2,1,0:T(8,128)S(1)}, u32[]{:S(2)}, u32[]{:S(2)}) %collective-permute-start.7) | collective-permute-done | bytes 45088 | tf_op jit(solution)/shard_map/ppermute | solution.py:567
  58.2 1.8 %collective-permute-start.10 = (f32[38,8,128]{2,1,0:T(8,128)S(1)}, f32[38,8,128]{2,1,0:T(8,128)S(1)}, u32[]{:S(2)}, u32[]{:S(2)}) collective-permute-start(f32[38,8,128]{2,1,0:T(8,128)S(1)} %pad_maximum_fusion.refs_2_), channel_id=1, source_target_pairs={{0,8},{1,2},{2,1},{3,4},{4,3},{5,6},{6,5},{7,15},{8,0},{9,10},{10,... | collective-permute-start | bytes 466952 | tf_op jit(solution)/shard_map/ppermute | solution.py:583
  60.1 3.2 %collective-permute-done.10.refs_3_ = f32[38,8,128]{2,1,0:T(8,128)S(1)} collective-permute-done((f32[38,8,128]{2,1,0:T(8,128)S(1)}, f32[38,8,128]{2,1,0:T(8,128)S(1)}, u32[]{:S(2)}, u32[]{:S(2)}) %collective-permute-start.10) | collective-permute-done | bytes 155680 | tf_op jit(solution)/shard_map/ppermute | solution.py:583
  63.2 1.9 %shard_map.59 = (f32[256,128]{1,0:T(8,128)S(1)}, f32[80,128]{1,0:T(8,128)S(1)}, f32[480,128]{1,0:T(8,128)S(1)}, f32[320,128]{1,0:T(8,128)S(1)}, f32[352,128]{1,0:T(8,128)S(1)}) custom-call(s32[2]{0:T(128)S(1)} %pad_add_fusion.index.refs_0_, f32[38,8,128]{2,1,0:T(8,128)S(1)} %collective-permute-done.9.refs_1_, f32[38,8,128]{2,1,0:T(8,128)S(1)} %pad_maximum_fusion.refs_2_, ...), custom_call_target="tpu_custom_call" | custom-call | tf_op jit(solution)/shard_map/pallas_call | solution.py:489
  65.1 17.2 %all_to_all.11 = f32[128,2,128]{2,1,0:T(2,128)S(1)} all-to-all(f32[128,2,128]{2,1,0:T(2,128)S(1)} %bitcast.13), channel_id=1, replica_groups=mesh['gz'=32,'gx'=4,'core'=2] {'gz','gx'}, dimensions={0} | all-to-all | bytes 262144 | tf_op jit(solution)/shard_map/all_to_all | solution.py:589
  82.4 2.2 %collective-permute-start.11 = (f32[256,128]{1,0:T(8,128)S(1)}, f32[256,128]{1,0:T(8,128)S(1)}, u32[]{:S(2)}, u32[]{:S(2)}) collective-permute-start(f32[256,128]{1,0:T(8,128)S(1)} %bitcast.10), channel_id=1, source_target_pairs={{0,1},{1,0},{2,3},{3,2},{4,5},{5,4},{6,7},{7,6},{8,9},{9,8},{10,11... | collective-permute-start | bytes 393224 | tf_op jit(solution)/shard_map/ppermute | solution.py:567
  84.7 0.5 collective-permute-start.12
  85.2 0.4 collective-permute-done.11.refs_2_
  85.6 2.3 %shard_map.60.refs_5_ = f32[48,128]{1,0:T(8,128)S(1)} custom-call(s32[2]{0:T(128)S(1)} %pad_add_fusion.index.refs_0_, f32[256,128]{1,0:T(8,128)S(1)} %bitcast.11, f32[256,128]{1,0:T(8,128)S(1)} %collective-permute-done.11.refs_2_, f32[6,352,128]{2,1,0:T(8,128)S(1)} %get-tuple-element.48.refs_3_, f32[6,176,128]{2,1,0:T(8,128)S(1)} %get-tuple-element.49.refs_4_, ...), custom_call_target="tpu_custom_call" | custom-call | tf_op jit(solution)/shard_map/pallas_call | solution.py:489
  88.2 2.1 %shard_map.61 = f32[16,8,128]{2,1,0:T(8,128)} custom-call(s32[2]{0:T(128)S(1)} %pad_add_fusion.index.refs_0_, f32[960,128]{1,0:T(8,128)S(1)} %get-tuple-element.34.refs_1_.refs_4_, f32[10,11,24,128]{3,2,1,0:T(8,128)S(1)} %get-tuple-element.35.refs_2_.refs_5_, f32[11,24,128]{2,1,0:T(8,128)S(1)} %get-tuple-element.36.refs_3_.refs_6_, ...), custom_call_target="tpu_custom_call" | custom-call | tf_op jit(solution)/shard_map/pallas_call | solution.py:489
  (23 shorter events, 0.8 us)
Async XLA Ops:
  1.7 10.4 %collective-permute-start = (f32[11,8,128]{2,1,0:T(8,128)S(1)}, f32[11,8,128]{2,1,0:T(8,128)S(1)}, u32[]{:S(2)}, u32[]{:S(2)}) collective-permute-start(f32[11,8,128]{2,1,0:T(8,128)S(1)} %get-tuple-element.30), channel_id=1, source_target_pairs={{0,248},{8,16},{16,8},{24,32},{32,24},{40,48},{48,40},{56,64},{64,... | collective-permute-start | bytes 135176 | tf_op jit(solution)/shard_map/ppermute | solution.py:567
  10.6 2.9 %collective-permute-start.1 = (f32[11,8,128]{2,1,0:T(8,128)S(1)}, f32[11,8,128]{2,1,0:T(8,128)S(1)}, u32[]{:S(2)}, u32[]{:S(2)}) collective-permute-start(f32[11,8,128]{2,1,0:T(8,128)S(1)} %get-tuple-element.31), channel_id=1, source_target_pairs={{0,8},{8,0},{16,24},{24,16},{32,40},{40,32},{48,56},{56,48},{64,72... | collective-permute-start | bytes 135176 | tf_op jit(solution)/shard_map/ppermute | solution.py:567
  13.6 6.5 %collective-permute-start.3 = (f32[39,8,128]{2,1,0:T(8,128)S(1)}, f32[39,8,128]{2,1,0:T(8,128)S(1)}, u32[]{:S(2)}, u32[]{:S(2)}) collective-permute-start(f32[39,8,128]{2,1,0:T(8,128)S(1)} %constant_dynamic-update-slice_fusion.refs_2_), channel_id=1, source_target_pairs={{0,8},{1,2},{2,1},{3,4},{4,3},{5,6},{6,5},{7,15},{8,0},{9,10},{10,... | collective-permute-start | bytes 479240 | tf_op jit(solution)/shard_map/ppermute | solution.py:583
  16.9 3.3 %collective-permute-start.2 = (f32[39,8,128]{2,1,0:T(8,128)S(1)}, f32[39,8,128]{2,1,0:T(8,128)S(1)}, u32[]{:S(2)}, u32[]{:S(2)}) collective-permute-start(f32[39,8,128]{2,1,0:T(8,128)S(1)} %constant_dynamic-update-slice_fusion.refs_2_), channel_id=1, source_target_pairs={{0,1},{1,0},{2,3},{3,2},{4,5},{5,4},{6,7},{7,6},{8,9},{9,8},{10,11... | collective-permute-start | bytes 479240 | tf_op jit(solution)/shard_map/ppermute | solution.py:567
  43.2 4.1 %collective-permute-start.4 = (f32[512,128]{1,0:T(8,128)S(1)}, f32[512,128]{1,0:T(8,128)S(1)}, u32[]{:S(2)}, u32[]{:S(2)}) collective-permute-start(f32[512,128]{1,0:T(8,128)S(1)} %bitcast.8), channel_id=1, source_target_pairs={{0,1},{1,0},{2,3},{3,2},{4,5},{5,4},{6,7},{7,6},{8,9},{9,8},{10,11... | collective-permute-start | bytes 786440 | tf_op jit(solution)/shard_map/ppermute | solution.py:567
  46.1 4.2 %collective-permute-start.6 = (f32[80,128]{1,0:T(8,128)S(1)}, f32[80,128]{1,0:T(8,128)S(1)}, u32[]{:S(2)}, u32[]{:S(2)}) collective-permute-start(f32[80,128]{1,0:T(8,128)S(1)} %get-tuple-element.40), channel_id=1, source_target_pairs={{0,8},{1,2},{2,1},{3,4},{4,3},{5,6},{6,5},{7,15},{8,0},{9,10},{10,... | collective-permute-start | bytes 122888 | tf_op jit(solution)/shard_map/ppermute | solution.py:583
  46.2 4.2 %collective-permute-start.5 = (f32[80,128]{1,0:T(8,128)S(1)}, f32[80,128]{1,0:T(8,128)S(1)}, u32[]{:S(2)}, u32[]{:S(2)}) collective-permute-start(f32[80,128]{1,0:T(8,128)S(1)} %get-tuple-element.40), channel_id=1, source_target_pairs={{0,1},{1,0},{2,3},{3,2},{4,5},{5,4},{6,7},{7,6},{8,9},{9,8},{10,11... | collective-permute-start | bytes 122888 | tf_op jit(solution)/shard_map/ppermute | solution.py:567
  51.8 6.3 %collective-permute-start.7 = (f32[11,8,128]{2,1,0:T(8,128)S(1)}, f32[11,8,128]{2,1,0:T(8,128)S(1)}, u32[]{:S(2)}, u32[]{:S(2)}) collective-permute-start(f32[11,8,128]{2,1,0:T(8,128)S(1)} %get-tuple-element.44), channel_id=1, source_target_pairs={{0,248},{8,16},{16,8},{24,32},{32,24},{40,48},{48,40},{56,64},{64,... | collective-permute-start | bytes 135176 | tf_op jit(solution)/shard_map/ppermute | solution.py:567
  53.0 5.2 %collective-permute-start.8 = (f32[11,8,128]{2,1,0:T(8,128)S(1)}, f32[11,8,128]{2,1,0:T(8,128)S(1)}, u32[]{:S(2)}, u32[]{:S(2)}) collective-permute-start(f32[11,8,128]{2,1,0:T(8,128)S(1)} %get-tuple-element.45), channel_id=1, source_target_pairs={{0,8},{8,0},{16,24},{24,16},{32,40},{40,32},{48,56},{56,48},{64,72... | collective-permute-start | bytes 135176 | tf_op jit(solution)/shard_map/ppermute | solution.py:567
  58.2 5.1 %collective-permute-start.10 = (f32[38,8,128]{2,1,0:T(8,128)S(1)}, f32[38,8,128]{2,1,0:T(8,128)S(1)}, u32[]{:S(2)}, u32[]{:S(2)}) collective-permute-start(f32[38,8,128]{2,1,0:T(8,128)S(1)} %pad_maximum_fusion.refs_2_), channel_id=1, source_target_pairs={{0,8},{1,2},{2,1},{3,4},{4,3},{5,6},{6,5},{7,15},{8,0},{9,10},{10,... | collective-permute-start | bytes 466952 | tf_op jit(solution)/shard_map/ppermute | solution.py:583
  60.0 3.2 %collective-permute-start.9 = (f32[38,8,128]{2,1,0:T(8,128)S(1)}, f32[38,8,128]{2,1,0:T(8,128)S(1)}, u32[]{:S(2)}, u32[]{:S(2)}) collective-permute-start(f32[38,8,128]{2,1,0:T(8,128)S(1)} %pad_maximum_fusion.refs_2_), channel_id=1, source_target_pairs={{0,1},{1,0},{2,3},{3,2},{4,5},{5,4},{6,7},{7,6},{8,9},{9,8},{10,11... | collective-permute-start | bytes 466952 | tf_op jit(solution)/shard_map/ppermute | solution.py:567
  82.4 3.2 %collective-permute-start.11 = (f32[256,128]{1,0:T(8,128)S(1)}, f32[256,128]{1,0:T(8,128)S(1)}, u32[]{:S(2)}, u32[]{:S(2)}) collective-permute-start(f32[256,128]{1,0:T(8,128)S(1)} %bitcast.10), channel_id=1, source_target_pairs={{0,1},{1,0},{2,3},{3,2},{4,5},{5,4},{6,7},{7,6},{8,9},{9,8},{10,11... | collective-permute-start | bytes 393224 | tf_op jit(solution)/shard_map/ppermute | solution.py:567
  84.6 3.6 %collective-permute-start.13 = (f32[80,128]{1,0:T(8,128)S(1)}, f32[80,128]{1,0:T(8,128)S(1)}, u32[]{:S(2)}, u32[]{:S(2)}) collective-permute-start(f32[80,128]{1,0:T(8,128)S(1)} %get-tuple-element.51), channel_id=1, source_target_pairs={{0,8},{1,2},{2,1},{3,4},{4,3},{5,6},{6,5},{7,15},{8,0},{9,10},{10,... | collective-permute-start | bytes 122888 | tf_op jit(solution)/shard_map/ppermute | solution.py:583
  84.7 3.5 %collective-permute-start.12 = (f32[80,128]{1,0:T(8,128)S(1)}, f32[80,128]{1,0:T(8,128)S(1)}, u32[]{:S(2)}, u32[]{:S(2)}) collective-permute-start(f32[80,128]{1,0:T(8,128)S(1)} %get-tuple-element.51), channel_id=1, source_target_pairs={{0,1},{1,0},{2,3},{3,2},{4,5},{5,4},{6,7},{7,6},{8,9},{9,8},{10,11... | collective-permute-start | bytes 122888 | tf_op jit(solution)/shard_map/ppermute | solution.py:567

commit v10 on v8

--- a/solution.py
+++ b/solution.py
@@ -340,8 +340,8 @@
     tile = jnp.concatenate(values * repeats, axis=0)
     for at in range(0, copies // repeats):
         chunk[at * 8 : at * 8 + 8] = tile
-    for plane in range(20):
-        edge[plane * 4 : plane * 4 + 4] = kept_one[16 + plane * 16 + 4 : 16 + plane * 16 + 8]
+    for plane in range(3, 17):
+        edge[plane * 4 - 12 : plane * 4 - 8] = kept_one[16 + plane * 16 + 4 : 16 + plane * 16 + 8]
 
 
 def coarse_levels():
@@ -447,10 +447,10 @@
     by_z = [
         dot(spread_y, lane_map(lambda r, c, z=z: matrix(r == z * 32 + (c >> 2), 1.0))) for z in range(4)
     ]
-    for plane in range(20):
+    for plane in range(3, 17):
         part, z = divmod(plane // 2 + 1, 4)
         at = 16 + plane * 16
-        one, two = edge_mate[plane * 4 : plane * 4 + 4], edge_other[plane * 4 : plane * 4 + 4]
+        one, two = edge_mate[plane * 4 - 12 : plane * 4 - 8], edge_other[plane * 4 - 12 : plane * 4 - 8]
         field = jnp.concatenate(
             [jnp.where(even, two, one), kept_one[at + 4 : at + 8], jnp.where(even, one, two),
              jnp.zeros((4, 128), jnp.float32)], axis=0
@@ -507,7 +507,7 @@
     copies = lax.axis_size("gz") * lax.axis_size("gx")
     outs = [
         floats(copies * (4 if first else 2), 128),
-        floats(80, 128),
+        floats(56, 128),
         floats(20 * WY, 128),
         floats(320, 128),
         floats(352, 128),

time: 90.7 us -> 90.4 us (level)
  no operation moved by 1% of the time
where the time goes in v10:
time: 90.4 us; the launch traced here: 90.2 us
  blocking collectives  38.3 us (42%)
  starting transfers between devices  22 us (24%)
  waiting for transfers between devices  15.2 us (17%)
  Pallas kernels  14.2 us (16%)
    all_to_all x2, blocking collectives, to_all(): out = lax.all_to_all(copies, ('gz', 'gx'), 0, 0)  38.3 us
    ppermute x10, starting transfers between devices, swap(): lax.ppermute(array, axis, [(i, partner(i) % count) for i in range(count)])  16.8 us
    pallas_call x7, Pallas kernels, call(): pl.pallas_call(body, out_shape=outs, in_specs=[pl.BlockSpec(memory_space=...  14.2 us
    ppermute x10, waiting for transfers between devices, swap(): lax.ppermute(array, axis, [(i, partner(i) % count) for i in range(count)])  8.64 us
    ppermute x4, waiting for transfers between devices, far_in_y(): return lax.ppermute(array, ('gz', 'gx', 'core'), pairs)  6.6 us
    ppermute x4, starting transfers between devices, far_in_y(): return lax.ppermute(array, ('gz', 'gx', 'core'), pairs)  5.28 us
  transfers between devices with their start and end apart: 14, of which 8 were waited for; matrix products, arithmetic and copies ran while one was open for 0% of the time, Pallas kernels for 6%

profile of v10, /device:TPU:1, one launch (start us, length us, event | category | flops | bytes accessed | tf_op | source)
XLA Modules:
  0.0 90.2 jit_solution(9269881101648733501)
XLA Ops:
  0.1 1.6 %shard_map.55 = (f32[1,8,128]{2,1,0:T(8,128)S(1)}, f32[16,8,128]{2,1,0:T(8,128)S(1)}, f32[11,8,128]{2,1,0:T(8,128)S(1)}, f32[11,8,128]{2,1,0:T(8,128)S(1)}) custom-call(s32[2]{0:T(128)S(1)} %pad_add_fusion.index.refs_0_, s32[64]{0:T(128)} %class_hbm.1, f32[3,4]{1,0:T(4,128)} %diff_hbm.1, s32[4,4,8,128]{3,2,1,0:T(8,128)} %bitcast.14, ...), custom_call_target="tpu_custom_call" | custom-call | tf_op jit(solution)/shard_map/pallas_call | solution.py:489
  1.7 8.9 %collective-permute-start = (f32[11,8,128]{2,1,0:T(8,128)S(1)}, f32[11,8,128]{2,1,0:T(8,128)S(1)}, u32[]{:S(2)}, u32[]{:S(2)}) collective-permute-start(f32[11,8,128]{2,1,0:T(8,128)S(1)} %get-tuple-element.30), channel_id=1, source_target_pairs={{0,248},{8,16},{16,8},{24,32},{32,24},{40,48},{48,40},{56,64},{64,... | collective-permute-start | bytes 135176 | tf_op jit(solution)/shard_map/ppermute | solution.py:567
  10.6 1.4 %collective-permute-done = f32[11,8,128]{2,1,0:T(8,128)S(1)} collective-permute-done((f32[11,8,128]{2,1,0:T(8,128)S(1)}, f32[11,8,128]{2,1,0:T(8,128)S(1)}, u32[]{:S(2)}, u32[]{:S(2)}) %collective-permute-start) | collective-permute-done | bytes 45088 | tf_op jit(solution)/shard_map/ppermute | solution.py:567
  12.0 1.5 %collective-permute-done.1 = f32[11,8,128]{2,1,0:T(8,128)S(1)} collective-permute-done((f32[11,8,128]{2,1,0:T(8,128)S(1)}, f32[11,8,128]{2,1,0:T(8,128)S(1)}, u32[]{:S(2)}, u32[]{:S(2)}) %collective-permute-start.1) | collective-permute-done | bytes 45088 | tf_op jit(solution)/shard_map/ppermute | solution.py:567
  13.6 3.3 %collective-permute-start.3 = (f32[39,8,128]{2,1,0:T(8,128)S(1)}, f32[39,8,128]{2,1,0:T(8,128)S(1)}, u32[]{:S(2)}, u32[]{:S(2)}) collective-permute-start(f32[39,8,128]{2,1,0:T(8,128)S(1)} %constant_dynamic-update-slice_fusion.refs_2_), channel_id=1, source_target_pairs={{0,8},{1,2},{2,1},{3,4},{4,3},{5,6},{6,5},{7,15},{8,0},{9,10},{10,... | collective-permute-start | bytes 479240 | tf_op jit(solution)/shard_map/ppermute | solution.py:583
  16.9 3.3 %collective-permute-done.3.refs_3_ = f32[39,8,128]{2,1,0:T(8,128)S(1)} collective-permute-done((f32[39,8,128]{2,1,0:T(8,128)S(1)}, f32[39,8,128]{2,1,0:T(8,128)S(1)}, u32[]{:S(2)}, u32[]{:S(2)}) %collective-permute-start.3) | collective-permute-done | bytes 159776 | tf_op jit(solution)/shard_map/ppermute | solution.py:583
  20.1 1.9 %shard_map.56 = (f32[512,128]{1,0:T(8,128)S(1)}, f32[56,128]{1,0:T(8,128)S(1)}, f32[480,128]{1,0:T(8,128)S(1)}, f32[320,128]{1,0:T(8,128)S(1)}, f32[352,128]{1,0...) custom-call(s32[2]{0:T(128)S(1)} %pad_add_fusion.index.refs_0_, ...), custom_call_target="tpu_custom_call" | custom-call | tf_op jit(solution)/shard_map/pallas_call | solution.py:489
  22.1 21.1 %all_to_all.10 = f32[128,4,128]{2,1,0:T(4,128)S(1)} all-to-all(f32[128,4,128]{2,1,0:T(4,128)S(1)} %bitcast.12), channel_id=1, replica_groups=mesh['gz'=32,'gx'=4,'core'=2] {'gz','gx'}, dimensions={0} | all-to-all | bytes 524288 | tf_op jit(solution)/shard_map/all_to_all | solution.py:589
  43.1 3.0 %collective-permute-start.4 = (f32[512,128]{1,0:T(8,128)S(1)}, f32[512,128]{1,0:T(8,128)S(1)}, u32[]{:S(2)}, u32[]{:S(2)}) collective-permute-start(f32[512,128]{1,0:T(8,128)S(1)} %bitcast.8), channel_id=1, source_target_pairs={{0,1},{1,0},{2,3},{3,2},{4,5},{5,4},{6,7},{7,6},{8,9},{9,8},{10,11... | collective-permute-start | bytes 786440 | tf_op jit(solution)/shard_map/ppermute | solution.py:567
  46.1 0.8 collective-permute-start.5
  46.9 0.4 collective-permute-done.4.refs_2_
  47.3 3.1 %shard_map.57 = (f32[48,128]{1,0:T(8,128)S(1)}, f32[6,352,128]{2,1,0:T(8,128)S(1)}, f32[6,176,128]{2,1,0:T(8,128)S(1)}, f32[6,96,128]{2,1,0:T(8,128)S(1)}) custom-call(s32[2]{0:T(128)S(1)} %pad_add_fusion.index.refs_0_, f32[512,128]{1,0:T(8,128)S(1)} %bitcast.9, f32[512,128]{1,0:T(8,128)S(1)} %collective-permute-done.4.refs_2_), custom_call_target="tpu_custom_call" | custom-call | tf_op jit(solution)/shard_map/pallas_call | solution.py:489
  50.3 1.4 %shard_map.58 = (f32[16,8,128]{2,1,0:T(8,128)S(1)}, f32[11,8,128]{2,1,0:T(8,128)S(1)}, f32[11,8,128]{2,1,0:T(8,128)S(1)}) custom-call(s32[2]{0:T(128)S(1)} %pad_add_fusion.index.refs_0_, f32[960,128]{1,0:T(8,128)S(1)} %get-tuple-element.34.refs_1_.refs_4_, f32[10,11,24,128]{3,2,1,0:T(8,128)S(1)} %get-tuple-element.35.refs_2_.refs_5_, ...), custom_call_target="tpu_custom_call" | custom-call | tf_op jit(solution)/shard_map/pallas_call | solution.py:489
  51.8 1.1 %collective-permute-start.7 = (f32[11,8,128]{2,1,0:T(8,128)S(1)}, f32[11,8,128]{2,1,0:T(8,128)S(1)}, u32[]{:S(2)}, u32[]{:S(2)}) collective-permute-start(f32[11,8,128]{2,1,0:T(8,128)S(1)} %get-tuple-element.44), channel_id=1, source_target_pairs={{0,248},{8,16},{16,8},{24,32},{32,24},{40,48},{48,40},{56,64},{64,... | collective-permute-start | bytes 135176 | tf_op jit(solution)/shard_map/ppermute | solution.py:567
  53.1 5.0 %collective-permute-done.7 = f32[11,8,128]{2,1,0:T(8,128)S(1)} collective-permute-done((f32[11,8,128]{2,1,0:T(8,128)S(1)}, f32[11,8,128]{2,1,0:T(8,128)S(1)}, u32[]{:S(2)}, u32[]{:S(2)}) %collective-permute-start.7) | collective-permute-done | bytes 45088 | tf_op jit(solution)/shard_map/ppermute | solution.py:567
  58.1 1.8 %collective-permute-start.10 = (f32[38,8,128]{2,1,0:T(8,128)S(1)}, f32[38,8,128]{2,1,0:T(8,128)S(1)}, u32[]{:S(2)}, u32[]{:S(2)}) collective-permute-start(f32[38,8,128]{2,1,0:T(8,128)S(1)} %pad_maximum_fusion.refs_2_), channel_id=1, source_target_pairs={{0,8},{1,2},{2,1},{3,4},{4,3},{5,6},{6,5},{7,15},{8,0},{9,10},{10,... | collective-permute-start | bytes 466952 | tf_op jit(solution)/shard_map/ppermute | solution.py:583
  60.0 3.2 %collective-permute-done.10.refs_3_ = f32[38,8,128]{2,1,0:T(8,128)S(1)} collective-permute-done((f32[38,8,128]{2,1,0:T(8,128)S(1)}, f32[38,8,128]{2,1,0:T(8,128)S(1)}, u32[]{:S(2)}, u32[]{:S(2)}) %collective-permute-start.10) | collective-permute-done | bytes 155680 | tf_op jit(solution)/shard_map/ppermute | solution.py:583
  63.2 1.8 %shard_map.59 = (f32[256,128]{1,0:T(8,128)S(1)}, f32[56,128]{1,0:T(8,128)S(1)}, f32[480,128]{1,0:T(8,128)S(1)}, f32[320,128]{1,0:T(8,128)S(1)}, f32[352,128]{1,0:T(8,128)S(1)}) custom-call(s32[2]{0:T(128)S(1)} %pad_add_fusion.index.refs_0_, f32[38,8,128]{2,1,0:T(8,128)S(1)} %collective-permute-done.9.refs_1_, f32[38,8,128]{2,1,0:T(8,128)S(1)} %pad_maximum_fusion.refs_2_, ...), custom_call_target="tpu_custom_call" | custom-call | tf_op jit(solution)/shard_map/pallas_call | solution.py:489
  65.0 17.2 %all_to_all.11 = f32[128,2,128]{2,1,0:T(2,128)S(1)} all-to-all(f32[128,2,128]{2,1,0:T(2,128)S(1)} %bitcast.13), channel_id=1, replica_groups=mesh['gz'=32,'gx'=4,'core'=2] {'gz','gx'}, dimensions={0} | all-to-all | bytes 262144 | tf_op jit(solution)/shard_map/all_to_all | solution.py:589
  82.2 2.2 %collective-permute-start.11 = (f32[256,128]{1,0:T(8,128)S(1)}, f32[256,128]{1,0:T(8,128)S(1)}, u32[]{:S(2)}, u32[]{:S(2)}) collective-permute-start(f32[256,128]{1,0:T(8,128)S(1)} %bitcast.10), channel_id=1, source_target_pairs={{0,1},{1,0},{2,3},{3,2},{4,5},{5,4},{6,7},{7,6},{8,9},{9,8},{10,11... | collective-permute-start | bytes 393224 | tf_op jit(solution)/shard_map/ppermute | solution.py:567
  84.6 0.5 collective-permute-start.12
  85.1 0.4 collective-permute-done.11.refs_2_
  85.4 2.3 %shard_map.60.refs_5_ = f32[48,128]{1,0:T(8,128)S(1)} custom-call(s32[2]{0:T(128)S(1)} %pad_add_fusion.index.refs_0_, f32[256,128]{1,0:T(8,128)S(1)} %bitcast.11, f32[256,128]{1,0:T(8,128)S(1)} %collective-permute-done.11.refs_2_, f32[6,352,128]{2,1,0:T(8,128)S(1)} %get-tuple-element.48.refs_3_, f32[6,176,128]{2,1,0:T(8,128)S(1)} %get-tuple-element.49.refs_4_, ...), custom_call_target="tpu_custom_call" | custom-call | tf_op jit(solution)/shard_map/pallas_call | solution.py:489
  87.9 2.1 %shard_map.61 = f32[16,8,128]{2,1,0:T(8,128)} custom-call(s32[2]{0:T(128)S(1)} %pad_add_fusion.index.refs_0_, f32[960,128]{1,0:T(8,128)S(1)} %get-tuple-element.34.refs_1_.refs_4_, f32[10,11,24,128]{3,2,1,0:T(8,128)S(1)} %get-tuple-element.35.refs_2_.refs_5_, f32[11,24,128]{2,1,0:T(8,128)S(1)} %get-tuple-element.36.refs_3_.refs_6_, ...), custom_call_target="tpu_custom_call" | custom-call | tf_op jit(solution)/shard_map/pallas_call | solution.py:489
  (23 shorter events, 0.7 us)
Async XLA Ops:
  1.7 10.4 %collective-permute-start = (f32[11,8,128]{2,1,0:T(8,128)S(1)}, f32[11,8,128]{2,1,0:T(8,128)S(1)}, u32[]{:S(2)}, u32[]{:S(2)}) collective-permute-start(f32[11,8,128]{2,1,0:T(8,128)S(1)} %get-tuple-element.30), channel_id=1, source_target_pairs={{0,248},{8,16},{16,8},{24,32},{32,24},{40,48},{48,40},{56,64},{64,... | collective-permute-start | bytes 135176 | tf_op jit(solution)/shard_map/ppermute | solution.py:567
  10.6 2.9 %collective-permute-start.1 = (f32[11,8,128]{2,1,0:T(8,128)S(1)}, f32[11,8,128]{2,1,0:T(8,128)S(1)}, u32[]{:S(2)}, u32[]{:S(2)}) collective-permute-start(f32[11,8,128]{2,1,0:T(8,128)S(1)} %get-tuple-element.31), channel_id=1, source_target_pairs={{0,8},{8,0},{16,24},{24,16},{32,40},{40,32},{48,56},{56,48},{64,72... | collective-permute-start | bytes 135176 | tf_op jit(solution)/shard_map/ppermute | solution.py:567
  13.6 6.5 %collective-permute-start.3 = (f32[39,8,128]{2,1,0:T(8,128)S(1)}, f32[39,8,128]{2,1,0:T(8,128)S(1)}, u32[]{:S(2)}, u32[]{:S(2)}) collective-permute-start(f32[39,8,128]{2,1,0:T(8,128)S(1)} %constant_dynamic-update-slice_fusion.refs_2_), channel_id=1, source_target_pairs={{0,8},{1,2},{2,1},{3,4},{4,3},{5,6},{6,5},{7,15},{8,0},{9,10},{10,... | collective-permute-start | bytes 479240 | tf_op jit(solution)/shard_map/ppermute | solution.py:583
  16.9 3.3 %collective-permute-start.2 = (f32[39,8,128]{2,1,0:T(8,128)S(1)}, f32[39,8,128]{2,1,0:T(8,128)S(1)}, u32[]{:S(2)}, u32[]{:S(2)}) collective-permute-start(f32[39,8,128]{2,1,0:T(8,128)S(1)} %constant_dynamic-update-slice_fusion.refs_2_), channel_id=1, source_target_pairs={{0,1},{1,0},{2,3},{3,2},{4,5},{5,4},{6,7},{7,6},{8,9},{9,8},{10,11... | collective-permute-start | bytes 479240 | tf_op jit(solution)/shard_map/ppermute | solution.py:567
  43.1 4.1 %collective-permute-start.4 = (f32[512,128]{1,0:T(8,128)S(1)}, f32[512,128]{1,0:T(8,128)S(1)}, u32[]{:S(2)}, u32[]{:S(2)}) collective-permute-start(f32[512,128]{1,0:T(8,128)S(1)} %bitcast.8), channel_id=1, source_target_pairs={{0,1},{1,0},{2,3},{3,2},{4,5},{5,4},{6,7},{7,6},{8,9},{9,8},{10,11... | collective-permute-start | bytes 786440 | tf_op jit(solution)/shard_map/ppermute | solution.py:567
  46.1 4.2 %collective-permute-start.6 = (f32[56,128]{1,0:T(8,128)S(1)}, f32[56,128]{1,0:T(8,128)S(1)}, u32[]{:S(2)}, u32[]{:S(2)}) collective-permute-start(f32[56,128]{1,0:T(8,128)S(1)} %get-tuple-element.40), channel_id=1, source_target_pairs={{0,8},{1,2},{2,1},{3,4},{4,3},{5,6},{6,5},{7,15},{8,0},{9,10},{10,... | collective-permute-start | bytes 86024 | tf_op jit(solution)/shard_map/ppermute | solution.py:583
  46.1 4.2 %collective-permute-start.5 = (f32[56,128]{1,0:T(8,128)S(1)}, f32[56,128]{1,0:T(8,128)S(1)}, u32[]{:S(2)}, u32[]{:S(2)}) collective-permute-start(f32[56,128]{1,0:T(8,128)S(1)} %get-tuple-element.40), channel_id=1, source_target_pairs={{0,1},{1,0},{2,3},{3,2},{4,5},{5,4},{6,7},{7,6},{8,9},{9,8},{10,11... | collective-permute-start | bytes 86024 | tf_op jit(solution)/shard_map/ppermute | solution.py:567
  51.8 6.3 %collective-permute-start.7 = (f32[11,8,128]{2,1,0:T(8,128)S(1)}, f32[11,8,128]{2,1,0:T(8,128)S(1)}, u32[]{:S(2)}, u32[]{:S(2)}) collective-permute-start(f32[11,8,128]{2,1,0:T(8,128)S(1)} %get-tuple-element.44), channel_id=1, source_target_pairs={{0,248},{8,16},{16,8},{24,32},{32,24},{40,48},{48,40},{56,64},{64,... | collective-permute-start | bytes 135176 | tf_op jit(solution)/shard_map/ppermute | solution.py:567
  52.9 5.2 %collective-permute-start.8 = (f32[11,8,128]{2,1,0:T(8,128)S(1)}, f32[11,8,128]{2,1,0:T(8,128)S(1)}, u32[]{:S(2)}, u32[]{:S(2)}) collective-permute-start(f32[11,8,128]{2,1,0:T(8,128)S(1)} %get-tuple-element.45), channel_id=1, source_target_pairs={{0,8},{8,0},{16,24},{24,16},{32,40},{40,32},{48,56},{56,48},{64,72... | collective-permute-start | bytes 135176 | tf_op jit(solution)/shard_map/ppermute | solution.py:567
  58.1 5.1 %collective-permute-start.10 = (f32[38,8,128]{2,1,0:T(8,128)S(1)}, f32[38,8,128]{2,1,0:T(8,128)S(1)}, u32[]{:S(2)}, u32[]{:S(2)}) collective-permute-start(f32[38,8,128]{2,1,0:T(8,128)S(1)} %pad_maximum_fusion.refs_2_), channel_id=1, source_target_pairs={{0,8},{1,2},{2,1},{3,4},{4,3},{5,6},{6,5},{7,15},{8,0},{9,10},{10,... | collective-permute-start | bytes 466952 | tf_op jit(solution)/shard_map/ppermute | solution.py:583
  60.0 3.2 %collective-permute-start.9 = (f32[38,8,128]{2,1,0:T(8,128)S(1)}, f32[38,8,128]{2,1,0:T(8,128)S(1)}, u32[]{:S(2)}, u32[]{:S(2)}) collective-permute-start(f32[38,8,128]{2,1,0:T(8,128)S(1)} %pad_maximum_fusion.refs_2_), channel_id=1, source_target_pairs={{0,1},{1,0},{2,3},{3,2},{4,5},{5,4},{6,7},{7,6},{8,9},{9,8},{10,11... | collective-permute-start | bytes 466952 | tf_op jit(solution)/shard_map/ppermute | solution.py:567
  82.2 3.2 %collective-permute-start.11 = (f32[256,128]{1,0:T(8,128)S(1)}, f32[256,128]{1,0:T(8,128)S(1)}, u32[]{:S(2)}, u32[]{:S(2)}) collective-permute-start(f32[256,128]{1,0:T(8,128)S(1)} %bitcast.10), channel_id=1, source_target_pairs={{0,1},{1,0},{2,3},{3,2},{4,5},{5,4},{6,7},{7,6},{8,9},{9,8},{10,11... | collective-permute-start | bytes 393224 | tf_op jit(solution)/shard_map/ppermute | solution.py:567
  84.5 3.5 %collective-permute-start.13 = (f32[56,128]{1,0:T(8,128)S(1)}, f32[56,128]{1,0:T(8,128)S(1)}, u32[]{:S(2)}, u32[]{:S(2)}) collective-permute-start(f32[56,128]{1,0:T(8,128)S(1)} %get-tuple-element.51), channel_id=1, source_target_pairs={{0,8},{1,2},{2,1},{3,4},{4,3},{5,6},{6,5},{7,15},{8,0},{9,10},{10,... | collective-permute-start | bytes 86024 | tf_op jit(solution)/shard_map/ppermute | solution.py:583
  84.6 3.4 %collective-permute-start.12 = (f32[56,128]{1,0:T(8,128)S(1)}, f32[56,128]{1,0:T(8,128)S(1)}, u32[]{:S(2)}, u32[]{:S(2)}) collective-permute-start(f32[56,128]{1,0:T(8,128)S(1)} %get-tuple-element.51), channel_id=1, source_target_pairs={{0,1},{1,0},{2,3},{3,2},{4,5},{5,4},{6,7},{7,6},{8,9},{9,8},{10,11... | collective-permute-start | bytes 86024 | tf_op jit(solution)/shard_map/ppermute | solution.py:567
